TPU v7x, 256 devices: a whole 4x4x8 slice. The times are simulated.
256 devices in a mesh: dp: 4 (over x), rad: 8 (over y, z_lo), azi: 8 (over z_hi, core).
Axes of the slice: x: 4, y: 4, z: 8 (z_hi: 4, z_lo: 2; z = z_hi * 2 + z_lo), core: 2. Of those that a mesh axis runs over, the one named last changes fastest.
Arguments:
- inputs: bfloat16 [4, 96, 32, 64, 256], P('dp', None, 'rad', 'azi'), may hold values from -6 to 6
- weight: bfloat16 [96, 2592], P('dp'), may hold values from -0.125 to 0.125
- bias: bfloat16 [96], P('dp'), may hold values from -3 to 3
- cotangent: bfloat16 [4, 96, 32, 64, 256], P('dp', None, 'rad', 'azi'), may hold values from -6 to 6
Outputs:
- output: bfloat16 [4, 96, 32, 64, 256], P('dp', None, 'rad', 'azi')
- input_grad: bfloat16 [4, 96, 32, 64, 256], P('dp', None, 'rad', 'azi')
- weight_grad: float32 [96, 2592], P('dp')
- bias_grad: float32 [96], P('dp')
All inputs are finite; a program needn't handle non-finite values.
Results may differ from a plain program's by a relative error of at most 0.015.
Values may be sent and summed in bfloat16 or wider, within the bound.
No kernel may reach another device: no remote copies, remote signals or barrier semaphores. Data moves between devices by JAX's collectives and lax.ppermute only.
A program may use at most 128 MiB of HBM per device.

v0:
```python
import jax
import jax.numpy as jnp
from jax import lax
from jax.sharding import PartitionSpec as P

inverse_scale = 1.0 / 1024.0


def with_halo(cells, sides, width):
    for axis, dim in sides:
        count = lax.axis_size(axis)
        head = lax.slice_in_dim(cells, 0, width, axis=dim)
        tail = lax.slice_in_dim(cells, cells.shape[dim] - width, cells.shape[dim], axis=dim)
        cells = jnp.concatenate(
            [
                lax.ppermute(tail, axis, [(i, (i + 1) % count) for i in range(count)]),
                cells,
                lax.ppermute(head, axis, [((i + 1) % count, i) for i in range(count)]),
            ],
            axis=dim,
        )
    return cells


def rim_fix(extended):
    rad_index = lax.axis_index("rad")
    rad_last = lax.axis_size("rad") - 1
    low_rim = jnp.where(rad_index > 0, extended[:, :, :1], jnp.zeros_like(extended[:, :, :1]))
    high_rim = jnp.where(
        rad_index < rad_last, extended[:, :, -1:], jnp.zeros_like(extended[:, :, -1:])
    )
    return jnp.concatenate([low_rim, extended[:, :, 1:-1], high_rim], axis=2)


def axial_pad(extended):
    return jnp.pad(extended, ((0, 0), (0, 0), (0, 0), (0, 0), (1, 1)))


def extend_input(field):
    extended = rim_fix(with_halo(field, (("rad", 2), ("azi", 3)), 1))
    return axial_pad(extended)


def extend_grad(field):
    extended = rim_fix(with_halo(field, (("rad", 2), ("azi", 3)), 1))
    return axial_pad(extended)


def convolve(left, right, numbers):
    return lax.conv_general_dilated(
        left,
        right,
        (1, 1, 1),
        "VALID",
        dimension_numbers=numbers,
        preferred_element_type=jnp.float32,
    )


def on_device(inputs, weight, bias, cotangent):
    channels = inputs.shape[1]
    full_weight, full_bias = (
        lax.all_gather(weight, "dp", axis=0, tiled=True),
        lax.all_gather(bias, "dp", axis=0, tiled=True),
    )
    out_rows = full_weight.shape[0]
    kernel_taps = full_weight.reshape(out_rows, 3, 3, 3, channels)
    kernel_fwd = kernel_taps.transpose(0, 4, 1, 2, 3)
    kernel_back = kernel_taps[:, ::-1, ::-1, ::-1, :].transpose(4, 0, 1, 2, 3)
    padded = extend_input(inputs)
    preact = convolve(padded, kernel_fwd, ("NCDHW", "OIDHW", "NCDHW"))
    preact = preact + full_bias.astype(jnp.float32)[None, :, None, None, None]
    gate_value = jax.nn.sigmoid(preact)
    output = (preact * gate_value).astype(jnp.bfloat16)
    delta_z = (
        cotangent.astype(jnp.float32) * gate_value * (1.0 + preact * (1.0 - gate_value))
    ).astype(jnp.bfloat16)
    delta_pad = extend_grad(delta_z)
    backward = convolve(delta_pad, kernel_back, ("NCDHW", "OIDHW", "NCDHW"))
    kernel_grad = convolve(padded, delta_z, ("CNDHW", "IODHW", "NCDHW"))
    weight_term = (
        kernel_grad.transpose(1, 2, 3, 4, 0).reshape(out_rows, 27 * channels) * inverse_scale
    )
    bias_term = jnp.sum(delta_z.astype(jnp.float32), axis=(0, 2, 3, 4)) * inverse_scale
    group_part = (
        lax.psum_scatter(
            weight_term.astype(jnp.bfloat16), "dp", scatter_dimension=0, tiled=True
        ).astype(jnp.float32),
        lax.psum_scatter(
            bias_term.astype(jnp.bfloat16), "dp", scatter_dimension=0, tiled=True
        ).astype(jnp.float32),
    )
    weight_grad, bias_grad = lax.psum((group_part[0], group_part[1]), ("rad", "azi"))
    return (output, backward.astype(jnp.bfloat16), weight_grad, bias_grad)


def solution(mesh):
    return jax.shard_map(
        on_device,
        mesh=mesh,
        in_specs=(
            P("dp", None, "rad", "azi", None),
            P("dp", None),
            P("dp"),
            P("dp", None, "rad", "azi", None),
        ),
        out_specs=(
            P("dp", None, "rad", "azi", None),
            P("dp", None, "rad", "azi", None),
            P("dp", None),
            P("dp"),
        ),
        check_vma=False,
    )
```

profile of v0, /device:TPU:2, one launch (start us, length us, event | category | flops | bytes accessed | tf_op | source)
XLA Modules:
  0.0 530.9 jit_solution(4180190173391444999)
XLA Ops:
  7.2 1.2 fusion.42
  8.4 4.4 collective-permute-start.1
  12.8 9.5 %collective-permute-done.1 = bf16[1,96,1,8,256]{4,3,2,1,0:T(8,128)(2,1)S(1)} collective-permute-done((bf16[1,96,1,8,256]{4,3,2,1,0:T(8,128)(2,1)S(1)}, bf16[1,96,1,8,256]{4,3,2,1,0:T(8,128)(2,1)S(1)}, u32[]{:S(2)}, u32[]{:S(2)}) %collective-permute-start.1) | collective-permute-done | bytes 393248 | tf_op jit(solution)/shard_map/ppermute | solution.py:18
  22.3 8.0 %collective-permute-done = bf16[1,96,1,8,256]{4,3,2,1,0:T(8,128)(2,1)S(1)} collective-permute-done((bf16[1,96,1,8,256]{4,3,2,1,0:T(8,128)(2,1)S(1)}, bf16[1,96,1,8,256]{4,3,2,1,0:T(8,128)(2,1)S(1)}, u32[]{:S(2)}, u32[]{:S(2)}) %collective-permute-start) | collective-permute-done | bytes 393248 | tf_op jit(solution)/shard_map/ppermute | solution.py:16
  30.4 1.7 pad_maximum_fusion.3
  32.1 0.8 fusion.40
  32.9 0.8 copy.97
  33.6 0.6 fusion.43
  34.9 0.2 dynamic-update-slice
  35.1 8.6 %all-reduce = bf16[96]{0:T(256)(128)(2,1)S(1)} all-reduce(bf16[96]{0:T(256)(128)(2,1)S(1)} %dynamic-update-slice), channel_id=1, replica_groups=mesh['dp'=4,'rad'=8,'azi'=8] {'dp'}, use_global_device_ids=true, to_apply=%add | all-reduce | flops 96 | bytes 384
  43.8 12.8 %all_gather.6 = bf16[96,2592]{1,0:T(8,128)(2,1)S(1)} all-gather(bf16[24,2592]{1,0:T(8,128)(2,1)} %param.5), channel_id=1, replica_groups=mesh['dp'=4,'rad'=8,'azi'=8] {'dp'}, dimensions={0}, use_global_device_ids=true | all-gather | bytes 622080 | tf_op jit(solution)/shard_map/all_gather | solution.py:63
  56.6 1.1 copy.67
  57.7 4.6 copy.69
  63.0 0.9 collective-permute-start.3
  63.9 1.0 constant_dynamic-update-slice_fusion.2
  64.9 0.8 constant_dynamic-update-slice_fusion.1
  65.7 5.6 %collective-permute-done.3 = bf16[1,96,6,1,256]{4,1,3,2,0:T(8,128)(2,1)S(1)} collective-permute-done((bf16[1,96,6,1,256]{4,1,3,2,0:T(8,128)(2,1)S(1)}, bf16[1,96,6,1,256]{4,1,3,2,0:T(8,128)(2,1)S(1)}, u32[]{:S(2)}, u32[]{:S(2)}) %collective-permute-start.3) | collective-permute-done | bytes 294944 | tf_op jit(solution)/shard_map/ppermute | solution.py:18
  71.3 0.1 slice.65
  71.5 0.1 slice_select_fusion.1
  71.5 1.8 pad_maximum_fusion.1
  73.4 3.6 copy.88
  77.0 5.5 %pad.3.clone = bf16[96,6,10,1,264]{0,4,2,1,3:T(8,128)(2,1)} pad(bf16[96,6,10,1,256]{0,4,2,1,3:T(8,128)(2,1)} %copy.88, bf16[]{:T(256)} %constant.6.clone.1), padding=0_0x0_0x0_0x0_0x1_7 | pad | bytes 5990402 | tf_op jit(solution)/shard_map/concatenate | solution.py:32
  82.5 7.2 %reshape.21 = bf16[96,6,10,1,8,33]{0,5,4,2,1,3:T(8,128)(2,1)} reshape(bf16[96,6,10,1,264]{0,4,2,1,3:T(8,128)(2,1)} %pad.3.clone) | data formatting | bytes 6082560 | tf_op jit(solution)/shard_map/conv_general_dilated | solution.py:50
  89.7 3.1 copy.66
  92.9 17.9 %add_divide_fusion = (f32[4,8,8,33,96]{4,2,3,1,0:T(8,128)S(1)}, bf16[4,8,8,33,96]{4,2,3,1,0:T(8,128)(2,1)}, f32[4,8,8,33,96]{4,2,3,1,0:T(8,128)S(1)}) fusion(f32[96]{0:T(128)S(1)} %convert_element_type.36, pred[8,33]{0,1:T(8,128)(4,1)S(1)} %copy-done.8, bf16[96,3,3,3,96]{0,4,3,2,1:T(8,128)(2,1)S(1)} %bitcast.55, ...), kind=kOutput, calls=%fused_computation.6 | convolution fusion | flops 4222052352 | bytes 11810952 | tf_op jit(solution)/shard_map/conv_general_dilated | solution.py:50
  110.9 0.8 copy.71
  111.6 0.8 copy.70
  112.4 0.8 copy-done.1
  113.2 1.6 convert_reduce_fusion
  114.8 0.1 fusion.41
  114.9 1.2 copy.73
  116.2 1.2 copy.72
  117.4 2.0 collective-permute-start.4
  119.4 16.3 %copy.83 = bf16[1,96,6,10,256]{1,0,4,3,2:T(2,128)(2,1)} copy(bf16[1,96,6,10,256]{4,1,3,2,0:T(8,128)(2,1)} %get-tuple-element.25) | data formatting | bytes 5898240 | tf_op jit(solution)/shard_map/concatenate | solution.py:32
  135.8 63.2 %fusion.28 = bf16[96,3,3,3,96]{0,4,3,2,1:T(8,128)(2,1)S(1)} fusion(bf16[1,96,6,10,256]{1,0,4,3,2:T(2,128)(2,1)} %copy.83, bf16[1,96,4,8,256]{1,3,4,2,0:T(8,128)(2,1)S(1)} %get-tuple-element.19), kind=kOutput, calls=%fused_computation.38 | convolution fusion | flops 4066744320 | bytes 5019648 | tf_op jit(solution)/shard_map/transpose | solution.py:82
  199.0 0.3 copy.68
  199.2 1.5 slice_bitcast_fusion.3
  200.7 4.6 copy.86
  205.4 1.1 copy.85
  206.4 1.5 copy.75
  208.0 1.5 copy.74
  209.5 0.7 pad_maximum_fusion
  210.3 1.6 copy-done
  211.9 1.2 fusion.39
  213.1 0.5 copy.77
  213.6 3.8 collective-permute-start.7
  217.4 0.5 copy.76
  217.9 0.1 collective-permute-start.6
  218.0 11.4 %all-reduce.2 = bf16[96]{0:T(256)(128)(2,1)S(1)} all-reduce(bf16[96]{0:T(256)(128)(2,1)S(1)} %multiply_convert_fusion.1), channel_id=3, replica_groups=mesh['dp'=4,'rad'=8,'azi'=8] {'dp'}, use_global_device_ids=true, to_apply=%region_3.4.clone | all-reduce | flops 96 | bytes 384
  229.4 0.1 dynamic-slice_convert_fusion
  229.5 3.7 copy.78
  233.3 0.4 pad_maximum_fusion.2
  233.6 0.1 slice.75
  233.8 0.1 maximum_select_fusion.1
  233.9 0.4 maximum_bitcast_fusion
  234.3 3.7 copy.89
  238.0 5.4 %pad.5.clone = bf16[96,6,10,1,264]{0,4,2,1,3:T(8,128)(2,1)} pad(bf16[96,6,10,1,256]{0,4,2,1,3:T(8,128)(2,1)} %copy.89, bf16[]{:T(256)} %constant.6.clone.1), padding=0_0x0_0x0_0x0_0x1_7 | pad | bytes 5990402 | tf_op jit(solution)/shard_map/concatenate | solution.py:32
  243.4 7.2 %reshape.28 = bf16[96,6,10,1,8,33]{0,5,4,2,1,3:T(8,128)(2,1)} reshape(bf16[96,6,10,1,264]{0,4,2,1,3:T(8,128)(2,1)} %pad.5.clone) | data formatting | bytes 6082560 | tf_op jit(solution)/shard_map/conv_general_dilated | solution.py:50
  250.7 3.1 copy.81
  253.9 15.8 %select_convert_fusion = bf16[4,8,8,33,96]{4,2,3,1,0:T(8,128)(2,1)S(1)} fusion(pred[8,33]{0,1:T(8,128)(4,1)S(1)} %copy-done.9, bf16[96,3,3,3,96]{0,4,3,2,1:T(8,128)(2,1)S(1)} %bitcast.56, bf16[96,6,10,1,7,2]{0,4,5,2,1,3:T(8,128)(2,1)S(1)} %slice.76, bf16[96,6,10,1,8,33]{0,4,5,2,1,3:T(8,128)(2,1)S(1)} %copy.81), kind=kOutput, calls=%fused_computation.3 | convolution fusion | flops 4215564288 | bytes 5322504 | tf_op jit(solution)/shard_map/conv_general_dilated | solution.py:50
  269.6 0.3 copy.82
  269.9 0.1 slice_bitcast_fusion.2
  270.1 3.0 copy.87
  273.1 250.6 %all-reduce.5 = (f32[24,2592]{1,0:T(8,128)}, f32[24]{0:T(128)}) all-reduce(bf16[24,2592]{1,0:T(8,128)(2,1)} %reduce-scatter.4.cloned.1.call-done, f32[24]{0:T(128)S(1)} %dynamic-slice_convert_fusion), channel_id=1, replica_groups=mesh['dp'=4,'rad'=8,'azi'=8] {'rad','azi'}, use_global_device_ids=true, to_apply=%region_1.2 | all-reduce | flops 62232 | bytes 373440 | tf_op jit(solution)/shard_map/psum | solution.py:93
  (36 shorter events, 0.3 us)
Async XLA Ops:
  7.2 265.9 %reduce-scatter.4.cloned.1.call-start = ((), (), s32[]{:S(2)}) async-start(), calls=%async_computation.1 | async-start | bytes 645120
  8.4 13.9 %collective-permute-start.1 = (bf16[1,96,1,8,256]{4,3,2,1,0:T(8,128)(2,1)S(1)}, bf16[1,96,1,8,256]{4,3,2,1,0:T(8,128)(2,1)S(1)}, u32[]{:S(2)}, u32[]{:S(2)}) collective-permute-start(bf16[1,96,1,8,256]{4,3,2,1,0:T(8,128)(2,1)S(1)} %get-tuple-element.36), channel_id=1, source_target_pairs={{8,0},{16,8},{24,16},{32,24},{40,32},{48,40},{56,48},{0,56},{9,1},... | collective-permute-start | bytes 1179656 | tf_op jit(solution)/shard_map/ppermute | solution.py:18
  12.8 20.8 %copy-start.5 = (u32[256]{0:T(256)S(1)}, u32[256]{0:T(256)}, u32[]{:S(2)}) copy-start(u32[256]{0:T(256)} %constant.33) | copy-start | bytes 3076
  12.8 22.0 %copy-start.7 = (bf16[24]{0:T(256)(128)(2,1)S(1)}, bf16[24]{0:T(256)(128)(2,1)}, u32[]{:S(2)}) copy-start(bf16[24]{0:T(256)(128)(2,1)} %param.6) | copy-start | bytes 148
  12.8 17.5 %collective-permute-start = (bf16[1,96,1,8,256]{4,3,2,1,0:T(8,128)(2,1)S(1)}, bf16[1,96,1,8,256]{4,3,2,1,0:T(8,128)(2,1)S(1)}, u32[]{:S(2)}, u32[]{:S(2)}) collective-permute-start(bf16[1,96,1,8,256]{4,3,2,1,0:T(8,128)(2,1)S(1)} %get-tuple-element.35), channel_id=1, source_target_pairs={{0,8},{8,16},{16,24},{24,32},{32,40},{40,48},{48,56},{56,0},{1,9},... | collective-permute-start | bytes 1179656 | tf_op jit(solution)/shard_map/ppermute | solution.py:16
  33.6 30.3 %collective-permute-start.2 = (bf16[1,96,6,1,256]{4,1,3,2,0:T(8,128)(2,1)}, bf16[1,96,6,1,256]{4,1,3,2,0:T(8,128)(2,1)}, u32[]{:S(2)}, u32[]{:S(2)}) collective-permute-start(bf16[1,96,6,1,256]{4,1,3,2,0:T(8,128)(2,1)} %copy.97), channel_id=1, source_target_pairs={{0,1},{1,2},{2,3},{3,4},{4,5},{5,6},{6,7},{7,0},{8,9},{9,10},{10,1... | collective-permute-start | bytes 884744 | tf_op jit(solution)/shard_map/ppermute | solution.py:16
  63.0 8.3 %collective-permute-start.3 = (bf16[1,96,6,1,256]{4,1,3,2,0:T(8,128)(2,1)S(1)}, bf16[1,96,6,1,256]{4,1,3,2,0:T(8,128)(2,1)S(1)}, u32[]{:S(2)}, u32[]{:S(2)}) collective-permute-start(bf16[1,96,6,1,256]{4,1,3,2,0:T(8,128)(2,1)S(1)} %copy.98), channel_id=1, source_target_pairs={{1,0},{2,1},{3,2},{4,3},{5,4},{6,5},{7,6},{0,7},{9,8},{10,9},{11,1... | collective-permute-start | bytes 884744 | tf_op jit(solution)/shard_map/ppermute | solution.py:18
  89.7 3.2 copy-start.3
  89.7 3.2 copy-start.8
  111.6 1.6 copy-start.1
  116.2 90.3 %collective-permute-start.5 = (bf16[1,96,1,8,256]{4,3,2,1,0:T(8,128)(2,1)}, bf16[1,96,1,8,256]{4,3,2,1,0:T(8,128)(2,1)}, u32[]{:S(2)}, u32[]{:S(2)}) collective-permute-start(bf16[1,96,1,8,256]{4,3,2,1,0:T(8,128)(2,1)} %copy.73), channel_id=1, source_target_pairs={{8,0},{16,8},{24,16},{32,24},{40,32},{48,40},{56,48},{0,56},{9,1},... | collective-permute-start | bytes 1179656 | tf_op jit(solution)/shard_map/ppermute | solution.py:18
  117.4 90.6 %collective-permute-start.4 = (bf16[1,96,1,8,256]{4,3,2,1,0:T(8,128)(2,1)}, bf16[1,96,1,8,256]{4,3,2,1,0:T(8,128)(2,1)}, u32[]{:S(2)}, u32[]{:S(2)}) collective-permute-start(bf16[1,96,1,8,256]{4,3,2,1,0:T(8,128)(2,1)} %copy.72), channel_id=1, source_target_pairs={{0,8},{8,16},{16,24},{24,32},{32,40},{40,48},{48,56},{56,0},{1,9},... | collective-permute-start | bytes 1179656 | tf_op jit(solution)/shard_map/ppermute | solution.py:16
  135.8 63.2 %copy-start.2 = (bf16[4,8,8,33,96]{4,2,3,1,0:T(8,128)(2,1)S(1)}, bf16[4,8,8,33,96]{4,2,3,1,0:T(8,128)(2,1)}, u32[]{:S(2)}) copy-start(bf16[4,8,8,33,96]{4,2,3,1,0:T(8,128)(2,1)} %get-tuple-element.21) | copy-start | bytes 4866052
  210.3 1.6 copy-start
  211.9 6.1 %copy-start.6 = (f32[96]{0:T(128)S(1)}, f32[96]{0:T(128)}, u32[]{:S(2)}) copy-start(f32[96]{0:T(128)} %get-tuple-element.18) | copy-start | bytes 1156
  213.6 19.7 %collective-permute-start.7 = (bf16[1,96,6,1,256]{4,1,3,2,0:T(8,128)(2,1)S(1)}, bf16[1,96,6,1,256]{4,1,3,2,0:T(8,128)(2,1)S(1)}, u32[]{:S(2)}, u32[]{:S(2)}) collective-permute-start(bf16[1,96,6,1,256]{4,1,3,2,0:T(8,128)(2,1)S(1)} %copy.77), channel_id=1, source_target_pairs={{1,0},{2,1},{3,2},{4,3},{5,4},{6,5},{7,6},{0,7},{9,8},{10,9},{11,1... | collective-permute-start | bytes 884744 | tf_op jit(solution)/shard_map/ppermute | solution.py:18
  217.9 15.4 %collective-permute-start.6 = (bf16[1,96,6,1,256]{4,1,3,2,0:T(8,128)(2,1)S(1)}, bf16[1,96,6,1,256]{4,1,3,2,0:T(8,128)(2,1)S(1)}, u32[]{:S(2)}, u32[]{:S(2)}) collective-permute-start(bf16[1,96,6,1,256]{4,1,3,2,0:T(8,128)(2,1)S(1)} %copy.76), channel_id=1, source_target_pairs={{0,1},{1,2},{2,3},{3,4},{4,5},{5,6},{6,7},{7,0},{8,9},{9,10},{10,1... | collective-permute-start | bytes 884744 | tf_op jit(solution)/shard_map/ppermute | solution.py:16
  250.7 3.2 copy-start.4
  250.7 3.2 copy-start.9
Sparse Core Ops, SparseCore 0:
  206.6 25.3 reduce-scatter.3
where the time goes:
time: 537 us; the launch traced here: 531 us
  blocking collectives  283 us (53%)
  matrix products  96.9 us (18%)
  local copies, waits for them, and re-layouts  93.1 us (17%)
  waiting for transfers between devices  23.2 us (4%)
  between operations  16.1 us (3%)
  starting transfers between devices  11.3 us (2%)
  other arithmetic  6.9 us (1%)
    psum x1, blocking collectives, on_device(): lax.psum((group_part[0], group_part[1]), ('rad', 'azi'))  251 us
    transpose x1, matrix products, on_device(): kernel_grad.transpose(1, 2, 3, 4, 0).reshape(out_rows, 27 * channels)  63.2 us
    conv_general_dilated x2, matrix products, convolve(): lax.conv_general_dilated(left, right, (1, 1, 1), 'VALID', dimension_numbe...  33.7 us
    concatenate x3, local copies, waits for them, and re-layouts, rim_fix(): return jnp.concatenate([low_rim, extended[:, :, 1:-1], high_rim], axis=2)  27.2 us
    unnamed x32, local copies, waits for them, and re-layouts  25.5 us
    conv_general_dilated x6, local copies, waits for them, and re-layouts, convolve(): lax.conv_general_dilated(left, right, (1, 1, 1), 'VALID', dimension_numbe...  20.8 us
    unnamed x2, blocking collectives  20.1 us
    ppermute x4, waiting for transfers between devices, with_halo(): lax.ppermute(head, axis, [((i + 1) % count, i) for i in range(count)])  15.1 us
  transfers between devices with their start and end apart: 9, of which 3 were waited for; matrix products, arithmetic and copies ran while one was open for 28% of the time, Pallas kernels for 0%

commit v1 on v0

v1 whole, which is shorter than its diff:
```python
import jax
import jax.numpy as jnp
from jax import lax
from jax.experimental import pallas as pl
from jax.experimental.pallas import tpu as pltpu
from jax.sharding import PartitionSpec as P

inverse_scale = 1.0 / 1024.0
bf16 = jnp.bfloat16
f32 = jnp.float32
C = 96
K9 = 9 * C
RAD_AZI = ("rad", "azi")


def params(*semantics):
    return pltpu.CompilerParams(
        dimension_semantics=semantics, vmem_limit_bytes=56 * 1024 * 1024
    )


def full(shape):
    return pl.BlockSpec(shape, lambda *_: (0,) * len(shape))


def put_rows(tmp, cells):
    c, na, z = cells.shape
    flat = cells.reshape(c * na, z)
    for h in range(z // 128):
        tmp[h] = flat[:, 128 * h : 128 * h + 128]


def get_rows(tmp, c, na):
    flat = jnp.concatenate([tmp[h] for h in range(tmp.shape[0])], axis=1)
    return flat.reshape(c, na, flat.shape[1])


def get_column(tmp, a, c, na):
    return jnp.concatenate(
        [tmp[h, pl.ds(a, c, stride=na), :] for h in range(tmp.shape[0])], axis=1
    )


def put_column(tmp, a, na, column):
    c = column.shape[0]
    for h in range(tmp.shape[0]):
        tmp[h, pl.ds(a, c, stride=na), :] = column[:, 128 * h : 128 * h + 128]


def to_columns_body(x_ref, o_ref, tmp):
    rows, az = x_ref.shape[1], x_ref.shape[3]
    put_rows(tmp, x_ref[0, :, 0].astype(f32))
    for a in range(az):
        o_ref[0, a] = get_column(tmp, a, rows, az).astype(bf16)


def to_columns(field):
    _, c, nr, na, nz = field.shape
    return pl.pallas_call(
        to_columns_body,
        grid=(nr,),
        in_specs=[pl.BlockSpec((1, c, 1, na, nz), lambda r: (0, 0, r, 0, 0))],
        out_specs=pl.BlockSpec((1, na, c, nz), lambda r: (r, 0, 0, 0)),
        out_shape=jax.ShapeDtypeStruct((nr, na, c, nz), bf16),
        scratch_shapes=[pltpu.VMEM((nz // 128, c * na, 128), f32)],
        compiler_params=params("arbitrary"),
        name="to_columns",
    )(field)


def fill(ext, x_ref, lo_ref, hi_ref, left_ref, right_ref):
    nr, na = x_ref.shape[0], x_ref.shape[1]
    ext[0, 1 : na + 1] = lo_ref[...]
    ext[nr + 1, 1 : na + 1] = hi_ref[...]
    for r in range(nr):
        ext[r + 1, 1 : na + 1] = x_ref[r]
    ext[:, 0] = left_ref[...]
    ext[:, na + 1] = right_ref[...]


def window(ext, r, a):
    c, z = ext.shape[2], ext.shape[3]
    return jnp.concatenate(
        [ext[r + i, pl.ds(a, 3)].reshape(3 * c, z) for i in range(3)], axis=0
    )


def taps_sum(parts):
    c = parts.shape[0] // 3
    z = parts.shape[1]
    lane = lax.broadcasted_iota(jnp.int32, (c, z), 1)
    before = jnp.where(lane == 0, 0.0, pltpu.roll(parts[:c], 1, 1))
    after = jnp.where(lane == z - 1, 0.0, pltpu.roll(parts[2 * c :], z - 1, 1))
    return parts[c : 2 * c] + before + after


def forward_body(x_ref, lo_ref, hi_ref, left_ref, right_ref, w_ref, b_ref, cot_ref,
                 out_ref, delta_ref, bsum_ref, ext, cot, res):
    r = pl.program_id(0)
    na, c, z = x_ref.shape[1:]

    @pl.when(r == 0)
    def _():
        fill(ext, x_ref, lo_ref, hi_ref, left_ref, right_ref)
        bsum_ref[...] = jnp.zeros_like(bsum_ref)

    put_rows(cot, cot_ref[0, :, 0].astype(f32))
    bias = b_ref[...].astype(f32)

    def pair(p, carry):
        a = 2 * p
        cols = jnp.concatenate([window(ext, r, a), window(ext, r, a + 1)], axis=1)
        both = jnp.dot(w_ref[...], cols, preferred_element_type=f32)
        for s in range(2):
            pre = taps_sum(both[:, s * z : (s + 1) * z]) + bias
            gate = jax.nn.sigmoid(pre)
            put_column(res, a + s, na, pre * gate)
            d = get_column(cot, a + s, c, na) * gate * (1.0 + pre * (1.0 - gate))
            d = d.astype(bf16)
            delta_ref[0, a + s] = d
            bsum_ref[...] += d.astype(f32)
        return carry

    lax.fori_loop(0, na // 2, pair, 0)
    out_ref[0, :, 0] = get_rows(res, c, na).astype(bf16)


def forward(x, lo, hi, left, right, w, b, cot):
    nr, na, c, z = x.shape
    return pl.pallas_call(
        forward_body,
        grid=(nr,),
        in_specs=[full(x.shape), full(lo.shape), full(hi.shape), full(left.shape),
                  full(right.shape), full(w.shape), full(b.shape),
                  pl.BlockSpec((1, c, 1, na, z), lambda r: (0, 0, r, 0, 0))],
        out_specs=[pl.BlockSpec((1, c, 1, na, z), lambda r: (0, 0, r, 0, 0)),
                   pl.BlockSpec((1, na, c, z), lambda r: (r, 0, 0, 0)),
                   full((c, z))],
        out_shape=[jax.ShapeDtypeStruct(cot.shape, bf16),
                   jax.ShapeDtypeStruct(x.shape, bf16),
                   jax.ShapeDtypeStruct((c, z), f32)],
        scratch_shapes=[pltpu.VMEM((nr + 2, na + 2, c, z), bf16),
                        pltpu.VMEM((z // 128, c * na, 128), f32),
                        pltpu.VMEM((z // 128, c * na, 128), f32)],
        compiler_params=params("arbitrary"),
        name="forward",
    )(x, lo, hi, left, right, w, b, cot)


def backward_body(x_ref, lo_ref, hi_ref, left_ref, right_ref, w_ref, out_ref, ext, res):
    r = pl.program_id(0)
    na, c, z = x_ref.shape[1:]

    @pl.when(r == 0)
    def _():
        fill(ext, x_ref, lo_ref, hi_ref, left_ref, right_ref)

    def pair(p, carry):
        a = 2 * p
        cols = jnp.concatenate([window(ext, r, a), window(ext, r, a + 1)], axis=1)
        both = jnp.dot(w_ref[...], cols, preferred_element_type=f32)
        for s in range(2):
            put_column(res, a + s, na, taps_sum(both[:, s * z : (s + 1) * z]))
        return carry

    lax.fori_loop(0, na // 2, pair, 0)
    out_ref[0, :, 0] = get_rows(res, c, na).astype(bf16)


def backward(x, lo, hi, left, right, w):
    nr, na, c, z = x.shape
    return pl.pallas_call(
        backward_body,
        grid=(nr,),
        in_specs=[full(x.shape), full(lo.shape), full(hi.shape), full(left.shape),
                  full(right.shape), full(w.shape)],
        out_specs=pl.BlockSpec((1, c, 1, na, z), lambda r: (0, 0, r, 0, 0)),
        out_shape=jax.ShapeDtypeStruct((1, c, nr, na, z), bf16),
        scratch_shapes=[pltpu.VMEM((nr + 2, na + 2, c, z), bf16),
                        pltpu.VMEM((z // 128, c * na, 128), f32)],
        compiler_params=params("arbitrary"),
        name="backward",
    )(x, lo, hi, left, right, w)


def weight_body(x_ref, lo_ref, hi_ref, left_ref, right_ref, d_ref, bsum_ref, out_ref,
                ext, acc, flat):
    r = pl.program_id(0)
    nr, na, c, z = x_ref.shape

    @pl.when(r == 0)
    def _():
        fill(ext, x_ref, lo_ref, hi_ref, left_ref, right_ref)
        acc[...] = jnp.zeros_like(acc)

    lane = lax.broadcasted_iota(jnp.int32, (c, z), 1)

    def pair(p, carry):
        a = 2 * p
        cols = jnp.concatenate([window(ext, r, a), window(ext, r, a + 1)], axis=1)
        rows = []
        for s in range(2):
            d = d_ref[r, a + s].astype(f32)
            ahead = jnp.where(lane == z - 1, 0.0, pltpu.roll(d, z - 1, 1))
            behind = jnp.where(lane == 0, 0.0, pltpu.roll(d, 1, 1))
            rows.append(jnp.concatenate([ahead, d, behind], axis=0).astype(bf16))
        rows = jnp.concatenate(rows, axis=1)
        acc[...] += lax.dot_general(rows, cols, (((1,), (1,)), ((), ())),
                                    preferred_element_type=f32)
        return carry

    lax.fori_loop(0, na // 2, pair, 0)

    @pl.when(r == nr - 1)
    def _():
        flat[...] = jnp.zeros_like(flat)
        for ij in range(9):
            for k in range(3):
                t = 3 * ij + k
                flat[:, t * c : (t + 1) * c] = acc[k * c : (k + 1) * c, ij * c : (ij + 1) * c]
        flat[:, 27 * c : 27 * c + 1] = jnp.sum(bsum_ref[...], axis=1, keepdims=True)
        for g in range(c // 8):
            for l in range(21):
                out_ref[g // 3, (g % 3) * 21 + l] = (
                    flat[8 * g : 8 * g + 8, 128 * l : 128 * l + 128] * inverse_scale
                ).astype(bf16)
        out_ref[:, 63] = jnp.zeros((4, 8, 128), bf16)


def weight_terms(x, lo, hi, left, right, d, bsum):
    nr, na, c, z = x.shape
    return pl.pallas_call(
        weight_body,
        grid=(nr,),
        in_specs=[full(x.shape), full(lo.shape), full(hi.shape), full(left.shape),
                  full(right.shape), full(d.shape), full(bsum.shape)],
        out_specs=full((4, 64, 8, 128)),
        out_shape=jax.ShapeDtypeStruct((4, 64, 8, 128), bf16),
        scratch_shapes=[pltpu.VMEM((nr + 2, na + 2, c, z), bf16),
                        pltpu.VMEM((3 * c, K9), f32),
                        pltpu.VMEM((c, 21 * 128), f32)],
        compiler_params=params("arbitrary"),
        name="weight_terms",
    )(x, lo, hi, left, right, d, bsum)


def rad_shift(x, step):
    n = lax.axis_size("rad")
    return lax.ppermute(x, "rad", [(i, i + step) for i in range(n) if 0 <= i + step < n])


def azi_shift(x, step):
    n = lax.axis_size("azi")
    return lax.ppermute(x, "azi", [(i, (i + step) % n) for i in range(n)])


def halos(x):
    hi = rad_shift(x[0], -1)
    lo = rad_shift(x[-1], 1)
    first = jnp.concatenate([lo[:1], x[:, 0], hi[:1]], axis=0)
    last = jnp.concatenate([lo[-1:], x[:, -1], hi[-1:]], axis=0)
    right = azi_shift(first, -1)
    left = azi_shift(last, 1)
    return lo, hi, left, right


def exchange(x, axis):
    return lax.all_to_all(x, axis, 0, 0, tiled=True)


def reduce_terms(tiles):
    def total(x, parts):
        return jnp.sum(x.reshape((parts, -1) + x.shape[1:]).astype(f32), axis=0)

    mine = total(exchange(tiles.reshape(256, 8, 128), "dp"), 4).astype(bf16)
    piece = total(exchange(mine, RAD_AZI), 64).astype(bf16)
    return exchange(jnp.broadcast_to(piece, (64, 8, 128)), RAD_AZI)


def on_device(inputs, weight, bias, cotangent):
    c = inputs.shape[1]
    x = to_columns(inputs)
    packed = jnp.concatenate(
        [weight, jnp.broadcast_to(bias[:, None], (weight.shape[0], 128))], axis=1
    )
    rows = packed.shape[0]
    d0 = lax.axis_index("dp")
    pieces = [packed] + [
        lax.ppermute(packed, "dp", [(i, (i + s) % 4) for i in range(4)]) for s in (1, 2, 3)
    ]
    stacked = jnp.stack(pieces)
    order = (d0 - jnp.arange(4)) % 4
    whole = stacked[order].reshape(4 * rows, packed.shape[1])
    taps = whole[:, : 27 * c].reshape(c, 3, 3, 3, c)
    w_fwd = taps.transpose(3, 0, 1, 2, 4).reshape(3 * c, K9)
    w_back = taps[:, ::-1, ::-1, ::-1].transpose(3, 4, 1, 2, 0).reshape(3 * c, K9)
    b_col = whole[:, 27 * c : 27 * c + 1]

    lo, hi, left, right = halos(x)
    output, delta, bsum = forward(x, lo, hi, left, right, w_fwd, b_col, cotangent)
    dlo, dhi, dleft, dright = halos(delta)
    terms = weight_terms(x, lo, hi, left, right, delta, bsum)
    input_grad = backward(delta, dlo, dhi, dleft, dright, w_back)
    tiles = reduce_terms(terms)
    summed = tiles[:63].reshape(3, 21, 8, 128).transpose(0, 2, 1, 3).reshape(24, 21 * 128)
    summed = summed.astype(f32)
    return output, input_grad, summed[:, : 27 * c], summed[:, 27 * c]


def solution(mesh):
    return jax.shard_map(
        on_device,
        mesh=mesh,
        in_specs=(
            P("dp", None, "rad", "azi", None),
            P("dp", None),
            P("dp"),
            P("dp", None, "rad", "azi", None),
        ),
        out_specs=(
            P("dp", None, "rad", "azi", None),
            P("dp", None, "rad", "azi", None),
            P("dp", None),
            P("dp"),
        ),
        check_vma=False,
    )
```

time: 537 us -> 138 us (0.26)
  blocking collectives: 283 us -> 0 us
  matrix products: 96.9 us -> 0 us
  local copies, waits for them, and re-layouts: 93.1 us -> 13.8 us
  starting transfers between devices: 11.3 us -> 62.5 us
  Pallas kernels: 0 us -> 42.4 us
  between operations: 16.1 us -> 0.89 us
  waiting for transfers between devices: 23.2 us -> 13.8 us
    psum x1 -> x0, blocking collectives: 251 us -> none  [on_device(): lax.psum((group_part[0], group_part[1]), ('rad', 'azi'))]
    transpose x1 -> x0, matrix products: 63.2 us -> none  [on_device(): kernel_grad.transpose(1, 2, 3, 4, 0).reshape(out_rows, 27 * channels)]
    pallas_call x0 -> x4, Pallas kernels: none -> 42.4 us  [the longest x1 13.8 us: forward(): pl.pallas_call(forward_body, grid=(nr,), in_specs=[full(x.shape), full(lo...]
    all_to_all x0 -> x3, starting transfers between devices: none -> 33.9 us  [exchange(): return lax.all_to_all(x, axis, 0, 0, tiled=True)]
    conv_general_dilated x2 -> x0, matrix products: 33.7 us -> none  [convolve(): lax.conv_general_dilated(left, right, (1, 1, 1), 'VALID', dimension_numbe...]
    concatenate x5 -> x0, local copies, waits for them, and re-layouts: 31 us -> none  [the longest x3 27.2 us: rim_fix(): return jnp.concatenate([low_rim, extended[:, :, 1:-1], high_rim], axis=2)]
    unnamed x32 -> x18, local copies, waits for them, and re-layouts: 25.5 us -> 2.15 us
    conv_general_dilated x6 -> x0, local copies, waits for them, and re-layouts: 20.8 us -> none  [convolve(): lax.conv_general_dilated(left, right, (1, 1, 1), 'VALID', dimension_numbe...]
  transfers between devices with their start and end apart: 9 -> 14, of which waited for: 3 -> 4; matrix products, arithmetic and copies ran while one was open for 28% -> 9% of each run, Pallas kernels for 0% -> 12%
where the time goes in v1:
time: 138 us; the launch traced here: 137 us
  starting transfers between devices  62.5 us (45%)
  Pallas kernels  42.4 us (31%)
  local copies, waits for them, and re-layouts  13.8 us (10%)
  waiting for transfers between devices  13.8 us (10%)
  other arithmetic  3.58 us (3%)
    all_to_all x3, starting transfers between devices, exchange(): return lax.all_to_all(x, axis, 0, 0, tiled=True)  33.9 us
    ppermute x4, starting transfers between devices, rad_shift(): lax.ppermute(x, 'rad', [(i, i + step) for i in range(n) if 0 <= i + step...  16.5 us
    pallas_call x1, Pallas kernels, forward(): pl.pallas_call(forward_body, grid=(nr,), in_specs=[full(x.shape), full(lo...  13.8 us
    pallas_call x1, Pallas kernels, weight_terms(): pl.pallas_call(weight_body, grid=(nr,), in_specs=[full(x.shape), full(lo....  12.4 us
    pallas_call x1, Pallas kernels, backward(): pl.pallas_call(backward_body, grid=(nr,), in_specs=[full(x.shape), full(l...  12.2 us
    ppermute x4, starting transfers between devices, azi_shift(): return lax.ppermute(x, 'azi', [(i, (i + step) % n) for i in range(n)])  7.86 us
    ppermute x4, waiting for transfers between devices, rad_shift(): lax.ppermute(x, 'rad', [(i, i + step) for i in range(n) if 0 <= i + step...  6.91 us
    all_to_all x3, waiting for transfers between devices, exchange(): return lax.all_to_all(x, axis, 0, 0, tiled=True)  5.96 us
  transfers between devices with their start and end apart: 14, of which 4 were waited for; matrix products, arithmetic and copies ran while one was open for 9% of the time, Pallas kernels for 12%

profile of v1, /device:TPU:2, one launch (start us, length us, event | category | flops | bytes accessed | tf_op | source)
XLA Modules:
  0.0 136.9 jit_solution(5510260290686838158)
XLA Ops:
  0.6 0.7 broadcast_in_dim.4
  1.4 1.0 fusion.2
  2.3 2.2 %collective-permute-start.5 = (bf16[24,2720]{1,0:T(8,128)(2,1)S(1)}, bf16[24,2720]{1,0:T(8,128)(2,1)S(1)}, u32[]{:S(2)}, u32[]{:S(2)}) collective-permute-start(bf16[24,2720]{1,0:T(8,128)(2,1)S(1)} %get-tuple-element.27), channel_id=1, source_target_pairs={{0,128},{64,192},{128,0},{192,64},{1,129},{65,193},{129,1},{193,65... | collective-permute-start | bytes 391688 | tf_op jit(solution)/shard_map/ppermute | solution.py:289
  4.5 1.6 %collective-permute-start.4 = (bf16[24,2720]{1,0:T(8,128)(2,1)S(1)}, bf16[24,2720]{1,0:T(8,128)(2,1)S(1)}, u32[]{:S(2)}, u32[]{:S(2)}) collective-permute-start(bf16[24,2720]{1,0:T(8,128)(2,1)S(1)} %get-tuple-element.27), channel_id=1, source_target_pairs={{0,64},{64,128},{128,192},{192,0},{1,65},{65,129},{129,193},{193,1... | collective-permute-start | bytes 391688 | tf_op jit(solution)/shard_map/ppermute | solution.py:289
  6.1 0.4 collective-permute-start.6
  6.5 3.9 %to_columns.1.x_ref = bf16[4,8,96,256]{3,2,1,0:T(8,128)(2,1)} custom-call(bf16[1,96,4,8,256]{4,3,2,1,0:T(8,128)(2,1)} %x_ref.1), custom_call_target="tpu_custom_call" | custom-call | tf_op jit(solution)/shard_map/to_columns/pallas_call | solution.py:59
  10.4 1.2 slice_bitcast_fusion
  11.6 1.3 collective-permute-start.1
  12.9 4.6 %collective-permute-start = (bf16[8,96,256]{2,1,0:T(8,128)(2,1)S(1)}, bf16[8,96,256]{2,1,0:T(8,128)(2,1)S(1)}, u32[]{:S(2)}, u32[]{:S(2)}) collective-permute-start(bf16[8,96,256]{2,1,0:T(8,128)(2,1)S(1)} %get-tuple-element.17), channel_id=1, source_target_pairs={{0,8},{8,16},{16,24},{24,32},{32,40},{40,48},{48,56},{1,9},{9,17},... | collective-permute-start | bytes 1179656 | tf_op jit(solution)/shard_map/ppermute | solution.py:249
  17.4 1.1 slice_bitcast_fusion.6
  18.5 6.9 %collective-permute-done.1.hi_ref = bf16[8,96,256]{2,1,0:T(8,128)(2,1)S(1)} collective-permute-done((bf16[8,96,256]{2,1,0:T(8,128)(2,1)S(1)}, bf16[8,96,256]{2,1,0:T(8,128)(2,1)S(1)}, u32[]{:S(2)}, u32[]{:S(2)}) %collective-permute-start.1) | collective-permute-done | bytes 393248 | tf_op jit(solution)/shard_map/ppermute | solution.py:249
  25.5 0.0 collective-permute-done.lo_ref
  25.5 0.0 copy-start.2
  25.5 0.8 pad_maximum_fusion.1
  26.3 0.0 collective-permute-start.2
  26.3 0.7 pad_maximum_fusion.2
  27.1 3.9 %collective-permute-start.3 = (bf16[6,96,256]{2,1,0:T(8,128)(2,1)}, bf16[6,96,256]{2,1,0:T(8,128)(2,1)S(1)}, u32[]{:S(2)}, u32[]{:S(2)}) collective-permute-start(bf16[6,96,256]{2,1,0:T(8,128)(2,1)} %pad_maximum_fusion.2), channel_id=1, source_target_pairs={{0,7},{1,0},{2,1},{3,2},{4,3},{5,4},{6,5},{7,6},{8,15},{9,8},{10,9... | collective-permute-start | bytes 884744 | tf_op jit(solution)/shard_map/ppermute | solution.py:254
  30.9 0.0 collective-permute-done.5
  30.9 0.0 collective-permute-done.4
  30.9 0.0 collective-permute-done.6
  30.9 0.1 pad_maximum_fusion
  31.0 0.6 gather_fusion
  31.6 0.0 copy-done.1
  31.6 0.0 copy-done.2
  31.6 0.7 slice.95.b_ref
  32.4 0.3 copy.23
  32.7 0.7 copy.24
  33.3 1.3 reshape.87.w_ref
  34.6 0.2 collective-permute-done.2.left_ref
  34.8 0.7 collective-permute-done.3.right_ref
  35.5 0.0 copy-done.3
  35.5 0.7 copy-done.4
  36.2 13.8 %forward.1 = (bf16[1,96,4,8,256]{4,3,2,1,0:T(8,128)(2,1)}, bf16[4,8,96,256]{3,2,1,0:T(8,128)(2,1)}, f32[96,256]{1,0:T(8,128)}) custom-call(bf16[4,8,96,256]{3,2,1,0:T(8,128)(2,1)} %to_columns.1.x_ref, bf16[8,96,256]{2,1,0:T(8,128)(2,1)} %copy-done.2, bf16[8,96,256]{2,1,0:T(8,128)(2,1)} %copy-done.1, bf16[6,96,256]{2,1,0:T(8,128)(2,1)} %copy-done.3, ...), custom_call_target="tpu_custom_call" | custom-call | tf_op jit(solution)/shard_map/forward/pallas_call | solution.py:130
  50.1 12.4 %weight_terms.1 = bf16[4,64,8,128]{3,2,1,0:T(8,128)(2,1)} custom-call(bf16[4,8,96,256]{3,2,1,0:T(8,128)(2,1)} %to_columns.1.x_ref, bf16[8,96,256]{2,1,0:T(8,128)(2,1)} %copy-done.2, bf16[8,96,256]{2,1,0:T(8,128)(2,1)} %copy-done.1, bf16[6,96,256]{2,1,0:T(8,128)(2,1)} %copy-done.3, bf16[6,96,256]{2,1,0:T(8,128)(2,1)} %copy-done.4, ...), custom_call_target="tpu_custom_call" | custom-call | tf_op jit(solution)/shard_map/weight_terms/pallas_call | solution.py:232
  62.5 6.1 %all-to-all-start = ((bf16[256,8,128]{2,1,0:T(8,128)(2,1)}), bf16[256,8,128]{2,1,0:T(8,128)(2,1)S(1)}, u32[]{:S(2)}, u32[]{:S(2)}) async-start(bf16[256,8,128]{2,1,0:T(8,128)(2,1)} %bitcast.46), calls=%async_computation | async-start | bytes 1048576 | tf_op jit(solution)/shard_map/all_to_all | solution.py:268
  68.6 0.0 copy-done
  68.6 0.9 slice_bitcast_fusion.2
  69.5 1.3 collective-permute-start.8
  70.8 9.4 %collective-permute-start.7 = (bf16[8,96,256]{2,1,0:T(8,128)(2,1)}, bf16[8,96,256]{2,1,0:T(8,128)(2,1)}, u32[]{:S(2)}, u32[]{:S(2)}) collective-permute-start(bf16[8,96,256]{2,1,0:T(8,128)(2,1)} %get-tuple-element.13), channel_id=1, source_target_pairs={{0,8},{8,16},{16,24},{24,32},{32,40},{40,48},{48,56},{1,9},{9,17},... | collective-permute-start | bytes 1179656 | tf_op jit(solution)/shard_map/ppermute | solution.py:249
  80.2 0.0 all-to-all-done
  80.2 0.7 reduce_sum.24
  81.0 18.9 %all-to-all-start.1 = ((bf16[64,8,128]{2,1,0:T(8,128)(2,1)}), bf16[64,8,128]{2,1,0:T(8,128)(2,1)S(1)}, u32[]{:S(2)}, u32[]{:S(2)}) async-start(bf16[64,8,128]{2,1,0:T(8,128)(2,1)} %reduce_sum.24), calls=%async_computation.1 | async-start | bytes 262144 | tf_op jit(solution)/shard_map/all_to_all | solution.py:268
  99.9 0.0 collective-permute-done.8.hi_ref
  99.9 0.0 copy-start.5
  99.9 0.0 collective-permute-done.7.lo_ref
  99.9 0.9 fusion.3
  100.9 0.1 collective-permute-start.9
  101.1 3.9 %collective-permute-start.10 = (bf16[6,96,256]{2,1,0:T(8,128)(2,1)S(1)}, bf16[6,96,256]{2,1,0:T(8,128)(2,1)S(1)}, u32[]{:S(2)}, u32[]{:S(2)}) collective-permute-start(bf16[6,96,256]{2,1,0:T(8,128)(2,1)S(1)} %pad_maximum_fusion.4), channel_id=1, source_target_pairs={{0,7},{1,0},{2,1},{3,2},{4,3},{5,4},{6,5},{7,6},{8,15},{9,8},{10,9... | collective-permute-start | bytes 884744 | tf_op jit(solution)/shard_map/ppermute | solution.py:254
  104.9 6.0 %all-to-all-done.1 = bf16[64,8,128]{2,1,0:T(8,128)(2,1)S(1)} async-done(((bf16[64,8,128]{2,1,0:T(8,128)(2,1)}), bf16[64,8,128]{2,1,0:T(8,128)(2,1)S(1)}, u32[]{:S(2)}, u32[]{:S(2)}) %all-to-all-start.1) | async-done | bytes 131104 | tf_op jit(solution)/shard_map/all_to_all | solution.py:268
  110.9 0.1 reduce_sum.25
  111.0 0.7 broadcast_in_dim.5
  111.7 9.0 %all-to-all-start.2 = ((bf16[64,8,128]{2,1,0:T(8,128)(2,1)}), bf16[64,8,128]{2,1,0:T(8,128)(2,1)S(1)}, u32[]{:S(2)}, u32[]{:S(2)}) async-start(bf16[64,8,128]{2,1,0:T(8,128)(2,1)} %broadcast_in_dim.5), calls=%async_computation.2 | async-start | bytes 262144 | tf_op jit(solution)/shard_map/all_to_all | solution.py:268
  120.7 0.0 copy-done.5
  120.7 0.5 copy.27
  121.2 1.3 reshape.88.w_ref
  122.5 0.0 collective-permute-done.9.left_ref
  122.5 0.0 collective-permute-done.10.right_ref
  122.5 0.7 copy-done.6
  123.2 0.7 copy-done.7
  123.9 12.2 %backward.1 = bf16[1,96,4,8,256]{4,3,2,1,0:T(8,128)(2,1)} custom-call(bf16[4,8,96,256]{3,2,1,0:T(8,128)(2,1)} %get-tuple-element.8.x_ref.d_ref, bf16[8,96,256]{2,1,0:T(8,128)(2,1)} %collective-permute-done.7.lo_ref, bf16[8,96,256]{2,1,0:T(8,128)(2,1)} %copy-done.5, bf16[6,96,256]{2,1,0:T(8,128)(2,1)} %copy-done.6, bf16[6,96,256]{2,1,0:T(8,128)(2,1)} %copy-done.7, ...), custom_call_target="tpu_custom_call" | custom-call | tf_op jit(solution)/shard_map/backward/pallas_call | solution.py:172
  136.1 0.0 all-to-all-done.2
  136.2 0.0 copy-start.8
  136.2 0.7 slice_reduce_fusion
  136.9 0.0 copy-done.8
  (18 shorter events, 0.3 us)
Async XLA Ops:
  2.3 28.6 %collective-permute-start.5 = (bf16[24,2720]{1,0:T(8,128)(2,1)S(1)}, bf16[24,2720]{1,0:T(8,128)(2,1)S(1)}, u32[]{:S(2)}, u32[]{:S(2)}) collective-permute-start(bf16[24,2720]{1,0:T(8,128)(2,1)S(1)} %get-tuple-element.27), channel_id=1, source_target_pairs={{0,128},{64,192},{128,0},{192,64},{1,129},{65,193},{129,1},{193,65... | collective-permute-start | bytes 391688 | tf_op jit(solution)/shard_map/ppermute | solution.py:289
  4.5 26.4 %collective-permute-start.4 = (bf16[24,2720]{1,0:T(8,128)(2,1)S(1)}, bf16[24,2720]{1,0:T(8,128)(2,1)S(1)}, u32[]{:S(2)}, u32[]{:S(2)}) collective-permute-start(bf16[24,2720]{1,0:T(8,128)(2,1)S(1)} %get-tuple-element.27), channel_id=1, source_target_pairs={{0,64},{64,128},{128,192},{192,0},{1,65},{65,129},{129,193},{193,1... | collective-permute-start | bytes 391688 | tf_op jit(solution)/shard_map/ppermute | solution.py:289
  6.1 24.9 %collective-permute-start.6 = (bf16[24,2720]{1,0:T(8,128)(2,1)S(1)}, bf16[24,2720]{1,0:T(8,128)(2,1)S(1)}, u32[]{:S(2)}, u32[]{:S(2)}) collective-permute-start(bf16[24,2720]{1,0:T(8,128)(2,1)S(1)} %get-tuple-element.27), channel_id=1, source_target_pairs={{0,192},{64,0},{128,64},{192,128},{1,193},{65,1},{129,65},{193,129... | collective-permute-start | bytes 391688 | tf_op jit(solution)/shard_map/ppermute | solution.py:289
  11.6 13.9 %collective-permute-start.1 = (bf16[8,96,256]{2,1,0:T(8,128)(2,1)S(1)}, bf16[8,96,256]{2,1,0:T(8,128)(2,1)S(1)}, u32[]{:S(2)}, u32[]{:S(2)}) collective-permute-start(bf16[8,96,256]{2,1,0:T(8,128)(2,1)S(1)} %get-tuple-element.16), channel_id=1, source_target_pairs={{8,0},{16,8},{24,16},{32,24},{40,32},{48,40},{56,48},{9,1},{17,9},... | collective-permute-start | bytes 1179656 | tf_op jit(solution)/shard_map/ppermute | solution.py:249
  12.9 12.6 %collective-permute-start = (bf16[8,96,256]{2,1,0:T(8,128)(2,1)S(1)}, bf16[8,96,256]{2,1,0:T(8,128)(2,1)S(1)}, u32[]{:S(2)}, u32[]{:S(2)}) collective-permute-start(bf16[8,96,256]{2,1,0:T(8,128)(2,1)S(1)} %get-tuple-element.17), channel_id=1, source_target_pairs={{0,8},{8,16},{16,24},{24,32},{32,40},{40,48},{48,56},{1,9},{9,17},... | collective-permute-start | bytes 1179656 | tf_op jit(solution)/shard_map/ppermute | solution.py:249
  25.4 6.2 %copy-start.1 = (bf16[8,96,256]{2,1,0:T(8,128)(2,1)}, bf16[8,96,256]{2,1,0:T(8,128)(2,1)S(1)}, u32[]{:S(2)}) copy-start(bf16[8,96,256]{2,1,0:T(8,128)(2,1)S(1)} %collective-permute-done.1.hi_ref) | copy-start | bytes 1179652
  25.5 6.2 %copy-start.2 = (bf16[8,96,256]{2,1,0:T(8,128)(2,1)}, bf16[8,96,256]{2,1,0:T(8,128)(2,1)S(1)}, u32[]{:S(2)}) copy-start(bf16[8,96,256]{2,1,0:T(8,128)(2,1)S(1)} %collective-permute-done.lo_ref) | copy-start | bytes 1179652
  26.3 8.5 %collective-permute-start.2 = (bf16[6,96,256]{2,1,0:T(8,128)(2,1)}, bf16[6,96,256]{2,1,0:T(8,128)(2,1)S(1)}, u32[]{:S(2)}, u32[]{:S(2)}) collective-permute-start(bf16[6,96,256]{2,1,0:T(8,128)(2,1)} %pad_maximum_fusion.1), channel_id=1, source_target_pairs={{0,1},{1,2},{2,3},{3,4},{4,5},{5,6},{6,7},{7,0},{8,9},{9,10},{10,1... | collective-permute-start | bytes 884744 | tf_op jit(solution)/shard_map/ppermute | solution.py:254
  27.1 8.5 %collective-permute-start.3 = (bf16[6,96,256]{2,1,0:T(8,128)(2,1)}, bf16[6,96,256]{2,1,0:T(8,128)(2,1)S(1)}, u32[]{:S(2)}, u32[]{:S(2)}) collective-permute-start(bf16[6,96,256]{2,1,0:T(8,128)(2,1)} %pad_maximum_fusion.2), channel_id=1, source_target_pairs={{0,7},{1,0},{2,1},{3,2},{4,3},{5,4},{6,5},{7,6},{8,15},{9,8},{10,9... | collective-permute-start | bytes 884744 | tf_op jit(solution)/shard_map/ppermute | solution.py:254
  34.8 0.7 copy-start.3
  35.5 0.7 copy-start.4
  50.1 18.5 %copy-start = (bf16[4,8,96,256]{3,2,1,0:T(8,128)(2,1)S(1)}, bf16[4,8,96,256]{3,2,1,0:T(8,128)(2,1)}, u32[]{:S(2)}) copy-start(bf16[4,8,96,256]{3,2,1,0:T(8,128)(2,1)} %get-tuple-element.8.x_ref.d_ref) | copy-start | bytes 4718596
  62.5 17.7 %all-to-all-start = ((bf16[256,8,128]{2,1,0:T(8,128)(2,1)}), bf16[256,8,128]{2,1,0:T(8,128)(2,1)S(1)}, u32[]{:S(2)}, u32[]{:S(2)}) async-start(bf16[256,8,128]{2,1,0:T(8,128)(2,1)} %bitcast.46), calls=%async_computation | async-start | bytes 1048576 | tf_op jit(solution)/shard_map/all_to_all | solution.py:268
  69.5 30.4 %collective-permute-start.8 = (bf16[8,96,256]{2,1,0:T(8,128)(2,1)}, bf16[8,96,256]{2,1,0:T(8,128)(2,1)S(1)}, u32[]{:S(2)}, u32[]{:S(2)}) collective-permute-start(bf16[8,96,256]{2,1,0:T(8,128)(2,1)} %get-tuple-element.12), channel_id=1, source_target_pairs={{8,0},{16,8},{24,16},{32,24},{40,32},{48,40},{56,48},{9,1},{17,9},... | collective-permute-start | bytes 1179656 | tf_op jit(solution)/shard_map/ppermute | solution.py:249
  70.8 29.1 %collective-permute-start.7 = (bf16[8,96,256]{2,1,0:T(8,128)(2,1)}, bf16[8,96,256]{2,1,0:T(8,128)(2,1)}, u32[]{:S(2)}, u32[]{:S(2)}) collective-permute-start(bf16[8,96,256]{2,1,0:T(8,128)(2,1)} %get-tuple-element.13), channel_id=1, source_target_pairs={{0,8},{8,16},{16,24},{24,32},{32,40},{40,48},{48,56},{1,9},{9,17},... | collective-permute-start | bytes 1179656 | tf_op jit(solution)/shard_map/ppermute | solution.py:249
  81.0 29.9 %all-to-all-start.1 = ((bf16[64,8,128]{2,1,0:T(8,128)(2,1)}), bf16[64,8,128]{2,1,0:T(8,128)(2,1)S(1)}, u32[]{:S(2)}, u32[]{:S(2)}) async-start(bf16[64,8,128]{2,1,0:T(8,128)(2,1)} %reduce_sum.24), calls=%async_computation.1 | async-start | bytes 262144 | tf_op jit(solution)/shard_map/all_to_all | solution.py:268
  99.9 20.8 %copy-start.5 = (bf16[8,96,256]{2,1,0:T(8,128)(2,1)}, bf16[8,96,256]{2,1,0:T(8,128)(2,1)S(1)}, u32[]{:S(2)}) copy-start(bf16[8,96,256]{2,1,0:T(8,128)(2,1)S(1)} %collective-permute-done.8.hi_ref) | copy-start | bytes 1179652
  100.9 21.6 %collective-permute-start.9 = (bf16[6,96,256]{2,1,0:T(8,128)(2,1)S(1)}, bf16[6,96,256]{2,1,0:T(8,128)(2,1)S(1)}, u32[]{:S(2)}, u32[]{:S(2)}) collective-permute-start(bf16[6,96,256]{2,1,0:T(8,128)(2,1)S(1)} %pad_maximum_fusion.3), channel_id=1, source_target_pairs={{0,1},{1,2},{2,3},{3,4},{4,5},{5,6},{6,7},{7,0},{8,9},{9,10},{10,1... | collective-permute-start | bytes 884744 | tf_op jit(solution)/shard_map/ppermute | solution.py:254
  101.1 21.4 %collective-permute-start.10 = (bf16[6,96,256]{2,1,0:T(8,128)(2,1)S(1)}, bf16[6,96,256]{2,1,0:T(8,128)(2,1)S(1)}, u32[]{:S(2)}, u32[]{:S(2)}) collective-permute-start(bf16[6,96,256]{2,1,0:T(8,128)(2,1)S(1)} %pad_maximum_fusion.4), channel_id=1, source_target_pairs={{0,7},{1,0},{2,1},{3,2},{4,3},{5,4},{6,5},{7,6},{8,15},{9,8},{10,9... | collective-permute-start | bytes 884744 | tf_op jit(solution)/shard_map/ppermute | solution.py:254
  111.7 24.5 %all-to-all-start.2 = ((bf16[64,8,128]{2,1,0:T(8,128)(2,1)}), bf16[64,8,128]{2,1,0:T(8,128)(2,1)S(1)}, u32[]{:S(2)}, u32[]{:S(2)}) async-start(bf16[64,8,128]{2,1,0:T(8,128)(2,1)} %broadcast_in_dim.5), calls=%async_computation.2 | async-start | bytes 262144 | tf_op jit(solution)/shard_map/all_to_all | solution.py:268
  122.5 0.7 copy-start.6
  123.2 0.7 copy-start.7
  136.2 0.7 copy-start.8

commit v2 on v0

v2 whole, which is shorter than its diff:
```python
import jax
import jax.numpy as jnp
from jax import lax
from jax.experimental import pallas as pl
from jax.experimental.pallas import tpu as pltpu
from jax.sharding import PartitionSpec as P


inverse_scale = 1.0 / 1024.0
bf16 = jnp.bfloat16
f32 = jnp.float32
C = 96
K9 = 9 * C


def full(x):
    return pl.BlockSpec(x.shape, lambda *_: (0,) * len(x.shape))


def shape(dims, dtype=bf16):
    return jax.ShapeDtypeStruct(dims, dtype)


def call(body, place, grid, args, in_specs, outs, out_specs, scratch, cost, alias=None):
    return pl.pallas_call(
        body,
        grid_spec=pltpu.PrefetchScalarGridSpec(
            num_scalar_prefetch=1, grid=(grid,), in_specs=in_specs, out_specs=out_specs,
            scratch_shapes=scratch),
        out_shape=outs,
        input_output_aliases=alias or {},
        compiler_params=pltpu.CompilerParams(
            dimension_semantics=("arbitrary",), vmem_limit_bytes=56 * 1024 * 1024),
        cost_estimate=pl.CostEstimate(flops=cost, transcendentals=0, bytes_accessed=4000000),
    )(place, *args)


def put_rows(tmp, cells):
    c, na, z = cells.shape
    flat = cells.reshape(c * na, z)
    for h in range(z // 128):
        tmp[h] = flat[:, 128 * h : 128 * h + 128]


def get_rows(tmp, c, na):
    flat = jnp.concatenate([tmp[h] for h in range(tmp.shape[0])], axis=1)
    return flat.reshape(c, na, flat.shape[1])


def get_column(tmp, a, c, na):
    return jnp.concatenate(
        [tmp[h, pl.ds(a, c, stride=na), :] for h in range(tmp.shape[0])], axis=1
    )


def put_column(tmp, a, na, column):
    c = column.shape[0]
    for h in range(tmp.shape[0]):
        tmp[h, pl.ds(a, c, stride=na), :] = column[:, 128 * h : 128 * h + 128]


def columns_body(place, x_ref, o_ref, near_ref, far_ref, tmp):
    c, nr, na = x_ref.shape[1:4]
    p = place[0]
    for r in range(nr):
        put_rows(tmp, x_ref[0, :, r].astype(f32))
        for a in range(na):
            o_ref[r, a] = get_column(tmp, a, c, na).astype(bf16)
        near_ref[r] = o_ref[r, (na - 1) * (1 - p)]
        far_ref[r] = o_ref[r, (na - 1) * p]


def to_columns(place, field):
    _, c, nr, na, nz = field.shape
    face = shape((nr, c, nz))
    part = c // 3
    face_spec = pl.BlockSpec((nr, part, nz), lambda g, _: (0, g, 0))
    return call(
        columns_body, place, 3, (field,),
        [pl.BlockSpec((1, part, nr, na, nz), lambda g, _: (0, g, 0, 0, 0))],
        [shape((nr, na, c, nz)), face, face],
        [pl.BlockSpec((nr, na, part, nz), lambda g, _: (0, 0, g, 0)), face_spec, face_spec],
        [pltpu.VMEM((nz // 128, part * na, 128), f32)], 10000000)


ANY = pl.BlockSpec(memory_space=pl.ANY)


def edges_body(place, rows, near, far, out_near, out_far, buf, sems):
    p, q = place[0], place[1]
    last, na = rows.shape[0] - 1, rows.shape[1]
    right, left = (na + 1) * (1 - p), (na + 1) * p
    step = (near.shape[0] - 1) // last
    loads = []
    for k, r in enumerate((last * (1 - q), last * q)):
        for n, (src, dst) in enumerate((
            (rows.at[r], buf.at[k, pl.ds(1, na)]),
            (near.at[step * r], buf.at[k, right]),
            (far.at[step * r], buf.at[k, left]),
        )):
            loads.append(pltpu.make_async_copy(src, dst, sems.at[k, n]))
    stores = [pltpu.make_async_copy(buf.at[k], out, sems.at[k, 3])
              for k, out in enumerate((out_near, out_far))]
    for copy in loads:
        copy.start()
    for k, store in enumerate(stores):
        for copy in loads[3 * k : 3 * k + 3]:
            copy.wait()
        store.start()
    for store in stores:
        store.wait()


def edges(place, rows, near, far):
    _, na, c, z = rows.shape
    out = shape((na + 2, c, z))
    return call(
        edges_body, place, 1, (rows, near, far), [ANY, ANY, ANY], [out, out],
        [ANY, ANY], [pltpu.VMEM((2, na + 2, c, z), bf16), pltpu.SemaphoreType.DMA((2, 4))],
        1000000)


class Loader:
    def __init__(self, ext, sems, place, rows, sides, ends=()):
        p, q = place[0], place[1]
        self.ext, self.sems, self.ends = ext, sems, ends
        na = ext.shape[1] - 2
        self.own = {}
        for e in range(1, 5):
            if len(rows) == 1:
                row = rows[0].at[e - 1]
            else:
                row = rows[0].at[e - 2] if e in (2, 3) else rows[1].at[0 if e == 1 else 1]
            self.own[e] = [
                pltpu.make_async_copy(row, ext.at[e, pl.ds(1, na)], sems.at[e, 0]),
                pltpu.make_async_copy(sides[0].at[e - 1], ext.at[e, (na + 1) * (1 - p)],
                                      sems.at[e, 1]),
                pltpu.make_async_copy(sides[1].at[e - 1], ext.at[e, (na + 1) * p],
                                      sems.at[e, 2]),
            ]
        self.q = q

    def end(self, k, e):
        return pltpu.make_async_copy(self.ends[k], self.ext.at[e], self.sems.at[e, 0])

    def start(self):
        if self.ends:
            self.end(0, 5 * (1 - self.q)).start()
            self.end(1, 5 * self.q).start()
        for e in range(1, 5):
            for copy in self.own[e]:
                copy.start()

    def wait(self, *rows):
        for e in rows:
            if e in (0, 5):
                self.end(0, e).wait()
            else:
                for copy in self.own[e]:
                    copy.wait()

    def step(self, g):
        first, second = ((0, 1, 2), (3, 4, 5)) if self.ends else ((1, 2, 3), (4,))

        @pl.when(g == 0)
        def _():
            self.start()
            self.wait(*first)

        pl.when(g == 1)(lambda: self.wait(*second))

    def all_rows(self, g):
        @pl.when(g == 0)
        def _():
            self.start()
            self.wait(0, 1, 2)

        for k in (1, 2, 3):
            pl.when(g == k)(lambda k=k: self.wait(k + 2))


def ext_scratch(na, c, z):
    return [pltpu.VMEM((6, na + 2, c, z), bf16), pltpu.SemaphoreType.DMA((6, 3))]


def window(ext, r, a):
    c, z = ext.shape[2], ext.shape[3]
    return jnp.concatenate(
        [ext[r + i, pl.ds(a, 3)].reshape(3 * c, z) for i in range(3)], axis=0
    )


def taps_sum(parts):
    c = parts.shape[0] // 3
    z = parts.shape[1]
    lane = lax.broadcasted_iota(jnp.int32, (c, z), 1)
    before = jnp.where(lane == 0, 0.0, pltpu.roll(parts[:c], 1, 1))
    after = jnp.where(lane == z - 1, 0.0, pltpu.roll(parts[2 * c :], z - 1, 1))
    return parts[c : 2 * c] + before + after


def forward_column(pre, cot, res, a, na):
    gate = jax.nn.sigmoid(pre)
    put_column(res, a, na, pre * gate)
    d = get_column(cot, a, pre.shape[0], na) * gate * (1.0 + pre * (1.0 - gate))
    return d.astype(bf16)


def shifted(d):
    c, z = d.shape
    lane = lax.broadcasted_iota(jnp.int32, (c, z), 1)
    d = d.astype(f32)
    ahead = jnp.where(lane == z - 1, 0.0, pltpu.roll(d, z - 1, 1))
    behind = jnp.where(lane == 0, 0.0, pltpu.roll(d, 1, 1))
    return jnp.concatenate([ahead, d, behind], axis=0).astype(bf16)


def forward_body(outer, place, x_ref, *refs):
    sides, refs = refs[:2], refs[2:]
    ends = ()
    if outer:
        ends, refs = refs[:2], refs[2:]
    w_ref, b_ref, cot_ref, *refs = refs
    if outer:
        _, near_in, far_in, bsum, acc_in, *refs = refs
        (out_ref, delta_ref, near_ref, far_ref, keep_ref, send_ref,
         ext, sems, cot, res, acc, total, flat, acc_sem) = refs
    else:
        out_ref, delta_ref, near_ref, far_ref, total, acc, ext, sems, cot, res = refs
    g = pl.program_id(0)
    r = 3 * g if outer else 1 + g
    p = place[0]
    _, na, c, z = x_ref.shape
    if outer:
        bring = pltpu.make_async_copy(acc_in, acc, acc_sem)
        pl.when(g == 0)(lambda: bring.start())
    Loader(ext, sems, place, [x_ref], sides, ends).step(g)

    @pl.when(g == 0)
    def _():
        if outer:
            total[...] = bsum[...]
            near_ref[1:3] = near_in[...]
            far_ref[1:3] = far_in[...]
            bring.wait()
        else:
            total[...] = jnp.zeros_like(total)
            acc[...] = jnp.zeros_like(acc)

    put_rows(cot, cot_ref[0, :, 0].astype(f32))
    bias = b_ref[...].astype(f32)

    def pair(k, carry):
        a = 2 * k
        cols = jnp.concatenate([window(ext, r, a), window(ext, r, a + 1)], axis=1)
        both = jnp.dot(w_ref[...], cols, preferred_element_type=f32)
        rows = []
        for s in range(2):
            pre = taps_sum(both[:, s * z : (s + 1) * z]) + bias
            d = forward_column(pre, cot, res, a + s, na)
            delta_ref[0, a + s] = d
            total[...] += d.astype(f32)
            rows.append(shifted(d))
        acc[...] += lax.dot_general(jnp.concatenate(rows, axis=1), cols,
                                    (((1,), (1,)), ((), ())), preferred_element_type=f32)
        return carry

    lax.fori_loop(0, na // 2, pair, 0)
    out_ref[0, :, 0] = get_rows(res, c, na).astype(bf16)
    slot = r if outer else g
    near_ref[slot] = delta_ref[0, (na - 1) * (1 - p)]
    far_ref[slot] = delta_ref[0, (na - 1) * p]
    if not outer:
        return

    def tiles(low, high):
        for s in range(4):
            first = 24 * ((place[2] + s) % 4)
            for b in range(3):
                rows = pl.ds(pl.multiple_of(first + 8 * b, 8), 8)
                for l in range(21):
                    n = b * 21 + l
                    (low if n < 32 else high)[s, n % 32] = (
                        flat[rows, 128 * l : 128 * l + 128] * inverse_scale
                    ).astype(bf16)
            high[s, 31] = jnp.zeros((8, 128), bf16)

    @pl.when(g == 1)
    def _():
        flat[:, 27 * c :] = jnp.zeros((c, flat.shape[1] - 27 * c), f32)
        for ij in range(9):
            for k in range(3):
                t = 3 * ij + k
                flat[:, t * c : (t + 1) * c] = acc[k * c : (k + 1) * c, ij * c : (ij + 1) * c]
        flat[:, 27 * c : 27 * c + 1] = jnp.sum(total[...], axis=1, keepdims=True)
        pl.when(p == 0)(lambda: tiles(keep_ref, send_ref))
        pl.when(p == 1)(lambda: tiles(send_ref, keep_ref))


def forward(place, x, sides, ends, w, b, cot, before=None):
    _, na, c, z = x.shape
    outer = before is not None
    field = pl.BlockSpec(
        (1, c, 1, na, z), lambda g, _: (0, 0, 3 * g if outer else 1 + g, 0, 0))
    args = [x, *sides, *ends, w, b, cot]
    specs = [ANY] * (3 + len(ends)) + [full(w), full(b), field]
    face = shape((4 if outer else 2, c, z))
    bsum, acc = shape((c, z), f32), shape((3 * c, K9), f32)
    half = shape((4, 32, 8, 128))
    rest = [face, face] + ([half, half] if outer else [bsum, acc])
    scratch = ext_scratch(na, c, z) + [pltpu.VMEM((z // 128, c * na, 128), f32)] * 2
    alias = None
    if outer:
        alias = {1 + len(args): 0}
        specs += [ANY] + [full(y) for y in before[1:4]] + [ANY]
        args += before
        scratch += [pltpu.VMEM(acc.shape, f32), pltpu.VMEM(bsum.shape, f32),
                    pltpu.VMEM((c, 21 * 128), f32), pltpu.SemaphoreType.DMA]
    return call(
        lambda *refs: forward_body(outer, *refs), place, 2,
        args, specs, [shape(cot.shape), shape((2, na, c, z))] + rest,
        [field, pl.BlockSpec((1, na, c, z), lambda g, _: (g, 0, 0, 0))]
        + [full(y) for y in rest],
        scratch, 5000000000, alias)


def backward_body(place, d_in, d_out, *refs):
    sides, ends = refs[:2], refs[2:4]
    w_ref, out_ref, ext, sems, res = refs[4:]
    r = pl.program_id(0)
    _, na, c, z = d_in.shape
    Loader(ext, sems, place, [d_in, d_out], sides, ends).all_rows(r)

    def pair(k, carry):
        a = 2 * k
        cols = jnp.concatenate([window(ext, r, a), window(ext, r, a + 1)], axis=1)
        both = jnp.dot(w_ref[...], cols, preferred_element_type=f32)
        for s in range(2):
            put_column(res, a + s, na, taps_sum(both[:, s * z : (s + 1) * z]))
        return carry

    lax.fori_loop(0, na // 2, pair, 0)
    out_ref[0, :, 0] = get_rows(res, c, na).astype(bf16)


def backward(place, d_in, d_out, sides, ends, w):
    _, na, c, z = d_in.shape
    return call(
        backward_body, place, 4, [d_in, d_out, *sides, *ends, w],
        [ANY] * 6 + [full(w)], shape((1, c, 4, na, z)),
        pl.BlockSpec((1, c, 1, na, z), lambda r, _: (0, 0, r, 0, 0)),
        ext_scratch(na, c, z) + [pltpu.VMEM((z // 128, c * na, 128), f32)], 5000000000)


def near_pairs(axis):
    return [(i, i ^ 1) for i in range(lax.axis_size(axis))]


def far_pairs(axis):
    n = lax.axis_size(axis)
    pairs = [(i, i - 1 if i % 2 == 0 else i + 1) for i in range(n)]
    if axis == "azi":
        return [(i, j % n) for i, j in pairs]
    return [(i, j) for i, j in pairs if 0 <= j < n]


def swap(x, axis):
    near, far = x
    got_far = lax.ppermute(far, axis, far_pairs(axis))
    got_near = lax.ppermute(near, axis, near_pairs(axis))
    return got_near, got_far


def sum_over(x, axis, step):
    n = lax.axis_size(axis)
    parts = [x] + [
        lax.ppermute(x, axis, [(i, (i + step * s) % n) for i in range(n)]) for s in (1, 2, 3)
    ]
    a, b, c, d = (y.astype(f32) for y in parts)
    return (a + c) + (b + d)


def reduce_terms(keep, send):
    core = [(i, i ^ 1) for i in range(lax.axis_size("azi"))]
    got = lax.ppermute(send, "azi", core)
    mine = [keep[s].astype(f32) + got[s].astype(f32) for s in range(4)]
    total = mine[0]
    for s in (1, 2, 3):
        y = lax.ppermute(mine[s].astype(bf16), "dp", [(i, (i + s) % 4) for i in range(4)])
        total = total + y.astype(f32)
    n = lax.axis_size("rad")
    for step in (2, 4):
        total = total.astype(bf16)
        y = lax.ppermute(total, "rad", [(i, i ^ step) for i in range(n)])
        total = total.astype(f32) + y.astype(f32)
    total = sum_over(total.astype(bf16), "azi", 2).astype(bf16)
    y = lax.ppermute(total, "rad", [(i, i ^ 1) for i in range(lax.axis_size("rad"))])
    total = total.astype(f32) + y.astype(f32)
    y = lax.ppermute(total, "azi", core)
    low = lax.axis_index("azi") % 2 == 0
    return jnp.concatenate([jnp.where(low, total, y), jnp.where(low, y, total)], axis=0)


def whole_weights(weight, bias):
    rows, width = weight.shape
    packed = jnp.concatenate([weight, jnp.broadcast_to(bias[:, None], (rows, 128))], axis=1)
    pieces = [packed] + [
        lax.ppermute(packed, "dp", [(i, (i + s) % 4) for i in range(4)]) for s in (1, 2, 3)
    ]
    order = (lax.axis_index("dp") - jnp.arange(4)) % 4
    whole = jnp.stack(pieces)[order].reshape(4 * rows, packed.shape[1])
    taps = whole[:, :width].reshape(4 * rows, 3, 3, 3, C)
    w_fwd = taps.transpose(3, 0, 1, 2, 4).reshape(3 * C, K9)
    w_back = taps[:, ::-1, ::-1, ::-1].transpose(3, 4, 1, 2, 0).reshape(3 * C, K9)
    return w_fwd, w_back, whole[:, width : width + 1]


def on_device(inputs, weight, bias, cotangent):
    place = jnp.stack(
        [lax.axis_index("azi") % 2, lax.axis_index("rad") % 2, lax.axis_index("dp")]
    ).astype(jnp.int32)
    x, near_face, far_face = to_columns(place, inputs)
    sides = swap((near_face, far_face), "azi")
    ends = swap(edges(place, x, *sides), "rad")
    w_fwd, w_back, b_col = whole_weights(weight, bias)
    out, d_in, near_in, far_in, bsum, acc = forward(
        place, x, sides, (), w_fwd, b_col, cotangent)
    output, d_out, near_face, far_face, keep, send = forward(
        place, x, sides, ends, w_fwd, b_col, cotangent, [out, near_in, far_in, bsum, acc])
    d_sides = swap((near_face, far_face), "azi")
    d_ends = swap(edges(place, d_out, *d_sides), "rad")
    tiles = reduce_terms(keep, send)
    input_grad = backward(place, d_in, d_out, d_sides, d_ends, w_back)
    summed = tiles[:63].reshape(3, 21, 8, 128).transpose(0, 2, 1, 3).reshape(24, 21 * 128)
    return output, input_grad, summed[:, : 27 * C], summed[:, 27 * C]


def solution(mesh):
    return jax.shard_map(
        on_device,
        mesh=mesh,
        in_specs=(
            P("dp", None, "rad", "azi", None),
            P("dp", None),
            P("dp"),
            P("dp", None, "rad", "azi", None),
        ),
        out_specs=(
            P("dp", None, "rad", "azi", None),
            P("dp", None, "rad", "azi", None),
            P("dp", None),
            P("dp"),
        ),
        check_vma=False,
    )
```

time: 537 us -> 145 us (0.27)
  the two profiles are of different devices: /device:TPU:2 before, /device:TPU:1 now
where the time goes in v2:
time: 145 us; the launch traced here: 144 us
  Pallas kernels  53 us (37%)
  starting transfers between devices  45.6 us (31%)
  waiting for transfers between devices  30.9 us (21%)
  local copies, waits for them, and re-layouts  10.1 us (7%)
  other arithmetic  3.65 us (3%)
    pallas_call x6, Pallas kernels, call(): pl.pallas_call(body, grid_spec=pltpu.PrefetchScalarGridSpec(num_scalar_pr...  53 us
    ppermute x1, waiting for transfers between devices, reduce_terms(): lax.ppermute(total, 'rad', [(i, i ^ 1) for i in range(lax.axis_size('rad'...  17.3 us
    ppermute x3, starting transfers between devices, sum_over(): lax.ppermute(x, axis, [(i, (i + step * s) % n) for i in range(n)])  8.34 us
    ppermute x4, starting transfers between devices, swap(): got_near = lax.ppermute(near, axis, near_pairs(axis))  6.69 us
    ppermute x2, starting transfers between devices, reduce_terms(): y = lax.ppermute(total, 'rad', [(i, i ^ step) for i in range(n)])  6.6 us
    ppermute x3, starting transfers between devices, whole_weights(): lax.ppermute(packed, 'dp', [(i, (i + s) % 4) for i in range(4)])  6.27 us
    ppermute x4, waiting for transfers between devices, swap(): got_far = lax.ppermute(far, axis, far_pairs(axis))  5.93 us
    ppermute x4, starting transfers between devices, swap(): got_far = lax.ppermute(far, axis, far_pairs(axis))  5.42 us
  transfers between devices with their start and end apart: 22, of which 7 were waited for; matrix products, arithmetic and copies ran while one was open for 4% of the time, Pallas kernels for 26%

profile of v2, /device:TPU:1, one launch (start us, length us, event | category | flops | bytes accessed | tf_op | source)
XLA Modules:
  0.0 144.1 jit_solution(12010106840512902697)
XLA Ops:
  0.6 0.7 broadcast_in_dim.2
  1.4 1.0 fusion.8
  2.3 3.6 %collective-permute-start.5 = (bf16[24,2720]{1,0:T(8,128)(2,1)S(1)}, bf16[24,2720]{1,0:T(8,128)(2,1)S(1)}, u32[]{:S(2)}, u32[]{:S(2)}) collective-permute-start(bf16[24,2720]{1,0:T(8,128)(2,1)S(1)} %get-tuple-element.48), channel_id=1, source_target_pairs={{0,128},{64,192},{128,0},{192,64},{1,129},{65,193},{129,1},{193,65... | collective-permute-start | bytes 391688 | tf_op jit(solution)/shard_map/ppermute | solution.py:408
  5.9 0.3 collective-permute-start.4
  6.2 2.4 %collective-permute-start.6 = (bf16[24,2720]{1,0:T(8,128)(2,1)S(1)}, bf16[24,2720]{1,0:T(8,128)(2,1)S(1)}, u32[]{:S(2)}, u32[]{:S(2)}) collective-permute-start(bf16[24,2720]{1,0:T(8,128)(2,1)S(1)} %get-tuple-element.48), channel_id=1, source_target_pairs={{0,192},{64,0},{128,64},{192,128},{1,193},{65,1},{129,65},{193,129... | collective-permute-start | bytes 391688 | tf_op jit(solution)/shard_map/ppermute | solution.py:408
  8.6 0.6 pad_add_fusion.place.refs_0_
  9.2 4.5 %shard_map.75 = (bf16[4,8,96,256]{3,2,1,0:T(8,128)(2,1)}, bf16[4,96,256]{2,1,0:T(8,128)(2,1)}, bf16[4,96,256]{2,1,0:T(8,128)(2,1)}) custom-call(s32[3]{0:T(128)} %pad_add_fusion.place.refs_0_, bf16[1,96,4,8,256]{4,3,2,1,0:T(8,128)(2,1)} %x_ref.1), custom_call_target="tpu_custom_call" | custom-call | flops 10000000 | bytes 4000000 | tf_op jit(solution)/shard_map/pallas_call | solution.py:25
  13.7 1.5 %collective-permute-start = (bf16[4,96,256]{2,1,0:T(8,128)(2,1)}, bf16[4,96,256]{2,1,0:T(8,128)(2,1)S(1)}, u32[]{:S(2)}, u32[]{:S(2)}) collective-permute-start(bf16[4,96,256]{2,1,0:T(8,128)(2,1)} %get-tuple-element.24), channel_id=1, source_target_pairs={{0,1},{1,0},{2,3},{3,2},{4,5},{5,4},{6,7},{7,6},{8,9},{9,8},{10,11... | collective-permute-start | bytes 589832 | tf_op jit(solution)/shard_map/ppermute | solution.py:370
  15.2 2.9 %collective-permute-start.1 = (bf16[4,96,256]{2,1,0:T(8,128)(2,1)}, bf16[4,96,256]{2,1,0:T(8,128)(2,1)S(1)}, u32[]{:S(2)}, u32[]{:S(2)}) collective-permute-start(bf16[4,96,256]{2,1,0:T(8,128)(2,1)} %get-tuple-element.25), channel_id=1, source_target_pairs={{0,7},{1,2},{2,1},{3,4},{4,3},{5,6},{6,5},{7,0},{8,15},{9,10},{10,... | collective-permute-start | bytes 589832 | tf_op jit(solution)/shard_map/ppermute | solution.py:369
  18.2 0.0 collective-permute-done.near.refs_2_
  18.2 0.0 copy-start.1
  18.2 5.9 %collective-permute-done.1.far.refs_3_ = bf16[4,96,256]{2,1,0:T(8,128)(2,1)S(1)} collective-permute-done((bf16[4,96,256]{2,1,0:T(8,128)(2,1)}, bf16[4,96,256]{2,1,0:T(8,128)(2,1)S(1)}, u32[]{:S(2)}, u32[]{:S(2)}) %collective-permute-start.1) | collective-permute-done | bytes 196640 | tf_op jit(solution)/shard_map/ppermute | solution.py:369
  24.1 0.7 copy-done.2
  24.8 2.7 %shard_map.76 = (bf16[10,96,256]{2,1,0:T(8,128)(2,1)}, bf16[10,96,256]{2,1,0:T(8,128)(2,1)}) custom-call(s32[3]{0:T(128)} %pad_add_fusion.place.refs_0_, bf16[4,8,96,256]{3,2,1,0:T(8,128)(2,1)} %get-tuple-element.23.rows.refs_1_, bf16[4,96,256]{2,1,0:T(8,128)(2,1)} %copy-done.1, bf16[4,96,256]{2,1,0:T(8,128)(2,1)} %copy-done.2), custom_call_target="tpu_custom_call" | custom-call | flops 1000000 | bytes 4000000 | tf_op jit(solution)/shard_map/pallas_call | solution.py:25
  27.5 0.4 collective-permute-start.2
  27.9 0.7 collective-permute-start.3
  28.6 0.0 collective-permute-done.6
  28.6 0.1 pad_maximum_fusion
  28.7 0.6 gather_fusion
  29.3 0.7 slice.55.refs_5_.refs_7_
  30.0 0.3 copy.11
  30.3 0.7 copy.12
  31.0 1.3 reshape.93.refs_4_.refs_6_
  32.3 14.1 %shard_map.77 = (bf16[1,96,4,8,256]{4,3,2,1,0:T(8,128)(2,1)}, bf16[2,8,96,256]{3,2,1,0:T(8,128)(2,1)}, bf16[2,96,256]{2,1,0:T(8,128)(2,1)}, bf16[2,96,256]{2,1,0...) custom-call(s32[3]{0:T(128)} %pad_add_fusion.place.refs_0_, ...), custom_call_target="tpu_custom_call" | custom-call | flops 5000000000 | bytes 4000000 | tf_op jit(solution)/shard_map/pallas_call | solution.py:25
  46.4 0.0 collective-permute-done.2.refs_4_
  46.4 0.0 collective-permute-done.3.refs_5_
  46.5 0.8 copy-done.5
  47.2 0.2 copy-done.6
  47.4 15.4 %shard_map.78 = (bf16[1,96,4,8,256]{4,3,2,1,0:T(8,128)(2,1)}, bf16[2,8,96,256]{3,2,1,0:T(8,128)(2,1)}, bf16[4,96,256]{2,1,0:T(8,128)(2,1)}, bf16[4,96,256]{2,1,0...) custom-call(s32[3]{0:T(128)} %pad_add_fusion.place.refs_0_, ...), custom_call_target="tpu_custom_call", output_to_operand_aliasing={{0}: (9, {})} | custom-call | flops 5000000000 | bytes 4000000 | tf_op jit(solution)/shard_map/pallas_call | solution.py:25
  62.8 4.0 %collective-permute-start.11 = (bf16[4,32,8,128]{3,2,1,0:T(8,128)(2,1)}, bf16[4,32,8,128]{3,2,1,0:T(8,128)(2,1)S(1)}, u32[]{:S(2)}, u32[]{:S(2)}) collective-permute-start(bf16[4,32,8,128]{3,2,1,0:T(8,128)(2,1)} %get-tuple-element.41), channel_id=1, source_target_pairs={{0,1},{1,0},{2,3},{3,2},{4,5},{5,4},{6,7},{7,6},{8,9},{9,8},{10,11... | collective-permute-start | bytes 786440 | tf_op jit(solution)/shard_map/ppermute | solution.py:385
  66.8 1.4 collective-permute-done.11
  68.1 1.0 fusion.3
  69.1 0.1 collective-permute-start.12
  69.2 2.7 %collective-permute-start.14 = (bf16[32,8,128]{2,1,0:T(8,128)(2,1)S(1)}, bf16[32,8,128]{2,1,0:T(8,128)(2,1)S(1)}, u32[]{:S(2)}, u32[]{:S(2)}) collective-permute-start(bf16[32,8,128]{2,1,0:T(8,128)(2,1)S(1)} %get-tuple-element.43), channel_id=1, source_target_pairs={{0,192},{64,0},{128,64},{192,128},{1,193},{65,1},{129,65},{193,129... | collective-permute-start | bytes 196616 | tf_op jit(solution)/shard_map/ppermute | solution.py:389
  71.9 0.0 collective-permute-start.13
  71.9 1.6 %collective-permute-done.12 = bf16[32,8,128]{2,1,0:T(8,128)(2,1)S(1)} collective-permute-done((bf16[32,8,128]{2,1,0:T(8,128)(2,1)S(1)}, bf16[32,8,128]{2,1,0:T(8,128)(2,1)S(1)}, u32[]{:S(2)}, u32[]{:S(2)}) %collective-permute-start.12) | collective-permute-done | bytes 65568 | tf_op jit(solution)/shard_map/ppermute | solution.py:389
  73.5 0.4 collective-permute-done.14
  73.9 2.6 %collective-permute-done.13 = bf16[32,8,128]{2,1,0:T(8,128)(2,1)S(1)} collective-permute-done((bf16[32,8,128]{2,1,0:T(8,128)(2,1)S(1)}, bf16[32,8,128]{2,1,0:T(8,128)(2,1)S(1)}, u32[]{:S(2)}, u32[]{:S(2)}) %collective-permute-start.13) | collective-permute-done | bytes 65568 | tf_op jit(solution)/shard_map/ppermute | solution.py:389
  76.5 0.9 fusion.2
  77.4 3.4 %collective-permute-start.15 = (bf16[32,8,128]{2,1,0:T(8,128)(2,1)S(1)}, bf16[32,8,128]{2,1,0:T(8,128)(2,1)S(1)}, u32[]{:S(2)}, u32[]{:S(2)}) collective-permute-start(bf16[32,8,128]{2,1,0:T(8,128)(2,1)S(1)} %fusion.2), channel_id=1, source_target_pairs={{0,16},{8,24},{16,0},{24,8},{32,48},{40,56},{48,32},{56,40},{1,17}... | collective-permute-start | bytes 196616 | tf_op jit(solution)/shard_map/ppermute | solution.py:394
  80.8 1.7 %collective-permute-done.15 = bf16[32,8,128]{2,1,0:T(8,128)(2,1)S(1)} collective-permute-done((bf16[32,8,128]{2,1,0:T(8,128)(2,1)S(1)}, bf16[32,8,128]{2,1,0:T(8,128)(2,1)S(1)}, u32[]{:S(2)}, u32[]{:S(2)}) %collective-permute-start.15) | collective-permute-done | bytes 65568 | tf_op jit(solution)/shard_map/ppermute | solution.py:394
  82.5 3.2 %collective-permute-start.16 = (bf16[32,8,128]{2,1,0:T(8,128)(2,1)S(1)}, bf16[32,8,128]{2,1,0:T(8,128)(2,1)S(1)}, u32[]{:S(2)}, u32[]{:S(2)}) collective-permute-start(bf16[32,8,128]{2,1,0:T(8,128)(2,1)S(1)} %add_convert_fusion.2), channel_id=1, source_target_pairs={{0,32},{8,40},{16,48},{24,56},{32,0},{40,8},{48,16},{56,24},{1,33}... | collective-permute-start | bytes 196616 | tf_op jit(solution)/shard_map/ppermute | solution.py:394
  85.7 3.5 %collective-permute-start.7 = (bf16[4,96,256]{2,1,0:T(8,128)(2,1)}, bf16[4,96,256]{2,1,0:T(8,128)(2,1)S(1)}, u32[]{:S(2)}, u32[]{:S(2)}) collective-permute-start(bf16[4,96,256]{2,1,0:T(8,128)(2,1)} %get-tuple-element.36), channel_id=1, source_target_pairs={{0,1},{1,0},{2,3},{3,2},{4,5},{5,4},{6,7},{7,6},{8,9},{9,8},{10,11... | collective-permute-start | bytes 589832 | tf_op jit(solution)/shard_map/ppermute | solution.py:370
  89.2 1.1 collective-permute-start.8
  90.3 0.0 collective-permute-done.16
  90.3 3.7 %collective-permute-start.19 = (bf16[32,8,128]{2,1,0:T(8,128)(2,1)S(1)}, bf16[32,8,128]{2,1,0:T(8,128)(2,1)S(1)}, u32[]{:S(2)}, u32[]{:S(2)}) collective-permute-start(bf16[32,8,128]{2,1,0:T(8,128)(2,1)S(1)} %add_convert_fusion.1), channel_id=1, source_target_pairs={{0,6},{1,7},{2,0},{3,1},{4,2},{5,3},{6,4},{7,5},{8,14},{9,15},{10,... | collective-permute-start | bytes 196616 | tf_op jit(solution)/shard_map/ppermute | solution.py:377
  94.0 1.4 collective-permute-start.18
  95.5 3.2 %collective-permute-start.17 = (bf16[32,8,128]{2,1,0:T(8,128)(2,1)S(1)}, bf16[32,8,128]{2,1,0:T(8,128)(2,1)S(1)}, u32[]{:S(2)}, u32[]{:S(2)}) collective-permute-start(bf16[32,8,128]{2,1,0:T(8,128)(2,1)S(1)} %add_convert_fusion.1), channel_id=1, source_target_pairs={{0,4},{1,5},{2,6},{3,7},{4,0},{5,1},{6,2},{7,3},{8,12},{9,13},{10,... | collective-permute-start | bytes 196616 | tf_op jit(solution)/shard_map/ppermute | solution.py:377
  98.7 0.0 collective-permute-done.7.near.refs_0_
  98.7 0.7 copy-done.3
  99.3 0.1 copy-done.4
  99.4 2.7 %shard_map.79 = (bf16[10,96,256]{2,1,0:T(8,128)(2,1)}, bf16[10,96,256]{2,1,0:T(8,128)(2,1)}) custom-call(s32[3]{0:T(128)} %pad_add_fusion.place.refs_0_, bf16[2,8,96,256]{3,2,1,0:T(8,128)(2,1)} %get-tuple-element.35.rows.d_out, bf16[4,96,256]{2,1,0:T(8,128)(2,1)} %copy-done.3, bf16[4,96,256]{2,1,0:T(8,128)(2,1)} %copy-done.4), custom_call_target="tpu_custom_call" | custom-call | flops 1000000 | bytes 4000000 | tf_op jit(solution)/shard_map/pallas_call | solution.py:25
  102.1 1.3 collective-permute-start.9
  103.4 0.7 collective-permute-start.10
  104.1 3.0 %collective-permute-start.20 = (bf16[32,8,128]{2,1,0:T(8,128)(2,1)S(1)}, bf16[32,8,128]{2,1,0:T(8,128)(2,1)S(1)}, u32[]{:S(2)}, u32[]{:S(2)}) collective-permute-start(bf16[32,8,128]{2,1,0:T(8,128)(2,1)S(1)} %add_convert_fusion), channel_id=1, source_target_pairs={{0,8},{8,0},{16,24},{24,16},{32,40},{40,32},{48,56},{56,48},{1,9},... | collective-permute-start | bytes 196616 | tf_op jit(solution)/shard_map/ppermute | solution.py:397
  107.2 0.5 copy.13
  107.6 1.3 reshape.94.refs_4_
  108.9 17.3 %collective-permute-done.20 = bf16[32,8,128]{2,1,0:T(8,128)(2,1)S(1)} collective-permute-done((bf16[32,8,128]{2,1,0:T(8,128)(2,1)S(1)}, bf16[32,8,128]{2,1,0:T(8,128)(2,1)S(1)}, u32[]{:S(2)}, u32[]{:S(2)}) %collective-permute-start.20) | collective-permute-done | bytes 65568 | tf_op jit(solution)/shard_map/ppermute | solution.py:397
  126.2 2.5 %collective-permute-start.21 = (f32[32,8,128]{2,1,0:T(8,128)S(1)}, f32[32,8,128]{2,1,0:T(8,128)S(1)}, u32[]{:S(2)}, u32[]{:S(2)}) collective-permute-start(f32[32,8,128]{2,1,0:T(8,128)S(1)} %convert_add_fusion), channel_id=1, source_target_pairs={{0,1},{1,0},{2,3},{3,2},{4,5},{5,4},{6,7},{7,6},{8,9},{9,8},{10,11... | collective-permute-start | bytes 393224 | tf_op jit(solution)/shard_map/ppermute | solution.py:399
  128.8 0.8 copy-done.7
  129.6 0.2 copy-done.8
  129.7 13.6 %shard_map.80 = bf16[1,96,4,8,256]{4,3,2,1,0:T(8,128)(2,1)} custom-call(s32[3]{0:T(128)} %pad_add_fusion.place.refs_0_, bf16[2,8,96,256]{3,2,1,0:T(8,128)(2,1)} %get-tuple-element.34.d_in, bf16[2,8,96,256]{3,2,1,0:T(8,128)(2,1)} %get-tuple-element.35.rows.d_out, bf16[4,96,256]{2,1,0:T(8,128)(2,1)} %copy-done.3, bf16[4,96,256]{2,1,0:T(8,128)(2,1)} %copy-done.4, ...), custom_call_target="tpu_custom_call" | custom-call | flops 5000000000 | bytes 4000000 | tf_op jit(solution)/shard_map/pallas_call | solution.py:25
  143.4 0.0 copy-start
  143.4 0.7 slice_reduce_fusion
  (28 shorter events, 0.3 us)
Async XLA Ops:
  2.3 26.2 %collective-permute-start.5 = (bf16[24,2720]{1,0:T(8,128)(2,1)S(1)}, bf16[24,2720]{1,0:T(8,128)(2,1)S(1)}, u32[]{:S(2)}, u32[]{:S(2)}) collective-permute-start(bf16[24,2720]{1,0:T(8,128)(2,1)S(1)} %get-tuple-element.48), channel_id=1, source_target_pairs={{0,128},{64,192},{128,0},{192,64},{1,129},{65,193},{129,1},{193,65... | collective-permute-start | bytes 391688 | tf_op jit(solution)/shard_map/ppermute | solution.py:408
  5.9 22.7 %collective-permute-start.4 = (bf16[24,2720]{1,0:T(8,128)(2,1)S(1)}, bf16[24,2720]{1,0:T(8,128)(2,1)S(1)}, u32[]{:S(2)}, u32[]{:S(2)}) collective-permute-start(bf16[24,2720]{1,0:T(8,128)(2,1)S(1)} %get-tuple-element.48), channel_id=1, source_target_pairs={{0,64},{64,128},{128,192},{192,0},{1,65},{65,129},{129,193},{193,1... | collective-permute-start | bytes 391688 | tf_op jit(solution)/shard_map/ppermute | solution.py:408
  6.2 22.3 %collective-permute-start.6 = (bf16[24,2720]{1,0:T(8,128)(2,1)S(1)}, bf16[24,2720]{1,0:T(8,128)(2,1)S(1)}, u32[]{:S(2)}, u32[]{:S(2)}) collective-permute-start(bf16[24,2720]{1,0:T(8,128)(2,1)S(1)} %get-tuple-element.48), channel_id=1, source_target_pairs={{0,192},{64,0},{128,64},{192,128},{1,193},{65,1},{129,65},{193,129... | collective-permute-start | bytes 391688 | tf_op jit(solution)/shard_map/ppermute | solution.py:408
  13.7 4.5 %collective-permute-start = (bf16[4,96,256]{2,1,0:T(8,128)(2,1)}, bf16[4,96,256]{2,1,0:T(8,128)(2,1)S(1)}, u32[]{:S(2)}, u32[]{:S(2)}) collective-permute-start(bf16[4,96,256]{2,1,0:T(8,128)(2,1)} %get-tuple-element.24), channel_id=1, source_target_pairs={{0,1},{1,0},{2,3},{3,2},{4,5},{5,4},{6,7},{7,6},{8,9},{9,8},{10,11... | collective-permute-start | bytes 589832 | tf_op jit(solution)/shard_map/ppermute | solution.py:370
  15.2 8.9 %collective-permute-start.1 = (bf16[4,96,256]{2,1,0:T(8,128)(2,1)}, bf16[4,96,256]{2,1,0:T(8,128)(2,1)S(1)}, u32[]{:S(2)}, u32[]{:S(2)}) collective-permute-start(bf16[4,96,256]{2,1,0:T(8,128)(2,1)} %get-tuple-element.25), channel_id=1, source_target_pairs={{0,7},{1,2},{2,1},{3,4},{4,3},{5,6},{6,5},{7,0},{8,15},{9,10},{10,... | collective-permute-start | bytes 589832 | tf_op jit(solution)/shard_map/ppermute | solution.py:369
  18.2 5.9 %copy-start.1 = (bf16[4,96,256]{2,1,0:T(8,128)(2,1)}, bf16[4,96,256]{2,1,0:T(8,128)(2,1)S(1)}, u32[]{:S(2)}) copy-start(bf16[4,96,256]{2,1,0:T(8,128)(2,1)S(1)} %collective-permute-done.near.refs_2_) | copy-start | bytes 589828
  24.1 0.7 copy-start.2
  27.5 18.9 %collective-permute-start.2 = (bf16[10,96,256]{2,1,0:T(8,128)(2,1)}, bf16[10,96,256]{2,1,0:T(8,128)(2,1)S(1)}, u32[]{:S(2)}, u32[]{:S(2)}) collective-permute-start(bf16[10,96,256]{2,1,0:T(8,128)(2,1)} %get-tuple-element.26), channel_id=1, source_target_pairs={{0,8},{8,0},{16,24},{24,16},{32,40},{40,32},{48,56},{56,48},{1,9},... | collective-permute-start | bytes 1474568 | tf_op jit(solution)/shard_map/ppermute | solution.py:370
  27.9 18.6 %collective-permute-start.3 = (bf16[10,96,256]{2,1,0:T(8,128)(2,1)}, bf16[10,96,256]{2,1,0:T(8,128)(2,1)S(1)}, u32[]{:S(2)}, u32[]{:S(2)}) collective-permute-start(bf16[10,96,256]{2,1,0:T(8,128)(2,1)} %get-tuple-element.27), channel_id=1, source_target_pairs={{8,16},{16,8},{24,32},{32,24},{40,48},{48,40},{9,17},{17,9},{25,33... | collective-permute-start | bytes 1474568 | tf_op jit(solution)/shard_map/ppermute | solution.py:369
  46.4 0.8 copy-start.5
  46.5 0.9 copy-start.6
  62.8 5.4 %collective-permute-start.11 = (bf16[4,32,8,128]{3,2,1,0:T(8,128)(2,1)}, bf16[4,32,8,128]{3,2,1,0:T(8,128)(2,1)S(1)}, u32[]{:S(2)}, u32[]{:S(2)}) collective-permute-start(bf16[4,32,8,128]{3,2,1,0:T(8,128)(2,1)} %get-tuple-element.41), channel_id=1, source_target_pairs={{0,1},{1,0},{2,3},{3,2},{4,5},{5,4},{6,7},{7,6},{8,9},{9,8},{10,11... | collective-permute-start | bytes 786440 | tf_op jit(solution)/shard_map/ppermute | solution.py:385
  69.1 4.4 %collective-permute-start.12 = (bf16[32,8,128]{2,1,0:T(8,128)(2,1)S(1)}, bf16[32,8,128]{2,1,0:T(8,128)(2,1)S(1)}, u32[]{:S(2)}, u32[]{:S(2)}) collective-permute-start(bf16[32,8,128]{2,1,0:T(8,128)(2,1)S(1)} %get-tuple-element.42), channel_id=1, source_target_pairs={{0,64},{64,128},{128,192},{192,0},{1,65},{65,129},{129,193},{193,1... | collective-permute-start | bytes 196616 | tf_op jit(solution)/shard_map/ppermute | solution.py:389
  69.2 4.7 %collective-permute-start.14 = (bf16[32,8,128]{2,1,0:T(8,128)(2,1)S(1)}, bf16[32,8,128]{2,1,0:T(8,128)(2,1)S(1)}, u32[]{:S(2)}, u32[]{:S(2)}) collective-permute-start(bf16[32,8,128]{2,1,0:T(8,128)(2,1)S(1)} %get-tuple-element.43), channel_id=1, source_target_pairs={{0,192},{64,0},{128,64},{192,128},{1,193},{65,1},{129,65},{193,129... | collective-permute-start | bytes 196616 | tf_op jit(solution)/shard_map/ppermute | solution.py:389
  71.9 4.6 %collective-permute-start.13 = (bf16[32,8,128]{2,1,0:T(8,128)(2,1)S(1)}, bf16[32,8,128]{2,1,0:T(8,128)(2,1)S(1)}, u32[]{:S(2)}, u32[]{:S(2)}) collective-permute-start(bf16[32,8,128]{2,1,0:T(8,128)(2,1)S(1)} %get-tuple-element.44), channel_id=1, source_target_pairs={{0,128},{64,192},{128,0},{192,64},{1,129},{65,193},{129,1},{193,65... | collective-permute-start | bytes 196616 | tf_op jit(solution)/shard_map/ppermute | solution.py:389
  77.4 5.1 %collective-permute-start.15 = (bf16[32,8,128]{2,1,0:T(8,128)(2,1)S(1)}, bf16[32,8,128]{2,1,0:T(8,128)(2,1)S(1)}, u32[]{:S(2)}, u32[]{:S(2)}) collective-permute-start(bf16[32,8,128]{2,1,0:T(8,128)(2,1)S(1)} %fusion.2), channel_id=1, source_target_pairs={{0,16},{8,24},{16,0},{24,8},{32,48},{40,56},{48,32},{56,40},{1,17}... | collective-permute-start | bytes 196616 | tf_op jit(solution)/shard_map/ppermute | solution.py:394
  82.5 7.8 %collective-permute-start.16 = (bf16[32,8,128]{2,1,0:T(8,128)(2,1)S(1)}, bf16[32,8,128]{2,1,0:T(8,128)(2,1)S(1)}, u32[]{:S(2)}, u32[]{:S(2)}) collective-permute-start(bf16[32,8,128]{2,1,0:T(8,128)(2,1)S(1)} %add_convert_fusion.2), channel_id=1, source_target_pairs={{0,32},{8,40},{16,48},{24,56},{32,0},{40,8},{48,16},{56,24},{1,33}... | collective-permute-start | bytes 196616 | tf_op jit(solution)/shard_map/ppermute | solution.py:394
  85.7 13.0 %collective-permute-start.7 = (bf16[4,96,256]{2,1,0:T(8,128)(2,1)}, bf16[4,96,256]{2,1,0:T(8,128)(2,1)S(1)}, u32[]{:S(2)}, u32[]{:S(2)}) collective-permute-start(bf16[4,96,256]{2,1,0:T(8,128)(2,1)} %get-tuple-element.36), channel_id=1, source_target_pairs={{0,1},{1,0},{2,3},{3,2},{4,5},{5,4},{6,7},{7,6},{8,9},{9,8},{10,11... | collective-permute-start | bytes 589832 | tf_op jit(solution)/shard_map/ppermute | solution.py:370
  89.2 9.5 %collective-permute-start.8 = (bf16[4,96,256]{2,1,0:T(8,128)(2,1)}, bf16[4,96,256]{2,1,0:T(8,128)(2,1)S(1)}, u32[]{:S(2)}, u32[]{:S(2)}) collective-permute-start(bf16[4,96,256]{2,1,0:T(8,128)(2,1)} %get-tuple-element.37), channel_id=1, source_target_pairs={{0,7},{1,2},{2,1},{3,4},{4,3},{5,6},{6,5},{7,0},{8,15},{9,10},{10,... | collective-permute-start | bytes 589832 | tf_op jit(solution)/shard_map/ppermute | solution.py:369
  90.3 13.7 %collective-permute-start.19 = (bf16[32,8,128]{2,1,0:T(8,128)(2,1)S(1)}, bf16[32,8,128]{2,1,0:T(8,128)(2,1)S(1)}, u32[]{:S(2)}, u32[]{:S(2)}) collective-permute-start(bf16[32,8,128]{2,1,0:T(8,128)(2,1)S(1)} %add_convert_fusion.1), channel_id=1, source_target_pairs={{0,6},{1,7},{2,0},{3,1},{4,2},{5,3},{6,4},{7,5},{8,14},{9,15},{10,... | collective-permute-start | bytes 196616 | tf_op jit(solution)/shard_map/ppermute | solution.py:377
  94.0 10.0 %collective-permute-start.18 = (bf16[32,8,128]{2,1,0:T(8,128)(2,1)S(1)}, bf16[32,8,128]{2,1,0:T(8,128)(2,1)S(1)}, u32[]{:S(2)}, u32[]{:S(2)}) collective-permute-start(bf16[32,8,128]{2,1,0:T(8,128)(2,1)S(1)} %add_convert_fusion.1), channel_id=1, source_target_pairs={{0,2},{1,3},{2,4},{3,5},{4,6},{5,7},{6,0},{7,1},{8,10},{9,11},{10,... | collective-permute-start | bytes 196616 | tf_op jit(solution)/shard_map/ppermute | solution.py:377
  95.5 8.6 %collective-permute-start.17 = (bf16[32,8,128]{2,1,0:T(8,128)(2,1)S(1)}, bf16[32,8,128]{2,1,0:T(8,128)(2,1)S(1)}, u32[]{:S(2)}, u32[]{:S(2)}) collective-permute-start(bf16[32,8,128]{2,1,0:T(8,128)(2,1)S(1)} %add_convert_fusion.1), channel_id=1, source_target_pairs={{0,4},{1,5},{2,6},{3,7},{4,0},{5,1},{6,2},{7,3},{8,12},{9,13},{10,... | collective-permute-start | bytes 196616 | tf_op jit(solution)/shard_map/ppermute | solution.py:377
  98.7 0.7 copy-start.3
  98.7 0.7 copy-start.4
  102.1 26.7 %collective-permute-start.9 = (bf16[10,96,256]{2,1,0:T(8,128)(2,1)}, bf16[10,96,256]{2,1,0:T(8,128)(2,1)S(1)}, u32[]{:S(2)}, u32[]{:S(2)}) collective-permute-start(bf16[10,96,256]{2,1,0:T(8,128)(2,1)} %get-tuple-element.38), channel_id=1, source_target_pairs={{0,8},{8,0},{16,24},{24,16},{32,40},{40,32},{48,56},{56,48},{1,9},... | collective-permute-start | bytes 1474568 | tf_op jit(solution)/shard_map/ppermute | solution.py:370
  103.4 25.4 %collective-permute-start.10 = (bf16[10,96,256]{2,1,0:T(8,128)(2,1)}, bf16[10,96,256]{2,1,0:T(8,128)(2,1)S(1)}, u32[]{:S(2)}, u32[]{:S(2)}) collective-permute-start(bf16[10,96,256]{2,1,0:T(8,128)(2,1)} %get-tuple-element.39), channel_id=1, source_target_pairs={{8,16},{16,8},{24,32},{32,24},{40,48},{48,40},{9,17},{17,9},{25,33... | collective-permute-start | bytes 1474568 | tf_op jit(solution)/shard_map/ppermute | solution.py:369
  104.1 22.1 %collective-permute-start.20 = (bf16[32,8,128]{2,1,0:T(8,128)(2,1)S(1)}, bf16[32,8,128]{2,1,0:T(8,128)(2,1)S(1)}, u32[]{:S(2)}, u32[]{:S(2)}) collective-permute-start(bf16[32,8,128]{2,1,0:T(8,128)(2,1)S(1)} %add_convert_fusion), channel_id=1, source_target_pairs={{0,8},{8,0},{16,24},{24,16},{32,40},{40,32},{48,56},{56,48},{1,9},... | collective-permute-start | bytes 196616 | tf_op jit(solution)/shard_map/ppermute | solution.py:397
  126.2 17.1 %collective-permute-start.21 = (f32[32,8,128]{2,1,0:T(8,128)S(1)}, f32[32,8,128]{2,1,0:T(8,128)S(1)}, u32[]{:S(2)}, u32[]{:S(2)}) collective-permute-start(f32[32,8,128]{2,1,0:T(8,128)S(1)} %convert_add_fusion), channel_id=1, source_target_pairs={{0,1},{1,0},{2,3},{3,2},{4,5},{5,4},{6,7},{7,6},{8,9},{9,8},{10,11... | collective-permute-start | bytes 393224 | tf_op jit(solution)/shard_map/ppermute | solution.py:399
  128.8 0.8 copy-start.7
  128.8 1.0 copy-start.8
  143.4 0.7 copy-start

commit v3 on v2

--- a/solution.py
+++ b/solution.py
@@ -120,44 +120,88 @@
         1000000)
 
 
+def sides_body(place, near_face, far_face, near_end, far_end, out_near, out_far, buf, sems):
+    p, q = place[0], place[1]
+    last = near_end.shape[0] - 1
+    loads = []
+    for k, (face, col) in enumerate(((near_face, last * (1 - p)), (far_face, last * p))):
+        for n, (src, dst) in enumerate((
+            (face, buf.at[k, pl.ds(1, 4)]),
+            (near_end.at[col], buf.at[k, 5 * (1 - q)]),
+            (far_end.at[col], buf.at[k, 5 * q]),
+        )):
+            loads.append(pltpu.make_async_copy(src, dst, sems.at[k, n]))
+    stores = [pltpu.make_async_copy(buf.at[k], out, sems.at[k, 3])
+              for k, out in enumerate((out_near, out_far))]
+    for copy in loads:
+        copy.start()
+    for k, store in enumerate(stores):
+        for copy in loads[3 * k : 3 * k + 3]:
+            copy.wait()
+        store.start()
+    for store in stores:
+        store.wait()
+
+
+def six_rows(place, near_face, far_face, ends):
+    _, c, z = ends[0].shape
+    out = shape((6, c, z))
+    return call(
+        sides_body, place, 1, (near_face, far_face, *ends), [ANY] * 4, [out, out],
+        [ANY, ANY], [pltpu.VMEM((2, 6, c, z), bf16), pltpu.SemaphoreType.DMA((2, 4))],
+        1000000)
+
+
 class Loader:
-    def __init__(self, ext, sems, place, rows, sides, ends=()):
+    def __init__(self, ext, sems, place, rows, sides, ends, w, w_buf):
         p, q = place[0], place[1]
+        self.w = pltpu.make_async_copy(w, w_buf, sems.at[0, 3])
         self.ext, self.sems, self.ends = ext, sems, ends
         na = ext.shape[1] - 2
+        six = sides[0].shape[0] == 6
         self.own = {}
-        for e in range(1, 5):
-            if len(rows) == 1:
-                row = rows[0].at[e - 1]
+        for e in range(6):
+            copies = []
+            if e in (0, 5):
+                if not ends:
+                    continue
+            elif len(rows) == 1:
+                copies.append(pltpu.make_async_copy(
+                    rows[0].at[e - 1], ext.at[e, pl.ds(1, na)], sems.at[e, 0]))
             else:
                 row = rows[0].at[e - 2] if e in (2, 3) else rows[1].at[0 if e == 1 else 1]
-            self.own[e] = [
-                pltpu.make_async_copy(row, ext.at[e, pl.ds(1, na)], sems.at[e, 0]),
-                pltpu.make_async_copy(sides[0].at[e - 1], ext.at[e, (na + 1) * (1 - p)],
-                                      sems.at[e, 1]),
-                pltpu.make_async_copy(sides[1].at[e - 1], ext.at[e, (na + 1) * p],
-                                      sems.at[e, 2]),
-            ]
+                copies.append(pltpu.make_async_copy(row, ext.at[e, pl.ds(1, na)], sems.at[e, 0]))
+            if six or e not in (0, 5):
+                for k, col in enumerate(((na + 1) * (1 - p), (na + 1) * p)):
+                    copies.append(pltpu.make_async_copy(
+                        sides[k].at[e if six else e - 1], ext.at[e, col], sems.at[e, 1 + k]))
+            self.own[e] = copies
         self.q = q
 
     def end(self, k, e):
-        return pltpu.make_async_copy(self.ends[k], self.ext.at[e], self.sems.at[e, 0])
+        dst = self.ext.at[e]
+        if self.ends[k].shape[0] < self.ext.shape[1]:
+            dst = self.ext.at[e, pl.ds(1, self.ends[k].shape[0])]
+        return pltpu.make_async_copy(self.ends[k], dst, self.sems.at[e, 0])
 
     def start(self):
+        for e in (1, 2):
+            for copy in self.own[e]:
+                copy.start()
         if self.ends:
             self.end(0, 5 * (1 - self.q)).start()
             self.end(1, 5 * self.q).start()
-        for e in range(1, 5):
-            for copy in self.own[e]:
+        self.w.start()
+        for e in (0, 5, 3, 4):
+            for copy in self.own.get(e, ()):
                 copy.start()
 
     def wait(self, *rows):
         for e in rows:
             if e in (0, 5):
                 self.end(0, e).wait()
-            else:
-                for copy in self.own[e]:
-                    copy.wait()
+            for copy in self.own[e]:
+                copy.wait()
 
     def step(self, g):
         first, second = ((0, 1, 2), (3, 4, 5)) if self.ends else ((1, 2, 3), (4,))
@@ -166,21 +210,24 @@
         def _():
             self.start()
             self.wait(*first)
+            self.w.wait()
 
         pl.when(g == 1)(lambda: self.wait(*second))
 
-    def all_rows(self, g):
-        @pl.when(g == 0)
+    def each(self, r):
+        @pl.when(r == 0)
         def _():
             self.start()
             self.wait(0, 1, 2)
+            self.w.wait()
 
         for k in (1, 2, 3):
-            pl.when(g == k)(lambda k=k: self.wait(k + 2))
+            pl.when(r == k)(lambda k=k: self.wait(k + 2))
 
 
 def ext_scratch(na, c, z):
-    return [pltpu.VMEM((6, na + 2, c, z), bf16), pltpu.SemaphoreType.DMA((6, 3))]
+    return [pltpu.VMEM((6, na + 2, c, z), bf16), pltpu.SemaphoreType.DMA((6, 5)),
+            pltpu.VMEM((3 * c, K9), bf16)]
 
 
 def window(ext, r, a):
@@ -222,47 +269,63 @@
         ends, refs = refs[:2], refs[2:]
     w_ref, b_ref, cot_ref, *refs = refs
     if outer:
-        _, near_in, far_in, bsum, acc_in, *refs = refs
-        (out_ref, delta_ref, near_ref, far_ref, keep_ref, send_ref,
-         ext, sems, cot, res, acc, total, flat, acc_sem) = refs
+        _, near_in, far_in, bsum_in, *refs = refs
+        (out_ref, delta_ref, near_ref, far_ref, total, near_row, far_row,
+         ext, sems, w_buf, cot, res, cot_buf, b_buf) = refs
     else:
-        out_ref, delta_ref, near_ref, far_ref, total, acc, ext, sems, cot, res = refs
+        (out_ref, delta_ref, near_ref, far_ref, total, acc,
+         ext, sems, w_buf, cot, res, cot_buf, b_buf) = refs
     g = pl.program_id(0)
     r = 3 * g if outer else 1 + g
-    p = place[0]
+    p, q = place[0], place[1]
     _, na, c, z = x_ref.shape
+    cots = [
+        pltpu.make_async_copy(cot_ref.at[0, :, 3 * k if outer else 1 + k], cot_buf.at[k],
+                              sems.at[1 + k, 3])
+        for k in range(2)
+    ]
+    small = [pltpu.make_async_copy(b_ref, b_buf, sems.at[3, 3])]
     if outer:
-        bring = pltpu.make_async_copy(acc_in, acc, acc_sem)
-        pl.when(g == 0)(lambda: bring.start())
-    Loader(ext, sems, place, [x_ref], sides, ends).step(g)
+        small += [
+            pltpu.make_async_copy(near_in, near_ref.at[pl.ds(1, 2)], sems.at[4, 3]),
+            pltpu.make_async_copy(far_in, far_ref.at[pl.ds(1, 2)], sems.at[5, 3]),
+            pltpu.make_async_copy(bsum_in, total, sems.at[0, 4]),
+        ]
 
     @pl.when(g == 0)
     def _():
-        if outer:
-            total[...] = bsum[...]
-            near_ref[1:3] = near_in[...]
-            far_ref[1:3] = far_in[...]
-            bring.wait()
-        else:
+        for copy in small + cots:
+            copy.start()
+
+    Loader(ext, sems, place, [x_ref], sides, ends, w_ref, w_buf).step(g)
+
+    @pl.when(g == 0)
+    def _():
+        for copy in small + cots[:1]:
+            copy.wait()
+        if not outer:
             total[...] = jnp.zeros_like(total)
             acc[...] = jnp.zeros_like(acc)
 
-    put_rows(cot, cot_ref[0, :, 0].astype(f32))
-    bias = b_ref[...].astype(f32)
+    pl.when(g == 1)(lambda: cots[1].wait())
+    put_rows(cot, cot_buf[g].astype(f32))
+    bias = b_buf[:, :1].astype(f32)
 
     def pair(k, carry):
         a = 2 * k
         cols = jnp.concatenate([window(ext, r, a), window(ext, r, a + 1)], axis=1)
-        both = jnp.dot(w_ref[...], cols, preferred_element_type=f32)
+        both = jnp.dot(w_buf[...], cols, preferred_element_type=f32)
         rows = []
         for s in range(2):
             pre = taps_sum(both[:, s * z : (s + 1) * z]) + bias
             d = forward_column(pre, cot, res, a + s, na)
             delta_ref[0, a + s] = d
             total[...] += d.astype(f32)
-            rows.append(shifted(d))
-        acc[...] += lax.dot_general(jnp.concatenate(rows, axis=1), cols,
-                                    (((1,), (1,)), ((), ())), preferred_element_type=f32)
+            rows.append(d)
+        if not outer:
+            rows = jnp.concatenate([shifted(d) for d in rows], axis=1)
+            acc[...] += lax.dot_general(rows, cols, (((1,), (1,)), ((), ())),
+                                        preferred_element_type=f32)
         return carry
 
     lax.fori_loop(0, na // 2, pair, 0)
@@ -270,8 +333,73 @@
     slot = r if outer else g
     near_ref[slot] = delta_ref[0, (na - 1) * (1 - p)]
     far_ref[slot] = delta_ref[0, (na - 1) * p]
-    if not outer:
-        return
+    if outer:
+        @pl.when(g != q)
+        def _():
+            near_row[...] = delta_ref[0]
+
+        @pl.when(g == q)
+        def _():
+            far_row[...] = delta_ref[0]
+
+
+def forward(place, x, sides, ends, w, b, cot, before=None):
+    _, na, c, z = x.shape
+    outer = before is not None
+    field = pl.BlockSpec(
+        (1, c, 1, na, z), lambda g, _: (0, 0, 3 * g if outer else 1 + g, 0, 0))
+    args = [x, *sides, *ends, w, b, cot]
+    face, row = shape((4 if outer else 2, c, z)), shape((na, c, z))
+    rest = [face, face, shape((c, z), f32)]
+    rest += [row, row] if outer else [shape((3 * c, K9), f32)]
+    alias = None
+    if outer:
+        alias = {1 + len(args): 0}
+        args += before
+    return call(
+        lambda *refs: forward_body(outer, *refs), place, 2,
+        args, [ANY] * len(args), [shape(cot.shape), shape((2, na, c, z))] + rest,
+        [field, pl.BlockSpec((1, na, c, z), lambda g, _: (g, 0, 0, 0))]
+        + [full(y) for y in rest],
+        ext_scratch(na, c, z) + [pltpu.VMEM((z // 128, c * na, 128), f32)] * 2
+        + [pltpu.VMEM((2, c, na, z), bf16), pltpu.VMEM(b.shape, bf16)],
+        5000000000, alias)
+
+
+def weight_body(place, x_ref, *refs):
+    sides, ends = refs[:2], refs[2:4]
+    (d_in, bsum_in, acc_in, keep_ref, send_ref,
+     ext, sems, acc, flat, d_ref, bsum_ref) = refs[4:]
+    g = pl.program_id(0)
+    r = 3 * g
+    p = place[0]
+    _, na, c, _ = x_ref.shape
+    deltas = [pltpu.make_async_copy(d_in.at[k], d_ref.at[k], sems.at[1 + k, 3])
+              for k in range(2)]
+    sums = pltpu.make_async_copy(bsum_in, bsum_ref, sems.at[3, 3])
+    pl.when(g == 0)(lambda: deltas[0].start())
+    Loader(ext, sems, place, [x_ref], sides, ends, acc_in, acc).step(g)
+
+    @pl.when(g == 0)
+    def _():
+        deltas[1].start()
+        sums.start()
+        deltas[0].wait()
+
+    @pl.when(g == 1)
+    def _():
+        deltas[1].wait()
+        sums.wait()
+
+    def pair(k, carry):
+        a = 2 * k
+        cols = jnp.concatenate([window(ext, r, a), window(ext, r, a + 1)], axis=1)
+        rows = jnp.concatenate([shifted(d_ref[g, a]), shifted(d_ref[g, a + 1])], axis=1)
+        acc[...] += lax.dot_general(rows, cols, (((1,), (1,)), ((), ())),
+                                    preferred_element_type=f32)
+        return carry
+
+    lax.fori_loop(0, na // 2, pair, 0)
 
     def tiles(low, high):
         for s in range(4):
@@ -292,49 +420,36 @@
             for k in range(3):
                 t = 3 * ij + k
                 flat[:, t * c : (t + 1) * c] = acc[k * c : (k + 1) * c, ij * c : (ij + 1) * c]
-        flat[:, 27 * c : 27 * c + 1] = jnp.sum(total[...], axis=1, keepdims=True)
+        flat[:, 27 * c : 27 * c + 1] = jnp.sum(bsum_ref[...], axis=1, keepdims=True)
         pl.when(p == 0)(lambda: tiles(keep_ref, send_ref))
         pl.when(p == 1)(lambda: tiles(send_ref, keep_ref))
 
 
-def forward(place, x, sides, ends, w, b, cot, before=None):
+def weight_terms(place, x, sides, ends, d_out, bsum, acc):
     _, na, c, z = x.shape
-    outer = before is not None
-    field = pl.BlockSpec(
-        (1, c, 1, na, z), lambda g, _: (0, 0, 3 * g if outer else 1 + g, 0, 0))
-    args = [x, *sides, *ends, w, b, cot]
-    specs = [ANY] * (3 + len(ends)) + [full(w), full(b), field]
-    face = shape((4 if outer else 2, c, z))
-    bsum, acc = shape((c, z), f32), shape((3 * c, K9), f32)
     half = shape((4, 32, 8, 128))
-    rest = [face, face] + ([half, half] if outer else [bsum, acc])
-    scratch = ext_scratch(na, c, z) + [pltpu.VMEM((z // 128, c * na, 128), f32)] * 2
-    alias = None
-    if outer:
-        alias = {1 + len(args): 0}
-        specs += [ANY] + [full(y) for y in before[1:4]] + [ANY]
-        args += before
-        scratch += [pltpu.VMEM(acc.shape, f32), pltpu.VMEM(bsum.shape, f32),
-                    pltpu.VMEM((c, 21 * 128), f32), pltpu.SemaphoreType.DMA]
     return call(
-        lambda *refs: forward_body(outer, *refs), place, 2,
-        args, specs, [shape(cot.shape), shape((2, na, c, z))] + rest,
-        [field, pl.BlockSpec((1, na, c, z), lambda g, _: (g, 0, 0, 0))]
-        + [full(y) for y in rest],
-        scratch, 5000000000, alias)
+        weight_body, place, 2, [x, *sides, *ends, d_out, bsum, acc],
+        [ANY] * 8,
+        [half, half], [full(half), full(half)],
+        ext_scratch(na, c, z)[:2] + [pltpu.VMEM((3 * c, K9), f32),
+                                     pltpu.VMEM((c, 21 * 128), f32),
+                                     pltpu.VMEM(d_out.shape, bf16),
+                                     pltpu.VMEM(bsum.shape, f32)],
+        2500000000)
 
 
 def backward_body(place, d_in, d_out, *refs):
     sides, ends = refs[:2], refs[2:4]
-    w_ref, out_ref, ext, sems, res = refs[4:]
+    w_ref, out_ref, ext, sems, w_buf, res = refs[4:]
     r = pl.program_id(0)
     _, na, c, z = d_in.shape
-    Loader(ext, sems, place, [d_in, d_out], sides, ends).all_rows(r)
+    Loader(ext, sems, place, [d_in, d_out], sides, ends, w_ref, w_buf).each(r)
 
     def pair(k, carry):
         a = 2 * k
         cols = jnp.concatenate([window(ext, r, a), window(ext, r, a + 1)], axis=1)
-        both = jnp.dot(w_ref[...], cols, preferred_element_type=f32)
+        both = jnp.dot(w_buf[...], cols, preferred_element_type=f32)
         for s in range(2):
             put_column(res, a + s, na, taps_sum(both[:, s * z : (s + 1) * z]))
         return carry
@@ -345,9 +460,9 @@
 
 def backward(place, d_in, d_out, sides, ends, w):
     _, na, c, z = d_in.shape
+    args = [d_in, d_out, *sides, *ends, w]
     return call(
-        backward_body, place, 4, [d_in, d_out, *sides, *ends, w],
-        [ANY] * 6 + [full(w)], shape((1, c, 4, na, z)),
+        backward_body, place, 4, args, [ANY] * len(args), shape((1, c, 4, na, z)),
         pl.BlockSpec((1, c, 1, na, z), lambda r, _: (0, 0, r, 0, 0)),
         ext_scratch(na, c, z) + [pltpu.VMEM((z // 128, c * na, 128), f32)], 5000000000)
 
@@ -412,7 +527,7 @@
     taps = whole[:, :width].reshape(4 * rows, 3, 3, 3, C)
     w_fwd = taps.transpose(3, 0, 1, 2, 4).reshape(3 * C, K9)
     w_back = taps[:, ::-1, ::-1, ::-1].transpose(3, 4, 1, 2, 0).reshape(3 * C, K9)
-    return w_fwd, w_back, whole[:, width : width + 1]
+    return w_fwd, w_back, whole[:, width : width + 128]
 
 
 def on_device(inputs, weight, bias, cotangent):
@@ -425,10 +540,11 @@
     w_fwd, w_back, b_col = whole_weights(weight, bias)
     out, d_in, near_in, far_in, bsum, acc = forward(
         place, x, sides, (), w_fwd, b_col, cotangent)
-    output, d_out, near_face, far_face, keep, send = forward(
-        place, x, sides, ends, w_fwd, b_col, cotangent, [out, near_in, far_in, bsum, acc])
-    d_sides = swap((near_face, far_face), "azi")
-    d_ends = swap(edges(place, d_out, *d_sides), "rad")
+    output, d_out, near_face, far_face, bsum, d_near, d_far = forward(
+        place, x, sides, ends, w_fwd, b_col, cotangent, [out, near_in, far_in, bsum])
+    d_ends = swap((d_near, d_far), "rad")
+    keep, send = weight_terms(place, x, sides, ends, d_out, bsum, acc)
+    d_sides = swap(six_rows(place, near_face, far_face, d_ends), "azi")
     tiles = reduce_terms(keep, send)
     input_grad = backward(place, d_in, d_out, d_sides, d_ends, w_back)
     summed = tiles[:63].reshape(3, 21, 8, 128).transpose(0, 2, 1, 3).reshape(24, 21 * 128)

time: 145 us -> 138 us (0.952)
  the two profiles are of different devices: /device:TPU:1 before, /device:TPU:8 now
where the time goes in v3:
time: 138 us
  Pallas kernels  54.2 us (39%)
  starting transfers between devices  46.1 us (33%)
  waiting for transfers between devices  23.3 us (17%)
  local copies, waits for them, and re-layouts  9.76 us (7%)
  other arithmetic  3.72 us (3%)
    pallas_call x7, Pallas kernels, call(): pl.pallas_call(body, grid_spec=pltpu.PrefetchScalarGridSpec(num_scalar_pr...  54.2 us
    ppermute x4, starting transfers between devices, swap(): got_far = lax.ppermute(far, axis, far_pairs(axis))  19.3 us
    ppermute x3, starting transfers between devices, sum_over(): lax.ppermute(x, axis, [(i, (i + step * s) % n) for i in range(n)])  9.7 us
    ppermute x4, waiting for transfers between devices, swap(): got_far = lax.ppermute(far, axis, far_pairs(axis))  8.09 us
    ppermute x3, starting transfers between devices, whole_weights(): lax.ppermute(packed, 'dp', [(i, (i + s) % 4) for i in range(4)])  6.29 us
    ppermute x3, waiting for transfers between devices, reduce_terms(): lax.ppermute(mine[s].astype(bf16), 'dp', [(i, (i + s) % 4) for i in range...  5.77 us
    ppermute x1, waiting for transfers between devices, reduce_terms(): lax.ppermute(total, 'rad', [(i, i ^ 1) for i in range(lax.axis_size('rad'...  4.3 us
    ppermute x4, starting transfers between devices, swap(): got_near = lax.ppermute(near, axis, near_pairs(axis))  3.89 us
  transfers between devices with their start and end apart: 22, of which 10 were waited for; matrix products, arithmetic and copies ran while one was open for 4% of the time, Pallas kernels for 26%

profile of v3, /device:TPU:8, one launch (start us, length us, event | category | flops | bytes accessed | tf_op | source)
XLA Modules:
  0.0 138.0 jit_solution(17976120474806042497)
XLA Ops:
  0.6 0.7 broadcast_in_dim.2
  1.4 1.0 fusion.8
  2.3 3.1 %collective-permute-start.5 = (bf16[24,2720]{1,0:T(8,128)(2,1)S(1)}, bf16[24,2720]{1,0:T(8,128)(2,1)S(1)}, u32[]{:S(2)}, u32[]{:S(2)}) collective-permute-start(bf16[24,2720]{1,0:T(8,128)(2,1)S(1)} %get-tuple-element.54), channel_id=1, source_target_pairs={{0,128},{64,192},{128,0},{192,64},{1,129},{65,193},{129,1},{193,65... | collective-permute-start | bytes 391688 | tf_op jit(solution)/shard_map/ppermute | solution.py:523
  5.4 0.6 collective-permute-start.4
  6.0 2.6 %collective-permute-start.6 = (bf16[24,2720]{1,0:T(8,128)(2,1)S(1)}, bf16[24,2720]{1,0:T(8,128)(2,1)S(1)}, u32[]{:S(2)}, u32[]{:S(2)}) collective-permute-start(bf16[24,2720]{1,0:T(8,128)(2,1)S(1)} %get-tuple-element.54), channel_id=1, source_target_pairs={{0,192},{64,0},{128,64},{192,128},{1,193},{65,1},{129,65},{193,129... | collective-permute-start | bytes 391688 | tf_op jit(solution)/shard_map/ppermute | solution.py:523
  8.6 0.6 pad_add_fusion.place.refs_0_
  9.3 4.5 %shard_map.75 = (bf16[4,8,96,256]{3,2,1,0:T(8,128)(2,1)}, bf16[4,96,256]{2,1,0:T(8,128)(2,1)}, bf16[4,96,256]{2,1,0:T(8,128)(2,1)}) custom-call(s32[3]{0:T(128)} %pad_add_fusion.place.refs_0_, bf16[1,96,4,8,256]{4,3,2,1,0:T(8,128)(2,1)} %x_ref.1), custom_call_target="tpu_custom_call" | custom-call | flops 10000000 | bytes 4000000 | tf_op jit(solution)/shard_map/pallas_call | solution.py:25
  13.8 0.0 collective-permute-start
  13.8 6.4 %collective-permute-start.1 = (bf16[4,96,256]{2,1,0:T(8,128)(2,1)}, bf16[4,96,256]{2,1,0:T(8,128)(2,1)S(1)}, u32[]{:S(2)}, u32[]{:S(2)}) collective-permute-start(bf16[4,96,256]{2,1,0:T(8,128)(2,1)} %get-tuple-element.28), channel_id=1, source_target_pairs={{0,7},{1,2},{2,1},{3,4},{4,3},{5,6},{6,5},{7,0},{8,15},{9,10},{10,... | collective-permute-start | bytes 589832 | tf_op jit(solution)/shard_map/ppermute | solution.py:484
  20.2 0.0 collective-permute-done.near.refs_2_.refs_0_
  20.2 0.0 copy-start.3
  20.3 5.6 %collective-permute-done.1.far.refs_3_.refs_1_ = bf16[4,96,256]{2,1,0:T(8,128)(2,1)S(1)} collective-permute-done((bf16[4,96,256]{2,1,0:T(8,128)(2,1)}, bf16[4,96,256]{2,1,0:T(8,128)(2,1)S(1)}, u32[]{:S(2)}, u32[]{:S(2)}) %collective-permute-start.1) | collective-permute-done | bytes 196640 | tf_op jit(solution)/shard_map/ppermute | solution.py:484
  25.8 0.7 copy-done.4
  26.5 2.7 %shard_map.76 = (bf16[10,96,256]{2,1,0:T(8,128)(2,1)}, bf16[10,96,256]{2,1,0:T(8,128)(2,1)}) custom-call(s32[3]{0:T(128)} %pad_add_fusion.place.refs_0_, bf16[4,8,96,256]{3,2,1,0:T(8,128)(2,1)} %get-tuple-element.26.rows.refs_1_.x_ref, bf16[4,96,256]{2,1,0:T(8,128)(2,1)} %copy-done.3, bf16[4,96,256]{2,1,0:T(8,128)(2,1)} %copy-done.4), custom_call_target="tpu_custom_call" | custom-call | flops 1000000 | bytes 4000000 | tf_op jit(solution)/shard_map/pallas_call | solution.py:25
  29.2 1.2 collective-permute-start.2
  30.4 2.7 %collective-permute-start.3 = (bf16[10,96,256]{2,1,0:T(8,128)(2,1)}, bf16[10,96,256]{2,1,0:T(8,128)(2,1)S(1)}, u32[]{:S(2)}, u32[]{:S(2)}) collective-permute-start(bf16[10,96,256]{2,1,0:T(8,128)(2,1)} %get-tuple-element.30), channel_id=1, source_target_pairs={{8,16},{16,8},{24,32},{32,24},{40,48},{48,40},{9,17},{17,9},{25,33... | collective-permute-start | bytes 1474568 | tf_op jit(solution)/shard_map/ppermute | solution.py:484
  33.1 0.0 collective-permute-done.5
  33.2 0.1 pad_maximum_fusion
  33.2 0.6 gather_fusion
  33.8 0.7 slice.55.refs_5_.refs_7_
  34.5 0.3 copy.11
  34.9 0.7 copy.12
  35.5 1.3 reshape.93.refs_4_.refs_6_
  36.8 13.4 %shard_map.77 = (bf16[1,96,4,8,256]{4,3,2,1,0:T(8,128)(2,1)}, bf16[2,8,96,256]{3,2,1,0:T(8,128)(2,1)}, bf16[2,96,256]{2,1,0:T(8,128)(2,1)}, bf16[2,96,256]{2,1,0...) custom-call(s32[3]{0:T(128)} %pad_add_fusion.place.refs_0_, ...), custom_call_target="tpu_custom_call" | custom-call | flops 5000000000 | bytes 4000000 | tf_op jit(solution)/shard_map/pallas_call | solution.py:25
  50.3 0.0 collective-permute-done.2.refs_4_.refs_2_
  50.3 0.2 collective-permute-done.3.refs_5_.refs_3_
  50.4 0.6 copy-done.5
  51.1 0.2 copy-done.6
  51.2 9.7 %shard_map.78 = (bf16[1,96,4,8,256]{4,3,2,1,0:T(8,128)(2,1)}, bf16[2,8,96,256]{3,2,1,0:T(8,128)(2,1)}, bf16[4,96,256]{2,1,0:T(8,128)(2,1)}, bf16[4,96,256]{2,1,0...) custom-call(s32[3]{0:T(128)} %pad_add_fusion.place.refs_0_, ...), custom_call_target="tpu_custom_call", output_to_operand_aliasing={{0}: (9, {})} | custom-call | flops 5000000000 | bytes 4000000 | tf_op jit(solution)/shard_map/pallas_call | solution.py:25
  61.0 8.6 %shard_map.81 = (bf16[4,32,8,128]{3,2,1,0:T(8,128)(2,1)}, bf16[4,32,8,128]{3,2,1,0:T(8,128)(2,1)}) custom-call(s32[3]{0:T(128)} %pad_add_fusion.place.refs_0_, bf16[4,8,96,256]{3,2,1,0:T(8,128)(2,1)} %get-tuple-element.26.rows.refs_1_.x_ref, bf16[4,96,256]{2,1,0:T(8,128)(2,1)} %copy-done.3, bf16[4,96,256]{2,1,0:T(8,128)(2,1)} %copy-done.4, ...), custom_call_target="tpu_custom_call" | custom-call | flops 2500000000 | bytes 4000000 | tf_op jit(solution)/shard_map/pallas_call | solution.py:25
  69.6 0.1 collective-permute-start.11
  69.7 1.7 %collective-permute-done.11 = bf16[4,32,8,128]{3,2,1,0:T(8,128)(2,1)S(1)} collective-permute-done((bf16[4,32,8,128]{3,2,1,0:T(8,128)(2,1)}, bf16[4,32,8,128]{3,2,1,0:T(8,128)(2,1)S(1)}, u32[]{:S(2)}, u32[]{:S(2)}) %collective-permute-start.11) | collective-permute-done | bytes 262176 | tf_op jit(solution)/shard_map/ppermute | solution.py:500
  71.4 1.0 fusion.3
  72.4 0.1 collective-permute-start.12
  72.5 3.2 %collective-permute-start.14 = (bf16[32,8,128]{2,1,0:T(8,128)(2,1)S(1)}, bf16[32,8,128]{2,1,0:T(8,128)(2,1)S(1)}, u32[]{:S(2)}, u32[]{:S(2)}) collective-permute-start(bf16[32,8,128]{2,1,0:T(8,128)(2,1)S(1)} %get-tuple-element.49), channel_id=1, source_target_pairs={{0,192},{64,0},{128,64},{192,128},{1,193},{65,1},{129,65},{193,129... | collective-permute-start | bytes 196616 | tf_op jit(solution)/shard_map/ppermute | solution.py:504
  75.7 0.0 collective-permute-start.13
  75.7 2.2 %collective-permute-done.12 = bf16[32,8,128]{2,1,0:T(8,128)(2,1)S(1)} collective-permute-done((bf16[32,8,128]{2,1,0:T(8,128)(2,1)S(1)}, bf16[32,8,128]{2,1,0:T(8,128)(2,1)S(1)}, u32[]{:S(2)}, u32[]{:S(2)}) %collective-permute-start.12) | collective-permute-done | bytes 65568 | tf_op jit(solution)/shard_map/ppermute | solution.py:504
  77.9 0.6 collective-permute-done.14
  78.5 3.0 %collective-permute-done.13 = bf16[32,8,128]{2,1,0:T(8,128)(2,1)S(1)} collective-permute-done((bf16[32,8,128]{2,1,0:T(8,128)(2,1)S(1)}, bf16[32,8,128]{2,1,0:T(8,128)(2,1)S(1)}, u32[]{:S(2)}, u32[]{:S(2)}) %collective-permute-start.13) | collective-permute-done | bytes 65568 | tf_op jit(solution)/shard_map/ppermute | solution.py:504
  81.5 0.9 fusion.2
  82.4 0.1 collective-permute-start.15
  82.5 2.6 %collective-permute-start.7 = (bf16[8,96,256]{2,1,0:T(8,128)(2,1)S(1)}, bf16[8,96,256]{2,1,0:T(8,128)(2,1)S(1)}, u32[]{:S(2)}, u32[]{:S(2)}) collective-permute-start(bf16[8,96,256]{2,1,0:T(8,128)(2,1)S(1)} %copy-done.8), channel_id=1, source_target_pairs={{0,8},{8,0},{16,24},{24,16},{32,40},{40,32},{48,56},{56,48},{1,9},... | collective-permute-start | bytes 1179656 | tf_op jit(solution)/shard_map/ppermute | solution.py:485
  85.1 3.1 %collective-permute-start.8 = (bf16[8,96,256]{2,1,0:T(8,128)(2,1)S(1)}, bf16[8,96,256]{2,1,0:T(8,128)(2,1)S(1)}, u32[]{:S(2)}, u32[]{:S(2)}) collective-permute-start(bf16[8,96,256]{2,1,0:T(8,128)(2,1)S(1)} %copy-done.7), channel_id=1, source_target_pairs={{8,16},{16,8},{24,32},{32,24},{40,48},{48,40},{9,17},{17,9},{25,33... | collective-permute-start | bytes 1179656 | tf_op jit(solution)/shard_map/ppermute | solution.py:484
  88.2 0.0 collective-permute-done.15
  88.3 2.5 %collective-permute-start.16 = (bf16[32,8,128]{2,1,0:T(8,128)(2,1)S(1)}, bf16[32,8,128]{2,1,0:T(8,128)(2,1)S(1)}, u32[]{:S(2)}, u32[]{:S(2)}) collective-permute-start(bf16[32,8,128]{2,1,0:T(8,128)(2,1)S(1)} %add_convert_fusion.2), channel_id=1, source_target_pairs={{0,32},{8,40},{16,48},{24,56},{32,0},{40,8},{48,16},{56,24},{1,33}... | collective-permute-start | bytes 196616 | tf_op jit(solution)/shard_map/ppermute | solution.py:509
  90.8 3.4 %collective-permute-done.16 = bf16[32,8,128]{2,1,0:T(8,128)(2,1)S(1)} collective-permute-done((bf16[32,8,128]{2,1,0:T(8,128)(2,1)S(1)}, bf16[32,8,128]{2,1,0:T(8,128)(2,1)S(1)}, u32[]{:S(2)}, u32[]{:S(2)}) %collective-permute-start.16) | collective-permute-done | bytes 65568 | tf_op jit(solution)/shard_map/ppermute | solution.py:509
  94.1 5.7 %collective-permute-start.19 = (bf16[32,8,128]{2,1,0:T(8,128)(2,1)S(1)}, bf16[32,8,128]{2,1,0:T(8,128)(2,1)S(1)}, u32[]{:S(2)}, u32[]{:S(2)}) collective-permute-start(bf16[32,8,128]{2,1,0:T(8,128)(2,1)S(1)} %add_convert_fusion.1), channel_id=1, source_target_pairs={{0,6},{1,7},{2,0},{3,1},{4,2},{5,3},{6,4},{7,5},{8,14},{9,15},{10,... | collective-permute-start | bytes 196616 | tf_op jit(solution)/shard_map/ppermute | solution.py:492
  99.8 4.0 %collective-permute-start.17 = (bf16[32,8,128]{2,1,0:T(8,128)(2,1)S(1)}, bf16[32,8,128]{2,1,0:T(8,128)(2,1)S(1)}, u32[]{:S(2)}, u32[]{:S(2)}) collective-permute-start(bf16[32,8,128]{2,1,0:T(8,128)(2,1)S(1)} %add_convert_fusion.1), channel_id=1, source_target_pairs={{0,4},{1,5},{2,6},{3,7},{4,0},{5,1},{6,2},{7,3},{8,12},{9,13},{10,... | collective-permute-start | bytes 196616 | tf_op jit(solution)/shard_map/ppermute | solution.py:492
  103.9 0.9 collective-permute-done.8.far_end.refs_3_
  104.8 0.7 copy-done.1
  105.5 2.5 %shard_map.79 = (bf16[6,96,256]{2,1,0:T(8,128)(2,1)}, bf16[6,96,256]{2,1,0:T(8,128)(2,1)}) custom-call(s32[3]{0:T(128)} %pad_add_fusion.place.refs_0_, bf16[4,96,256]{2,1,0:T(8,128)(2,1)} %get-tuple-element.38.near_face, bf16[4,96,256]{2,1,0:T(8,128)(2,1)} %get-tuple-element.39.far_face, bf16[8,96,256]{2,1,0:T(8,128)(2,1)} %copy-done, ...), custom_call_target="tpu_custom_call" | custom-call | flops 1000000 | bytes 4000000 | tf_op jit(solution)/shard_map/pallas_call | solution.py:25
  108.0 0.1 collective-permute-start.9
  108.1 7.1 %collective-permute-start.10 = (bf16[6,96,256]{2,1,0:T(8,128)(2,1)}, bf16[6,96,256]{2,1,0:T(8,128)(2,1)S(1)}, u32[]{:S(2)}, u32[]{:S(2)}) collective-permute-start(bf16[6,96,256]{2,1,0:T(8,128)(2,1)} %get-tuple-element.43), channel_id=1, source_target_pairs={{0,7},{1,2},{2,1},{3,4},{4,3},{5,6},{6,5},{7,0},{8,15},{9,10},{10,... | collective-permute-start | bytes 884744 | tf_op jit(solution)/shard_map/ppermute | solution.py:484
  115.2 0.0 collective-permute-done.19
  115.3 0.8 collective-permute-start.20
  116.1 0.5 copy.13
  116.6 1.3 reshape.94.refs_4_
  117.9 4.3 %collective-permute-done.20 = bf16[32,8,128]{2,1,0:T(8,128)(2,1)S(1)} collective-permute-done((bf16[32,8,128]{2,1,0:T(8,128)(2,1)S(1)}, bf16[32,8,128]{2,1,0:T(8,128)(2,1)S(1)}, u32[]{:S(2)}, u32[]{:S(2)}) %collective-permute-start.20) | collective-permute-done | bytes 65568 | tf_op jit(solution)/shard_map/ppermute | solution.py:512
  122.2 0.1 collective-permute-start.21
  122.3 1.4 %collective-permute-done.10.refs_1_ = bf16[6,96,256]{2,1,0:T(8,128)(2,1)S(1)} collective-permute-done((bf16[6,96,256]{2,1,0:T(8,128)(2,1)}, bf16[6,96,256]{2,1,0:T(8,128)(2,1)S(1)}, u32[]{:S(2)}, u32[]{:S(2)}) %collective-permute-start.10) | collective-permute-done | bytes 294944 | tf_op jit(solution)/shard_map/ppermute | solution.py:484
  123.8 0.7 copy-done.10
  124.5 12.8 %shard_map.80 = bf16[1,96,4,8,256]{4,3,2,1,0:T(8,128)(2,1)} custom-call(s32[3]{0:T(128)} %pad_add_fusion.place.refs_0_, bf16[2,8,96,256]{3,2,1,0:T(8,128)(2,1)} %get-tuple-element.36.d_in, bf16[2,8,96,256]{3,2,1,0:T(8,128)(2,1)} %get-tuple-element.37.d_out.refs_4_, bf16[6,96,256]{2,1,0:T(8,128)(2,1)} %copy-done.9, bf16[6,96,256]{2,1,0:T(8,128)(2,1)} %copy-done.10, ...), custom_call_target="tpu_custom_call" | custom-call | flops 5000000000 | bytes 4000000 | tf_op jit(solution)/shard_map/pallas_call | solution.py:25
  137.3 0.0 copy-start.2
  137.3 0.7 slice_reduce_fusion
  (33 shorter events, 0.3 us)
Async XLA Ops:
  2.3 30.8 %collective-permute-start.5 = (bf16[24,2720]{1,0:T(8,128)(2,1)S(1)}, bf16[24,2720]{1,0:T(8,128)(2,1)S(1)}, u32[]{:S(2)}, u32[]{:S(2)}) collective-permute-start(bf16[24,2720]{1,0:T(8,128)(2,1)S(1)} %get-tuple-element.54), channel_id=1, source_target_pairs={{0,128},{64,192},{128,0},{192,64},{1,129},{65,193},{129,1},{193,65... | collective-permute-start | bytes 391688 | tf_op jit(solution)/shard_map/ppermute | solution.py:523
  5.4 27.7 %collective-permute-start.4 = (bf16[24,2720]{1,0:T(8,128)(2,1)S(1)}, bf16[24,2720]{1,0:T(8,128)(2,1)S(1)}, u32[]{:S(2)}, u32[]{:S(2)}) collective-permute-start(bf16[24,2720]{1,0:T(8,128)(2,1)S(1)} %get-tuple-element.54), channel_id=1, source_target_pairs={{0,64},{64,128},{128,192},{192,0},{1,65},{65,129},{129,193},{193,1... | collective-permute-start | bytes 391688 | tf_op jit(solution)/shard_map/ppermute | solution.py:523
  6.0 27.2 %collective-permute-start.6 = (bf16[24,2720]{1,0:T(8,128)(2,1)S(1)}, bf16[24,2720]{1,0:T(8,128)(2,1)S(1)}, u32[]{:S(2)}, u32[]{:S(2)}) collective-permute-start(bf16[24,2720]{1,0:T(8,128)(2,1)S(1)} %get-tuple-element.54), channel_id=1, source_target_pairs={{0,192},{64,0},{128,64},{192,128},{1,193},{65,1},{129,65},{193,129... | collective-permute-start | bytes 391688 | tf_op jit(solution)/shard_map/ppermute | solution.py:523
  13.8 6.4 %collective-permute-start = (bf16[4,96,256]{2,1,0:T(8,128)(2,1)}, bf16[4,96,256]{2,1,0:T(8,128)(2,1)S(1)}, u32[]{:S(2)}, u32[]{:S(2)}) collective-permute-start(bf16[4,96,256]{2,1,0:T(8,128)(2,1)} %get-tuple-element.27), channel_id=1, source_target_pairs={{0,1},{1,0},{2,3},{3,2},{4,5},{5,4},{6,7},{7,6},{8,9},{9,8},{10,11... | collective-permute-start | bytes 589832 | tf_op jit(solution)/shard_map/ppermute | solution.py:485
  13.8 12.0 %collective-permute-start.1 = (bf16[4,96,256]{2,1,0:T(8,128)(2,1)}, bf16[4,96,256]{2,1,0:T(8,128)(2,1)S(1)}, u32[]{:S(2)}, u32[]{:S(2)}) collective-permute-start(bf16[4,96,256]{2,1,0:T(8,128)(2,1)} %get-tuple-element.28), channel_id=1, source_target_pairs={{0,7},{1,2},{2,1},{3,4},{4,3},{5,6},{6,5},{7,0},{8,15},{9,10},{10,... | collective-permute-start | bytes 589832 | tf_op jit(solution)/shard_map/ppermute | solution.py:484
  20.2 5.6 %copy-start.3 = (bf16[4,96,256]{2,1,0:T(8,128)(2,1)}, bf16[4,96,256]{2,1,0:T(8,128)(2,1)S(1)}, u32[]{:S(2)}) copy-start(bf16[4,96,256]{2,1,0:T(8,128)(2,1)S(1)} %collective-permute-done.near.refs_2_.refs_0_) | copy-start | bytes 589828
  25.8 0.7 copy-start.4
  29.2 21.1 %collective-permute-start.2 = (bf16[10,96,256]{2,1,0:T(8,128)(2,1)}, bf16[10,96,256]{2,1,0:T(8,128)(2,1)S(1)}, u32[]{:S(2)}, u32[]{:S(2)}) collective-permute-start(bf16[10,96,256]{2,1,0:T(8,128)(2,1)} %get-tuple-element.29), channel_id=1, source_target_pairs={{0,8},{8,0},{16,24},{24,16},{32,40},{40,32},{48,56},{56,48},{1,9},... | collective-permute-start | bytes 1474568 | tf_op jit(solution)/shard_map/ppermute | solution.py:485
  30.4 20.1 %collective-permute-start.3 = (bf16[10,96,256]{2,1,0:T(8,128)(2,1)}, bf16[10,96,256]{2,1,0:T(8,128)(2,1)S(1)}, u32[]{:S(2)}, u32[]{:S(2)}) collective-permute-start(bf16[10,96,256]{2,1,0:T(8,128)(2,1)} %get-tuple-element.30), channel_id=1, source_target_pairs={{8,16},{16,8},{24,32},{32,24},{40,48},{48,40},{9,17},{17,9},{25,33... | collective-permute-start | bytes 1474568 | tf_op jit(solution)/shard_map/ppermute | solution.py:484
  50.3 0.8 copy-start.5
  50.4 0.8 copy-start.6
  61.0 21.5 %copy-start.8 = (bf16[8,96,256]{2,1,0:T(8,128)(2,1)S(1)}, bf16[8,96,256]{2,1,0:T(8,128)(2,1)}, u32[]{:S(2)}) copy-start(bf16[8,96,256]{2,1,0:T(8,128)(2,1)} %get-tuple-element.40) | copy-start | bytes 1179652
  61.0 24.1 %copy-start.7 = (bf16[8,96,256]{2,1,0:T(8,128)(2,1)S(1)}, bf16[8,96,256]{2,1,0:T(8,128)(2,1)}, u32[]{:S(2)}) copy-start(bf16[8,96,256]{2,1,0:T(8,128)(2,1)} %get-tuple-element.41) | copy-start | bytes 1179652
  69.6 1.8 %collective-permute-start.11 = (bf16[4,32,8,128]{3,2,1,0:T(8,128)(2,1)}, bf16[4,32,8,128]{3,2,1,0:T(8,128)(2,1)S(1)}, u32[]{:S(2)}, u32[]{:S(2)}) collective-permute-start(bf16[4,32,8,128]{3,2,1,0:T(8,128)(2,1)} %get-tuple-element.47), channel_id=1, source_target_pairs={{0,1},{1,0},{2,3},{3,2},{4,5},{5,4},{6,7},{7,6},{8,9},{9,8},{10,11... | collective-permute-start | bytes 786440 | tf_op jit(solution)/shard_map/ppermute | solution.py:500
  72.4 5.6 %collective-permute-start.12 = (bf16[32,8,128]{2,1,0:T(8,128)(2,1)S(1)}, bf16[32,8,128]{2,1,0:T(8,128)(2,1)S(1)}, u32[]{:S(2)}, u32[]{:S(2)}) collective-permute-start(bf16[32,8,128]{2,1,0:T(8,128)(2,1)S(1)} %get-tuple-element.48), channel_id=1, source_target_pairs={{0,64},{64,128},{128,192},{192,0},{1,65},{65,129},{129,193},{193,1... | collective-permute-start | bytes 196616 | tf_op jit(solution)/shard_map/ppermute | solution.py:504
  72.5 6.0 %collective-permute-start.14 = (bf16[32,8,128]{2,1,0:T(8,128)(2,1)S(1)}, bf16[32,8,128]{2,1,0:T(8,128)(2,1)S(1)}, u32[]{:S(2)}, u32[]{:S(2)}) collective-permute-start(bf16[32,8,128]{2,1,0:T(8,128)(2,1)S(1)} %get-tuple-element.49), channel_id=1, source_target_pairs={{0,192},{64,0},{128,64},{192,128},{1,193},{65,1},{129,65},{193,129... | collective-permute-start | bytes 196616 | tf_op jit(solution)/shard_map/ppermute | solution.py:504
  75.7 5.8 %collective-permute-start.13 = (bf16[32,8,128]{2,1,0:T(8,128)(2,1)S(1)}, bf16[32,8,128]{2,1,0:T(8,128)(2,1)S(1)}, u32[]{:S(2)}, u32[]{:S(2)}) collective-permute-start(bf16[32,8,128]{2,1,0:T(8,128)(2,1)S(1)} %get-tuple-element.50), channel_id=1, source_target_pairs={{0,128},{64,192},{128,0},{192,64},{1,129},{65,193},{129,1},{193,65... | collective-permute-start | bytes 196616 | tf_op jit(solution)/shard_map/ppermute | solution.py:504
  82.4 5.9 %collective-permute-start.15 = (bf16[32,8,128]{2,1,0:T(8,128)(2,1)S(1)}, bf16[32,8,128]{2,1,0:T(8,128)(2,1)S(1)}, u32[]{:S(2)}, u32[]{:S(2)}) collective-permute-start(bf16[32,8,128]{2,1,0:T(8,128)(2,1)S(1)} %fusion.2), channel_id=1, source_target_pairs={{0,16},{8,24},{16,0},{24,8},{32,48},{40,56},{48,32},{56,40},{1,17}... | collective-permute-start | bytes 196616 | tf_op jit(solution)/shard_map/ppermute | solution.py:509
  82.5 21.4 %collective-permute-start.7 = (bf16[8,96,256]{2,1,0:T(8,128)(2,1)S(1)}, bf16[8,96,256]{2,1,0:T(8,128)(2,1)S(1)}, u32[]{:S(2)}, u32[]{:S(2)}) collective-permute-start(bf16[8,96,256]{2,1,0:T(8,128)(2,1)S(1)} %copy-done.8), channel_id=1, source_target_pairs={{0,8},{8,0},{16,24},{24,16},{32,40},{40,32},{48,56},{56,48},{1,9},... | collective-permute-start | bytes 1179656 | tf_op jit(solution)/shard_map/ppermute | solution.py:485
  85.1 19.7 %collective-permute-start.8 = (bf16[8,96,256]{2,1,0:T(8,128)(2,1)S(1)}, bf16[8,96,256]{2,1,0:T(8,128)(2,1)S(1)}, u32[]{:S(2)}, u32[]{:S(2)}) collective-permute-start(bf16[8,96,256]{2,1,0:T(8,128)(2,1)S(1)} %copy-done.7), channel_id=1, source_target_pairs={{8,16},{16,8},{24,32},{32,24},{40,48},{48,40},{9,17},{17,9},{25,33... | collective-permute-start | bytes 1179656 | tf_op jit(solution)/shard_map/ppermute | solution.py:484
  88.3 5.9 %collective-permute-start.16 = (bf16[32,8,128]{2,1,0:T(8,128)(2,1)S(1)}, bf16[32,8,128]{2,1,0:T(8,128)(2,1)S(1)}, u32[]{:S(2)}, u32[]{:S(2)}) collective-permute-start(bf16[32,8,128]{2,1,0:T(8,128)(2,1)S(1)} %add_convert_fusion.2), channel_id=1, source_target_pairs={{0,32},{8,40},{16,48},{24,56},{32,0},{40,8},{48,16},{56,24},{1,33}... | collective-permute-start | bytes 196616 | tf_op jit(solution)/shard_map/ppermute | solution.py:509
  94.1 21.1 %collective-permute-start.19 = (bf16[32,8,128]{2,1,0:T(8,128)(2,1)S(1)}, bf16[32,8,128]{2,1,0:T(8,128)(2,1)S(1)}, u32[]{:S(2)}, u32[]{:S(2)}) collective-permute-start(bf16[32,8,128]{2,1,0:T(8,128)(2,1)S(1)} %add_convert_fusion.1), channel_id=1, source_target_pairs={{0,6},{1,7},{2,0},{3,1},{4,2},{5,3},{6,4},{7,5},{8,14},{9,15},{10,... | collective-permute-start | bytes 196616 | tf_op jit(solution)/shard_map/ppermute | solution.py:492
  99.8 15.4 %collective-permute-start.18 = (bf16[32,8,128]{2,1,0:T(8,128)(2,1)S(1)}, bf16[32,8,128]{2,1,0:T(8,128)(2,1)S(1)}, u32[]{:S(2)}, u32[]{:S(2)}) collective-permute-start(bf16[32,8,128]{2,1,0:T(8,128)(2,1)S(1)} %add_convert_fusion.1), channel_id=1, source_target_pairs={{0,2},{1,3},{2,4},{3,5},{4,6},{5,7},{6,0},{7,1},{8,10},{9,11},{10,... | collective-permute-start | bytes 196616 | tf_op jit(solution)/shard_map/ppermute | solution.py:492
  99.8 15.4 %collective-permute-start.17 = (bf16[32,8,128]{2,1,0:T(8,128)(2,1)S(1)}, bf16[32,8,128]{2,1,0:T(8,128)(2,1)S(1)}, u32[]{:S(2)}, u32[]{:S(2)}) collective-permute-start(bf16[32,8,128]{2,1,0:T(8,128)(2,1)S(1)} %add_convert_fusion.1), channel_id=1, source_target_pairs={{0,4},{1,5},{2,6},{3,7},{4,0},{5,1},{6,2},{7,3},{8,12},{9,13},{10,... | collective-permute-start | bytes 196616 | tf_op jit(solution)/shard_map/ppermute | solution.py:492
  103.9 0.9 copy-start
  104.8 0.7 copy-start.1
  108.0 14.2 %collective-permute-start.9 = (bf16[6,96,256]{2,1,0:T(8,128)(2,1)}, bf16[6,96,256]{2,1,0:T(8,128)(2,1)S(1)}, u32[]{:S(2)}, u32[]{:S(2)}) collective-permute-start(bf16[6,96,256]{2,1,0:T(8,128)(2,1)} %get-tuple-element.42), channel_id=1, source_target_pairs={{0,1},{1,0},{2,3},{3,2},{4,5},{5,4},{6,7},{7,6},{8,9},{9,8},{10,11... | collective-permute-start | bytes 884744 | tf_op jit(solution)/shard_map/ppermute | solution.py:485
  108.1 15.6 %collective-permute-start.10 = (bf16[6,96,256]{2,1,0:T(8,128)(2,1)}, bf16[6,96,256]{2,1,0:T(8,128)(2,1)S(1)}, u32[]{:S(2)}, u32[]{:S(2)}) collective-permute-start(bf16[6,96,256]{2,1,0:T(8,128)(2,1)} %get-tuple-element.43), channel_id=1, source_target_pairs={{0,7},{1,2},{2,1},{3,4},{4,3},{5,6},{6,5},{7,0},{8,15},{9,10},{10,... | collective-permute-start | bytes 884744 | tf_op jit(solution)/shard_map/ppermute | solution.py:484
  115.3 6.9 %collective-permute-start.20 = (bf16[32,8,128]{2,1,0:T(8,128)(2,1)S(1)}, bf16[32,8,128]{2,1,0:T(8,128)(2,1)S(1)}, u32[]{:S(2)}, u32[]{:S(2)}) collective-permute-start(bf16[32,8,128]{2,1,0:T(8,128)(2,1)S(1)} %add_convert_fusion), channel_id=1, source_target_pairs={{0,8},{8,0},{16,24},{24,16},{32,40},{40,32},{48,56},{56,48},{1,9},... | collective-permute-start | bytes 196616 | tf_op jit(solution)/shard_map/ppermute | solution.py:512
  122.2 15.1 %collective-permute-start.21 = (f32[32,8,128]{2,1,0:T(8,128)S(1)}, f32[32,8,128]{2,1,0:T(8,128)S(1)}, u32[]{:S(2)}, u32[]{:S(2)}) collective-permute-start(f32[32,8,128]{2,1,0:T(8,128)S(1)} %convert_add_fusion), channel_id=1, source_target_pairs={{0,1},{1,0},{2,3},{3,2},{4,5},{5,4},{6,7},{7,6},{8,9},{9,8},{10,11... | collective-permute-start | bytes 393224 | tf_op jit(solution)/shard_map/ppermute | solution.py:514
  122.3 1.5 %copy-start.9 = (bf16[6,96,256]{2,1,0:T(8,128)(2,1)}, bf16[6,96,256]{2,1,0:T(8,128)(2,1)S(1)}, u32[]{:S(2)}) copy-start(bf16[6,96,256]{2,1,0:T(8,128)(2,1)S(1)} %collective-permute-done.9.refs_0_) | copy-start | bytes 884740
  123.8 0.7 copy-start.10
  137.3 0.7 copy-start.2

commit v4 on v3

--- a/solution.py
+++ b/solution.py
@@ -59,97 +59,64 @@
         tmp[h, pl.ds(a, c, stride=na), :] = column[:, 128 * h : 128 * h + 128]
 
 
-def columns_body(place, x_ref, o_ref, near_ref, far_ref, tmp):
+def columns_body(place, x_ref, o_ref, near_ref, far_ref, near_row, far_row, tmp):
     c, nr, na = x_ref.shape[1:4]
-    p = place[0]
+    p, q = place[0], place[1]
     for r in range(nr):
         put_rows(tmp, x_ref[0, :, r].astype(f32))
         for a in range(na):
             o_ref[r, a] = get_column(tmp, a, c, na).astype(bf16)
         near_ref[r] = o_ref[r, (na - 1) * (1 - p)]
         far_ref[r] = o_ref[r, (na - 1) * p]
+    near_row[1 : na + 1] = o_ref[(nr - 1) * (1 - q)]
+    far_row[1 : na + 1] = o_ref[(nr - 1) * q]
 
 
 def to_columns(place, field):
     _, c, nr, na, nz = field.shape
-    face = shape((nr, c, nz))
-    part = c // 3
-    face_spec = pl.BlockSpec((nr, part, nz), lambda g, _: (0, g, 0))
+    face, row = shape((nr, c, nz)), shape((na + 2, c, nz))
+    part = c // 2
+    rest = [face, face, row, row]
     return call(
-        columns_body, place, 3, (field,),
+        columns_body, place, 2, (field,),
         [pl.BlockSpec((1, part, nr, na, nz), lambda g, _: (0, g, 0, 0, 0))],
-        [shape((nr, na, c, nz)), face, face],
-        [pl.BlockSpec((nr, na, part, nz), lambda g, _: (0, 0, g, 0)), face_spec, face_spec],
+        [shape((nr, na, c, nz))] + rest,
+        [pl.BlockSpec((nr, na, part, nz), lambda g, _: (0, 0, g, 0))]
+        + [pl.BlockSpec((y.shape[0], part, nz), lambda g, _: (0, g, 0)) for y in rest],
         [pltpu.VMEM((nz // 128, part * na, 128), f32)], 10000000)
 
 
 ANY = pl.BlockSpec(memory_space=pl.ANY)
 
 
-def edges_body(place, rows, near, far, out_near, out_far, buf, sems):
-    p, q = place[0], place[1]
-    last, na = rows.shape[0] - 1, rows.shape[1]
-    right, left = (na + 1) * (1 - p), (na + 1) * p
-    step = (near.shape[0] - 1) // last
-    loads = []
-    for k, r in enumerate((last * (1 - q), last * q)):
-        for n, (src, dst) in enumerate((
-            (rows.at[r], buf.at[k, pl.ds(1, na)]),
-            (near.at[step * r], buf.at[k, right]),
-            (far.at[step * r], buf.at[k, left]),
-        )):
-            loads.append(pltpu.make_async_copy(src, dst, sems.at[k, n]))
-    stores = [pltpu.make_async_copy(buf.at[k], out, sems.at[k, 3])
-              for k, out in enumerate((out_near, out_far))]
+def insert_body(axis, place, a_near, a_far, h_near, h_far, out_near, out_far, buf, sems):
+    along, across = place[axis], place[1 - axis]
+    last = h_near.shape[0] - 1
+    end = out_near.shape[0] - 1
+    loads, stores = [], []
+    for k, (out, at) in enumerate(
+        ((out_near, last * (1 - across)), (out_far, last * across))
+    ):
+        for n, (halo, to) in enumerate(((h_near, end * (1 - along)), (h_far, end * along))):
+            i = 2 * k + n
+            loads.append(pltpu.make_async_copy(halo.at[at], buf.at[i], sems.at[0, i]))
+            stores.append(pltpu.make_async_copy(buf.at[i], out.at[to], sems.at[1, i]))
     for copy in loads:
         copy.start()
-    for k, store in enumerate(stores):
-        for copy in loads[3 * k : 3 * k + 3]:
-            copy.wait()
+    for load, store in zip(loads, stores):
+        load.wait()
         store.start()
-    for store in stores:
-        store.wait()
-
-
-def edges(place, rows, near, far):
-    _, na, c, z = rows.shape
-    out = shape((na + 2, c, z))
+    for copy in stores:
+        copy.wait()
+
+
+def insert(place, axis, messages, halos):
+    near, far = messages
+    _, c, z = near.shape
     return call(
-        edges_body, place, 1, (rows, near, far), [ANY, ANY, ANY], [out, out],
-        [ANY, ANY], [pltpu.VMEM((2, na + 2, c, z), bf16), pltpu.SemaphoreType.DMA((2, 4))],
-        1000000)
-
-
-def sides_body(place, near_face, far_face, near_end, far_end, out_near, out_far, buf, sems):
-    p, q = place[0], place[1]
-    last = near_end.shape[0] - 1
-    loads = []
-    for k, (face, col) in enumerate(((near_face, last * (1 - p)), (far_face, last * p))):
-        for n, (src, dst) in enumerate((
-            (face, buf.at[k, pl.ds(1, 4)]),
-            (near_end.at[col], buf.at[k, 5 * (1 - q)]),
-            (far_end.at[col], buf.at[k, 5 * q]),
-        )):
-            loads.append(pltpu.make_async_copy(src, dst, sems.at[k, n]))
-    stores = [pltpu.make_async_copy(buf.at[k], out, sems.at[k, 3])
-              for k, out in enumerate((out_near, out_far))]
-    for copy in loads:
-        copy.start()
-    for k, store in enumerate(stores):
-        for copy in loads[3 * k : 3 * k + 3]:
-            copy.wait()
-        store.start()
-    for store in stores:
-        store.wait()
-
-
-def six_rows(place, near_face, far_face, ends):
-    _, c, z = ends[0].shape
-    out = shape((6, c, z))
-    return call(
-        sides_body, place, 1, (near_face, far_face, *ends), [ANY] * 4, [out, out],
-        [ANY, ANY], [pltpu.VMEM((2, 6, c, z), bf16), pltpu.SemaphoreType.DMA((2, 4))],
-        1000000)
+        lambda *refs: insert_body(axis, *refs), place, 1, (near, far, *halos), [ANY] * 4,
+        [shape(near.shape)] * 2, [ANY, ANY],
+        [pltpu.VMEM((4, c, z), bf16), pltpu.SemaphoreType.DMA((2, 4))], 1000000, {1: 0, 2: 1})
 
 
 class Loader:
@@ -287,8 +254,8 @@
     small = [pltpu.make_async_copy(b_ref, b_buf, sems.at[3, 3])]
     if outer:
         small += [
-            pltpu.make_async_copy(near_in, near_ref.at[pl.ds(1, 2)], sems.at[4, 3]),
-            pltpu.make_async_copy(far_in, far_ref.at[pl.ds(1, 2)], sems.at[5, 3]),
+            pltpu.make_async_copy(near_in, near_ref.at[pl.ds(2, 2)], sems.at[4, 3]),
+            pltpu.make_async_copy(far_in, far_ref.at[pl.ds(2, 2)], sems.at[5, 3]),
             pltpu.make_async_copy(bsum_in, total, sems.at[0, 4]),
         ]
 
@@ -330,7 +297,7 @@
 
     lax.fori_loop(0, na // 2, pair, 0)
     out_ref[0, :, 0] = get_rows(res, c, na).astype(bf16)
-    slot = r if outer else g
+    slot = r + 1 if outer else g
     near_ref[slot] = delta_ref[0, (na - 1) * (1 - p)]
     far_ref[slot] = delta_ref[0, (na - 1) * p]
     if outer:
@@ -349,7 +316,7 @@
     field = pl.BlockSpec(
         (1, c, 1, na, z), lambda g, _: (0, 0, 3 * g if outer else 1 + g, 0, 0))
     args = [x, *sides, *ends, w, b, cot]
-    face, row = shape((4 if outer else 2, c, z)), shape((na, c, z))
+    face, row = shape((6 if outer else 2, c, z)), shape((na, c, z))
     rest = [face, face, shape((c, z), f32)]
     rest += [row, row] if outer else [shape((3 * c, K9), f32)]
     alias = None
@@ -504,13 +471,15 @@
         y = lax.ppermute(mine[s].astype(bf16), "dp", [(i, (i + s) % 4) for i in range(4)])
         total = total + y.astype(f32)
     n = lax.axis_size("rad")
-    for step in (2, 4):
-        total = total.astype(bf16)
-        y = lax.ppermute(total, "rad", [(i, i ^ step) for i in range(n)])
-        total = total.astype(f32) + y.astype(f32)
-    total = sum_over(total.astype(bf16), "azi", 2).astype(bf16)
-    y = lax.ppermute(total, "rad", [(i, i ^ 1) for i in range(lax.axis_size("rad"))])
-    total = total.astype(f32) + y.astype(f32)
+    total = total.astype(bf16)
+    y = lax.ppermute(total, "rad", [(i, i ^ 2) for i in range(n)])
+    total = (total.astype(f32) + y.astype(f32)).astype(bf16)
+    a, b, c = (
+        lax.ppermute(total, "rad", [(i, i ^ step) for i in range(n)]) for step in (1, 4, 5)
+    )
+    a, b, c, d = (y.astype(f32) for y in (a, b, c, total))
+    total = (d + a) + (b + c)
+    total = sum_over(total.astype(bf16), "azi", 2)
     y = lax.ppermute(total, "azi", core)
     low = lax.axis_index("azi") % 2 == 0
     return jnp.concatenate([jnp.where(low, total, y), jnp.where(low, y, total)], axis=0)
@@ -534,9 +503,9 @@
     place = jnp.stack(
         [lax.axis_index("azi") % 2, lax.axis_index("rad") % 2, lax.axis_index("dp")]
     ).astype(jnp.int32)
-    x, near_face, far_face = to_columns(place, inputs)
+    x, near_face, far_face, near_row, far_row = to_columns(place, inputs)
     sides = swap((near_face, far_face), "azi")
-    ends = swap(edges(place, x, *sides), "rad")
+    ends = swap(insert(place, 0, (near_row, far_row), sides), "rad")
     w_fwd, w_back, b_col = whole_weights(weight, bias)
     out, d_in, near_in, far_in, bsum, acc = forward(
         place, x, sides, (), w_fwd, b_col, cotangent)
@@ -544,7 +513,7 @@
         place, x, sides, ends, w_fwd, b_col, cotangent, [out, near_in, far_in, bsum])
     d_ends = swap((d_near, d_far), "rad")
     keep, send = weight_terms(place, x, sides, ends, d_out, bsum, acc)
-    d_sides = swap(six_rows(place, near_face, far_face, d_ends), "azi")
+    d_sides = swap(insert(place, 1, (near_face, far_face), d_ends), "azi")
     tiles = reduce_terms(keep, send)
     input_grad = backward(place, d_in, d_out, d_sides, d_ends, w_back)
     summed = tiles[:63].reshape(3, 21, 8, 128).transpose(0, 2, 1, 3).reshape(24, 21 * 128)

time: 138 us -> 152 us (1.10)
  the two profiles are of different devices: /device:TPU:8 before, /device:TPU:73 now
where the time goes in v4:
time: 152 us; the launch traced here: 151 us
  Pallas kernels  52.9 us (35%)
  starting transfers between devices  45.9 us (30%)
  waiting for transfers between devices  37.9 us (25%)
  local copies, waits for them, and re-layouts  9.72 us (6%)
  other arithmetic  3.68 us (2%)
    pallas_call x7, Pallas kernels, call(): pl.pallas_call(body, grid_spec=pltpu.PrefetchScalarGridSpec(num_scalar_pr...  52.9 us
    ppermute x4, waiting for transfers between devices, swap(): got_far = lax.ppermute(far, axis, far_pairs(axis))  24.2 us
    ppermute x4, starting transfers between devices, swap(): got_far = lax.ppermute(far, axis, far_pairs(axis))  12 us
    ppermute x3, starting transfers between devices, sum_over(): lax.ppermute(x, axis, [(i, (i + step * s) % n) for i in range(n)])  6.99 us
    ppermute x1, starting transfers between devices, reduce_terms(): y = lax.ppermute(total, 'azi', core)  6.31 us
    ppermute x4, starting transfers between devices, swap(): got_near = lax.ppermute(near, axis, near_pairs(axis))  6.21 us
    ppermute x3, starting transfers between devices, reduce_terms(): lax.ppermute(total, 'rad', [(i, i ^ step) for i in range(n)])  5.86 us
    ppermute x3, starting transfers between devices, whole_weights(): lax.ppermute(packed, 'dp', [(i, (i + s) % 4) for i in range(4)])  5.45 us
  transfers between devices with their start and end apart: 23, of which 12 were waited for; matrix products, arithmetic and copies ran while one was open for 5% of the time, Pallas kernels for 14%

profile of v4, /device:TPU:73, one launch (start us, length us, event | category | flops | bytes accessed | tf_op | source)
XLA Modules:
  0.0 151.2 jit_solution(12977977477535080672)
XLA Ops:
  0.6 0.7 broadcast_in_dim.2
  1.4 1.0 fusion.8
  2.3 2.8 %collective-permute-start.5 = (bf16[24,2720]{1,0:T(8,128)(2,1)S(1)}, bf16[24,2720]{1,0:T(8,128)(2,1)S(1)}, u32[]{:S(2)}, u32[]{:S(2)}) collective-permute-start(bf16[24,2720]{1,0:T(8,128)(2,1)S(1)} %get-tuple-element.58), channel_id=1, source_target_pairs={{0,128},{64,192},{128,0},{192,64},{1,129},{65,193},{129,1},{193,65... | collective-permute-start | bytes 391688 | tf_op jit(solution)/shard_map/ppermute | solution.py:492
  5.1 0.3 collective-permute-start.4
  5.4 2.4 %collective-permute-start.6 = (bf16[24,2720]{1,0:T(8,128)(2,1)S(1)}, bf16[24,2720]{1,0:T(8,128)(2,1)S(1)}, u32[]{:S(2)}, u32[]{:S(2)}) collective-permute-start(bf16[24,2720]{1,0:T(8,128)(2,1)S(1)} %get-tuple-element.58), channel_id=1, source_target_pairs={{0,192},{64,0},{128,64},{192,128},{1,193},{65,1},{129,65},{193,129... | collective-permute-start | bytes 391688 | tf_op jit(solution)/shard_map/ppermute | solution.py:492
  7.8 0.6 pad_add_fusion.place.refs_0_
  8.4 3.9 %shard_map.75 = (bf16[4,8,96,256]{3,2,1,0:T(8,128)(2,1)}, bf16[4,96,256]{2,1,0:T(8,128)(2,1)}, bf16[4,96,256]{2,1,0:T(8,128)(2,1)}, bf16[10,96,256]{2,1,0:T(8,128)(2,1)}, bf16[10,96,256]{2,1,0:T(8,128)(2,1)}) custom-call(s32[3]{0:T(128)} %pad_add_fusion.place.refs_0_, bf16[1,96,4,8,256]{4,3,2,1,0:T(8,128)(2,1)} %x_ref.1), custom_call_target="tpu_custom_call" | custom-call | flops 10000000 | bytes 4000000 | tf_op jit(solution)/shard_map/pallas_call | solution.py:25
  12.3 1.5 %collective-permute-start = (bf16[4,96,256]{2,1,0:T(8,128)(2,1)}, bf16[4,96,256]{2,1,0:T(8,128)(2,1)S(1)}, u32[]{:S(2)}, u32[]{:S(2)}) collective-permute-start(bf16[4,96,256]{2,1,0:T(8,128)(2,1)} %get-tuple-element.29), channel_id=1, source_target_pairs={{0,1},{1,0},{2,3},{3,2},{4,5},{5,4},{6,7},{7,6},{8,9},{9,8},{10,11... | collective-permute-start | bytes 589832 | tf_op jit(solution)/shard_map/ppermute | solution.py:452
  13.8 4.1 %collective-permute-start.1 = (bf16[4,96,256]{2,1,0:T(8,128)(2,1)}, bf16[4,96,256]{2,1,0:T(8,128)(2,1)S(1)}, u32[]{:S(2)}, u32[]{:S(2)}) collective-permute-start(bf16[4,96,256]{2,1,0:T(8,128)(2,1)} %get-tuple-element.30), channel_id=1, source_target_pairs={{0,7},{1,2},{2,1},{3,4},{4,3},{5,6},{6,5},{7,0},{8,15},{9,10},{10,... | collective-permute-start | bytes 589832 | tf_op jit(solution)/shard_map/ppermute | solution.py:451
  17.9 0.0 collective-permute-done.refs_3_.refs_2_.refs_0_
  17.9 0.0 copy-start.3
  18.0 5.6 %collective-permute-done.1.refs_4_.refs_3_.refs_1_ = bf16[4,96,256]{2,1,0:T(8,128)(2,1)S(1)} collective-permute-done((bf16[4,96,256]{2,1,0:T(8,128)(2,1)}, bf16[4,96,256]{2,1,0:T(8,128)(2,1)S(1)}, u32[]{:S(2)}, u32[]{:S(2)}) %collective-permute-start.1) | collective-permute-done | bytes 196640 | tf_op jit(solution)/shard_map/ppermute | solution.py:451
  23.6 0.7 copy-done.4
  24.2 2.2 %shard_map.76 = (bf16[10,96,256]{2,1,0:T(8,128)(2,1)}, bf16[10,96,256]{2,1,0:T(8,128)(2,1)}) custom-call(s32[3]{0:T(128)} %pad_add_fusion.place.refs_0_, bf16[10,96,256]{2,1,0:T(8,128)(2,1)} %get-tuple-element.31.refs_1_, bf16[10,96,256]{2,1,0:T(8,128)(2,1)} %get-tuple-element.32.refs_2_, ...), custom_call_target="tpu_custom_call", output_to_operand_aliasing={{0}: (1, {}), {1}: (2, {})} | custom-call | flops 1000000 | bytes 4000000 | tf_op jit(solution)/shard_map/pallas_call | solution.py:25
  26.5 0.1 collective-permute-start.2
  26.6 3.2 %collective-permute-start.3 = (bf16[10,96,256]{2,1,0:T(8,128)(2,1)}, bf16[10,96,256]{2,1,0:T(8,128)(2,1)S(1)}, u32[]{:S(2)}, u32[]{:S(2)}) collective-permute-start(bf16[10,96,256]{2,1,0:T(8,128)(2,1)} %get-tuple-element.34), channel_id=1, source_target_pairs={{8,16},{16,8},{24,32},{32,24},{40,48},{48,40},{9,17},{17,9},{25,33... | collective-permute-start | bytes 1474568 | tf_op jit(solution)/shard_map/ppermute | solution.py:451
  29.8 0.0 collective-permute-done.5
  29.8 0.0 collective-permute-done.6
  29.8 0.1 pad_maximum_fusion
  29.9 0.6 gather_fusion
  30.5 0.7 slice.55.refs_5_.refs_7_
  31.2 0.3 copy.15
  31.6 0.7 copy.16
  32.2 1.3 reshape.93.refs_4_.refs_6_
  33.5 13.4 %shard_map.77 = (bf16[1,96,4,8,256]{4,3,2,1,0:T(8,128)(2,1)}, bf16[2,8,96,256]{3,2,1,0:T(8,128)(2,1)}, bf16[2,96,256]{2,1,0:T(8,128)(2,1)}, bf16[2,96,256]{2,1,0...) custom-call(s32[3]{0:T(128)} %pad_add_fusion.place.refs_0_, ...), custom_call_target="tpu_custom_call" | custom-call | flops 5000000000 | bytes 4000000 | tf_op jit(solution)/shard_map/pallas_call | solution.py:25
  47.0 1.7 %collective-permute-done.3.refs_5_.refs_3_ = bf16[10,96,256]{2,1,0:T(8,128)(2,1)S(1)} collective-permute-done((bf16[10,96,256]{2,1,0:T(8,128)(2,1)}, bf16[10,96,256]{2,1,0:T(8,128)(2,1)S(1)}, u32[]{:S(2)}, u32[]{:S(2)}) %collective-permute-start.3) | collective-permute-done | bytes 491552 | tf_op jit(solution)/shard_map/ppermute | solution.py:451
  48.7 0.8 copy-done.6
  49.5 9.8 %shard_map.78 = (bf16[1,96,4,8,256]{4,3,2,1,0:T(8,128)(2,1)}, bf16[2,8,96,256]{3,2,1,0:T(8,128)(2,1)}, bf16[6,96,256]{2,1,0:T(8,128)(2,1)}, bf16[6,96,256]{2,1,0...) custom-call(s32[3]{0:T(128)} %pad_add_fusion.place.refs_0_, ...), custom_call_target="tpu_custom_call", output_to_operand_aliasing={{0}: (9, {})} | custom-call | flops 5000000000 | bytes 4000000 | tf_op jit(solution)/shard_map/pallas_call | solution.py:25
  59.3 8.6 %shard_map.81 = (bf16[4,32,8,128]{3,2,1,0:T(8,128)(2,1)}, bf16[4,32,8,128]{3,2,1,0:T(8,128)(2,1)}) custom-call(s32[3]{0:T(128)} %pad_add_fusion.place.refs_0_, bf16[4,8,96,256]{3,2,1,0:T(8,128)(2,1)} %get-tuple-element.28.refs_1_.x_ref, bf16[4,96,256]{2,1,0:T(8,128)(2,1)} %copy-done.3, bf16[4,96,256]{2,1,0:T(8,128)(2,1)} %copy-done.4, ...), custom_call_target="tpu_custom_call" | custom-call | flops 2500000000 | bytes 4000000 | tf_op jit(solution)/shard_map/pallas_call | solution.py:25
  67.9 0.2 collective-permute-start.11
  68.1 1.6 %collective-permute-done.11 = bf16[4,32,8,128]{3,2,1,0:T(8,128)(2,1)S(1)} collective-permute-done((bf16[4,32,8,128]{3,2,1,0:T(8,128)(2,1)}, bf16[4,32,8,128]{3,2,1,0:T(8,128)(2,1)S(1)}, u32[]{:S(2)}, u32[]{:S(2)}) %collective-permute-start.11) | collective-permute-done | bytes 262176 | tf_op jit(solution)/shard_map/ppermute | solution.py:467
  69.7 1.0 fusion.3
  70.7 0.1 collective-permute-start.12
  70.8 2.7 %collective-permute-start.14 = (bf16[32,8,128]{2,1,0:T(8,128)(2,1)S(1)}, bf16[32,8,128]{2,1,0:T(8,128)(2,1)S(1)}, u32[]{:S(2)}, u32[]{:S(2)}) collective-permute-start(bf16[32,8,128]{2,1,0:T(8,128)(2,1)S(1)} %get-tuple-element.53), channel_id=1, source_target_pairs={{0,192},{64,0},{128,64},{192,128},{1,193},{65,1},{129,65},{193,129... | collective-permute-start | bytes 196616 | tf_op jit(solution)/shard_map/ppermute | solution.py:471
  73.5 2.0 %collective-permute-done.12 = bf16[32,8,128]{2,1,0:T(8,128)(2,1)S(1)} collective-permute-done((bf16[32,8,128]{2,1,0:T(8,128)(2,1)S(1)}, bf16[32,8,128]{2,1,0:T(8,128)(2,1)S(1)}, u32[]{:S(2)}, u32[]{:S(2)}) %collective-permute-start.12) | collective-permute-done | bytes 65568 | tf_op jit(solution)/shard_map/ppermute | solution.py:471
  75.5 0.7 collective-permute-done.14
  76.2 1.8 %collective-permute-done.13 = bf16[32,8,128]{2,1,0:T(8,128)(2,1)S(1)} collective-permute-done((bf16[32,8,128]{2,1,0:T(8,128)(2,1)S(1)}, bf16[32,8,128]{2,1,0:T(8,128)(2,1)S(1)}, u32[]{:S(2)}, u32[]{:S(2)}) %collective-permute-start.13) | collective-permute-done | bytes 65568 | tf_op jit(solution)/shard_map/ppermute | solution.py:471
  78.1 0.9 fusion.2
  79.0 0.1 collective-permute-start.15
  79.1 3.1 %collective-permute-done.15 = bf16[32,8,128]{2,1,0:T(8,128)(2,1)S(1)} collective-permute-done((bf16[32,8,128]{2,1,0:T(8,128)(2,1)S(1)}, bf16[32,8,128]{2,1,0:T(8,128)(2,1)S(1)}, u32[]{:S(2)}, u32[]{:S(2)}) %collective-permute-start.15) | collective-permute-done | bytes 65568 | tf_op jit(solution)/shard_map/ppermute | solution.py:475
  82.2 3.6 %collective-permute-start.18 = (bf16[32,8,128]{2,1,0:T(8,128)(2,1)S(1)}, bf16[32,8,128]{2,1,0:T(8,128)(2,1)S(1)}, u32[]{:S(2)}, u32[]{:S(2)}) collective-permute-start(bf16[32,8,128]{2,1,0:T(8,128)(2,1)S(1)} %add_convert_fusion.1), channel_id=1, source_target_pairs={{0,40},{8,32},{16,56},{24,48},{32,8},{40,0},{48,24},{56,16},{1,41}... | collective-permute-start | bytes 196616 | tf_op jit(solution)/shard_map/ppermute | solution.py:478
  85.8 2.2 %collective-permute-start.17 = (bf16[32,8,128]{2,1,0:T(8,128)(2,1)S(1)}, bf16[32,8,128]{2,1,0:T(8,128)(2,1)S(1)}, u32[]{:S(2)}, u32[]{:S(2)}) collective-permute-start(bf16[32,8,128]{2,1,0:T(8,128)(2,1)S(1)} %add_convert_fusion.1), channel_id=1, source_target_pairs={{0,32},{8,40},{16,48},{24,56},{32,0},{40,8},{48,16},{56,24},{1,33}... | collective-permute-start | bytes 196616 | tf_op jit(solution)/shard_map/ppermute | solution.py:478
  88.1 0.0 collective-permute-done.18
  88.1 2.4 %collective-permute-done.17 = bf16[32,8,128]{2,1,0:T(8,128)(2,1)S(1)} collective-permute-done((bf16[32,8,128]{2,1,0:T(8,128)(2,1)S(1)}, bf16[32,8,128]{2,1,0:T(8,128)(2,1)S(1)}, u32[]{:S(2)}, u32[]{:S(2)}) %collective-permute-start.17) | collective-permute-done | bytes 65568 | tf_op jit(solution)/shard_map/ppermute | solution.py:478
  90.4 1.6 %collective-permute-done.16 = bf16[32,8,128]{2,1,0:T(8,128)(2,1)S(1)} collective-permute-done((bf16[32,8,128]{2,1,0:T(8,128)(2,1)S(1)}, bf16[32,8,128]{2,1,0:T(8,128)(2,1)S(1)}, u32[]{:S(2)}, u32[]{:S(2)}) %collective-permute-start.16) | collective-permute-done | bytes 65568 | tf_op jit(solution)/shard_map/ppermute | solution.py:478
  92.1 0.1 collective-permute-start.21
  92.2 3.6 %collective-permute-start.20 = (bf16[32,8,128]{2,1,0:T(8,128)(2,1)S(1)}, bf16[32,8,128]{2,1,0:T(8,128)(2,1)S(1)}, u32[]{:S(2)}, u32[]{:S(2)}) collective-permute-start(bf16[32,8,128]{2,1,0:T(8,128)(2,1)S(1)} %add_convert_fusion), channel_id=1, source_target_pairs={{0,2},{1,3},{2,4},{3,5},{4,6},{5,7},{6,0},{7,1},{8,10},{9,11},{10,... | collective-permute-start | bytes 196616 | tf_op jit(solution)/shard_map/ppermute | solution.py:459
  95.8 3.3 %collective-permute-start.19 = (bf16[32,8,128]{2,1,0:T(8,128)(2,1)S(1)}, bf16[32,8,128]{2,1,0:T(8,128)(2,1)S(1)}, u32[]{:S(2)}, u32[]{:S(2)}) collective-permute-start(bf16[32,8,128]{2,1,0:T(8,128)(2,1)S(1)} %add_convert_fusion), channel_id=1, source_target_pairs={{0,4},{1,5},{2,6},{3,7},{4,0},{5,1},{6,2},{7,3},{8,12},{9,13},{10,... | collective-permute-start | bytes 196616 | tf_op jit(solution)/shard_map/ppermute | solution.py:459
  99.1 0.8 collective-permute-start.7
  99.9 4.4 %collective-permute-start.8 = (bf16[8,96,256]{2,1,0:T(8,128)(2,1)S(1)}, bf16[8,96,256]{2,1,0:T(8,128)(2,1)S(1)}, u32[]{:S(2)}, u32[]{:S(2)}) collective-permute-start(bf16[8,96,256]{2,1,0:T(8,128)(2,1)S(1)} %copy-done.7), channel_id=1, source_target_pairs={{8,16},{16,8},{24,32},{32,24},{40,48},{48,40},{9,17},{17,9},{25,33... | collective-permute-start | bytes 1179656 | tf_op jit(solution)/shard_map/ppermute | solution.py:451
  104.3 6.3 %collective-permute-start.22 = (f32[32,8,128]{2,1,0:T(8,128)S(1)}, f32[32,8,128]{2,1,0:T(8,128)S(1)}, u32[]{:S(2)}, u32[]{:S(2)}) collective-permute-start(f32[32,8,128]{2,1,0:T(8,128)S(1)} %add_add_fusion), channel_id=1, source_target_pairs={{0,1},{1,0},{2,3},{3,2},{4,5},{5,4},{6,7},{7,6},{8,9},{9,8},{10,11... | collective-permute-start | bytes 393224 | tf_op jit(solution)/shard_map/ppermute | solution.py:483
  110.7 0.5 copy.17
  111.2 1.3 reshape.94.refs_4_
  112.5 6.6 %collective-permute-done.8.refs_4_.refs_3_ = bf16[8,96,256]{2,1,0:T(8,128)(2,1)S(1)} collective-permute-done((bf16[8,96,256]{2,1,0:T(8,128)(2,1)S(1)}, bf16[8,96,256]{2,1,0:T(8,128)(2,1)S(1)}, u32[]{:S(2)}, u32[]{:S(2)}) %collective-permute-start.8) | collective-permute-done | bytes 393248 | tf_op jit(solution)/shard_map/ppermute | solution.py:451
  119.1 0.7 copy-done.1
  119.8 2.3 %shard_map.79 = (bf16[6,96,256]{2,1,0:T(8,128)(2,1)}, bf16[6,96,256]{2,1,0:T(8,128)(2,1)}) custom-call(s32[3]{0:T(128)} %pad_add_fusion.place.refs_0_, bf16[6,96,256]{2,1,0:T(8,128)(2,1)} %get-tuple-element.42.refs_1_, bf16[6,96,256]{2,1,0:T(8,128)(2,1)} %get-tuple-element.43.refs_2_, ...), custom_call_target="tpu_custom_call", output_to_operand_aliasing={{0}: (1, {}), {1}: (2, {})} | custom-call | flops 1000000 | bytes 4000000 | tf_op jit(solution)/shard_map/pallas_call | solution.py:25
  122.1 3.8 %collective-permute-start.9 = (bf16[6,96,256]{2,1,0:T(8,128)(2,1)}, bf16[6,96,256]{2,1,0:T(8,128)(2,1)S(1)}, u32[]{:S(2)}, u32[]{:S(2)}) collective-permute-start(bf16[6,96,256]{2,1,0:T(8,128)(2,1)} %get-tuple-element.46), channel_id=1, source_target_pairs={{0,1},{1,0},{2,3},{3,2},{4,5},{5,4},{6,7},{7,6},{8,9},{9,8},{10,11... | collective-permute-start | bytes 884744 | tf_op jit(solution)/shard_map/ppermute | solution.py:452
  125.9 0.3 collective-permute-start.10
  126.2 0.0 copy-start.2
  126.2 0.7 slice_reduce_fusion
  126.9 0.4 collective-permute-done.9.refs_0_
  127.3 10.2 %collective-permute-done.10.refs_1_ = bf16[6,96,256]{2,1,0:T(8,128)(2,1)S(1)} collective-permute-done((bf16[6,96,256]{2,1,0:T(8,128)(2,1)}, bf16[6,96,256]{2,1,0:T(8,128)(2,1)S(1)}, u32[]{:S(2)}, u32[]{:S(2)}) %collective-permute-start.10) | collective-permute-done | bytes 294944 | tf_op jit(solution)/shard_map/ppermute | solution.py:451
  137.5 0.7 copy-done.10
  138.2 12.8 %shard_map.80 = bf16[1,96,4,8,256]{4,3,2,1,0:T(8,128)(2,1)} custom-call(s32[3]{0:T(128)} %pad_add_fusion.place.refs_0_, bf16[2,8,96,256]{3,2,1,0:T(8,128)(2,1)} %get-tuple-element.40.d_in, bf16[2,8,96,256]{3,2,1,0:T(8,128)(2,1)} %get-tuple-element.41.d_out.refs_4_, bf16[6,96,256]{2,1,0:T(8,128)(2,1)} %copy-done.9, bf16[6,96,256]{2,1,0:T(8,128)(2,1)} %copy-done.10, ...), custom_call_target="tpu_custom_call" | custom-call | flops 5000000000 | bytes 4000000 | tf_op jit(solution)/shard_map/pallas_call | solution.py:25
  (34 shorter events, 0.3 us)
Async XLA Ops:
  2.3 27.5 %collective-permute-start.5 = (bf16[24,2720]{1,0:T(8,128)(2,1)S(1)}, bf16[24,2720]{1,0:T(8,128)(2,1)S(1)}, u32[]{:S(2)}, u32[]{:S(2)}) collective-permute-start(bf16[24,2720]{1,0:T(8,128)(2,1)S(1)} %get-tuple-element.58), channel_id=1, source_target_pairs={{0,128},{64,192},{128,0},{192,64},{1,129},{65,193},{129,1},{193,65... | collective-permute-start | bytes 391688 | tf_op jit(solution)/shard_map/ppermute | solution.py:492
  5.1 24.7 %collective-permute-start.4 = (bf16[24,2720]{1,0:T(8,128)(2,1)S(1)}, bf16[24,2720]{1,0:T(8,128)(2,1)S(1)}, u32[]{:S(2)}, u32[]{:S(2)}) collective-permute-start(bf16[24,2720]{1,0:T(8,128)(2,1)S(1)} %get-tuple-element.58), channel_id=1, source_target_pairs={{0,64},{64,128},{128,192},{192,0},{1,65},{65,129},{129,193},{193,1... | collective-permute-start | bytes 391688 | tf_op jit(solution)/shard_map/ppermute | solution.py:492
  5.4 24.4 %collective-permute-start.6 = (bf16[24,2720]{1,0:T(8,128)(2,1)S(1)}, bf16[24,2720]{1,0:T(8,128)(2,1)S(1)}, u32[]{:S(2)}, u32[]{:S(2)}) collective-permute-start(bf16[24,2720]{1,0:T(8,128)(2,1)S(1)} %get-tuple-element.58), channel_id=1, source_target_pairs={{0,192},{64,0},{128,64},{192,128},{1,193},{65,1},{129,65},{193,129... | collective-permute-start | bytes 391688 | tf_op jit(solution)/shard_map/ppermute | solution.py:492
  12.3 5.7 %collective-permute-start = (bf16[4,96,256]{2,1,0:T(8,128)(2,1)}, bf16[4,96,256]{2,1,0:T(8,128)(2,1)S(1)}, u32[]{:S(2)}, u32[]{:S(2)}) collective-permute-start(bf16[4,96,256]{2,1,0:T(8,128)(2,1)} %get-tuple-element.29), channel_id=1, source_target_pairs={{0,1},{1,0},{2,3},{3,2},{4,5},{5,4},{6,7},{7,6},{8,9},{9,8},{10,11... | collective-permute-start | bytes 589832 | tf_op jit(solution)/shard_map/ppermute | solution.py:452
  13.8 9.8 %collective-permute-start.1 = (bf16[4,96,256]{2,1,0:T(8,128)(2,1)}, bf16[4,96,256]{2,1,0:T(8,128)(2,1)S(1)}, u32[]{:S(2)}, u32[]{:S(2)}) collective-permute-start(bf16[4,96,256]{2,1,0:T(8,128)(2,1)} %get-tuple-element.30), channel_id=1, source_target_pairs={{0,7},{1,2},{2,1},{3,4},{4,3},{5,6},{6,5},{7,0},{8,15},{9,10},{10,... | collective-permute-start | bytes 589832 | tf_op jit(solution)/shard_map/ppermute | solution.py:451
  17.9 5.6 %copy-start.3 = (bf16[4,96,256]{2,1,0:T(8,128)(2,1)}, bf16[4,96,256]{2,1,0:T(8,128)(2,1)S(1)}, u32[]{:S(2)}) copy-start(bf16[4,96,256]{2,1,0:T(8,128)(2,1)S(1)} %collective-permute-done.refs_3_.refs_2_.refs_0_) | copy-start | bytes 589828
  23.6 0.7 copy-start.4
  26.5 20.5 %collective-permute-start.2 = (bf16[10,96,256]{2,1,0:T(8,128)(2,1)}, bf16[10,96,256]{2,1,0:T(8,128)(2,1)S(1)}, u32[]{:S(2)}, u32[]{:S(2)}) collective-permute-start(bf16[10,96,256]{2,1,0:T(8,128)(2,1)} %get-tuple-element.33), channel_id=1, source_target_pairs={{0,8},{8,0},{16,24},{24,16},{32,40},{40,32},{48,56},{56,48},{1,9},... | collective-permute-start | bytes 1474568 | tf_op jit(solution)/shard_map/ppermute | solution.py:452
  26.6 22.1 %collective-permute-start.3 = (bf16[10,96,256]{2,1,0:T(8,128)(2,1)}, bf16[10,96,256]{2,1,0:T(8,128)(2,1)S(1)}, u32[]{:S(2)}, u32[]{:S(2)}) collective-permute-start(bf16[10,96,256]{2,1,0:T(8,128)(2,1)} %get-tuple-element.34), channel_id=1, source_target_pairs={{8,16},{16,8},{24,32},{32,24},{40,48},{48,40},{9,17},{17,9},{25,33... | collective-permute-start | bytes 1474568 | tf_op jit(solution)/shard_map/ppermute | solution.py:451
  47.0 1.7 %copy-start.5 = (bf16[10,96,256]{2,1,0:T(8,128)(2,1)}, bf16[10,96,256]{2,1,0:T(8,128)(2,1)S(1)}, u32[]{:S(2)}) copy-start(bf16[10,96,256]{2,1,0:T(8,128)(2,1)S(1)} %collective-permute-done.2.refs_4_.refs_2_) | copy-start | bytes 1474564
  48.7 0.8 copy-start.6
  59.3 39.8 %copy-start.8 = (bf16[8,96,256]{2,1,0:T(8,128)(2,1)S(1)}, bf16[8,96,256]{2,1,0:T(8,128)(2,1)}, u32[]{:S(2)}) copy-start(bf16[8,96,256]{2,1,0:T(8,128)(2,1)} %get-tuple-element.44) | copy-start | bytes 1179652
  59.3 40.6 %copy-start.7 = (bf16[8,96,256]{2,1,0:T(8,128)(2,1)S(1)}, bf16[8,96,256]{2,1,0:T(8,128)(2,1)}, u32[]{:S(2)}) copy-start(bf16[8,96,256]{2,1,0:T(8,128)(2,1)} %get-tuple-element.45) | copy-start | bytes 1179652
  67.9 1.8 %collective-permute-start.11 = (bf16[4,32,8,128]{3,2,1,0:T(8,128)(2,1)}, bf16[4,32,8,128]{3,2,1,0:T(8,128)(2,1)S(1)}, u32[]{:S(2)}, u32[]{:S(2)}) collective-permute-start(bf16[4,32,8,128]{3,2,1,0:T(8,128)(2,1)} %get-tuple-element.51), channel_id=1, source_target_pairs={{0,1},{1,0},{2,3},{3,2},{4,5},{5,4},{6,7},{7,6},{8,9},{9,8},{10,11... | collective-permute-start | bytes 786440 | tf_op jit(solution)/shard_map/ppermute | solution.py:467
  70.7 4.8 %collective-permute-start.12 = (bf16[32,8,128]{2,1,0:T(8,128)(2,1)S(1)}, bf16[32,8,128]{2,1,0:T(8,128)(2,1)S(1)}, u32[]{:S(2)}, u32[]{:S(2)}) collective-permute-start(bf16[32,8,128]{2,1,0:T(8,128)(2,1)S(1)} %get-tuple-element.52), channel_id=1, source_target_pairs={{0,64},{64,128},{128,192},{192,0},{1,65},{65,129},{129,193},{193,1... | collective-permute-start | bytes 196616 | tf_op jit(solution)/shard_map/ppermute | solution.py:471
  70.8 5.4 %collective-permute-start.14 = (bf16[32,8,128]{2,1,0:T(8,128)(2,1)S(1)}, bf16[32,8,128]{2,1,0:T(8,128)(2,1)S(1)}, u32[]{:S(2)}, u32[]{:S(2)}) collective-permute-start(bf16[32,8,128]{2,1,0:T(8,128)(2,1)S(1)} %get-tuple-element.53), channel_id=1, source_target_pairs={{0,192},{64,0},{128,64},{192,128},{1,193},{65,1},{129,65},{193,129... | collective-permute-start | bytes 196616 | tf_op jit(solution)/shard_map/ppermute | solution.py:471
  73.5 4.6 %collective-permute-start.13 = (bf16[32,8,128]{2,1,0:T(8,128)(2,1)S(1)}, bf16[32,8,128]{2,1,0:T(8,128)(2,1)S(1)}, u32[]{:S(2)}, u32[]{:S(2)}) collective-permute-start(bf16[32,8,128]{2,1,0:T(8,128)(2,1)S(1)} %get-tuple-element.54), channel_id=1, source_target_pairs={{0,128},{64,192},{128,0},{192,64},{1,129},{65,193},{129,1},{193,65... | collective-permute-start | bytes 196616 | tf_op jit(solution)/shard_map/ppermute | solution.py:471
  79.0 3.2 %collective-permute-start.15 = (bf16[32,8,128]{2,1,0:T(8,128)(2,1)S(1)}, bf16[32,8,128]{2,1,0:T(8,128)(2,1)S(1)}, u32[]{:S(2)}, u32[]{:S(2)}) collective-permute-start(bf16[32,8,128]{2,1,0:T(8,128)(2,1)S(1)} %fusion.2), channel_id=1, source_target_pairs={{0,16},{8,24},{16,0},{24,8},{32,48},{40,56},{48,32},{56,40},{1,17}... | collective-permute-start | bytes 196616 | tf_op jit(solution)/shard_map/ppermute | solution.py:475
  82.2 5.9 %collective-permute-start.18 = (bf16[32,8,128]{2,1,0:T(8,128)(2,1)S(1)}, bf16[32,8,128]{2,1,0:T(8,128)(2,1)S(1)}, u32[]{:S(2)}, u32[]{:S(2)}) collective-permute-start(bf16[32,8,128]{2,1,0:T(8,128)(2,1)S(1)} %add_convert_fusion.1), channel_id=1, source_target_pairs={{0,40},{8,32},{16,56},{24,48},{32,8},{40,0},{48,24},{56,16},{1,41}... | collective-permute-start | bytes 196616 | tf_op jit(solution)/shard_map/ppermute | solution.py:478
  85.8 4.6 %collective-permute-start.17 = (bf16[32,8,128]{2,1,0:T(8,128)(2,1)S(1)}, bf16[32,8,128]{2,1,0:T(8,128)(2,1)S(1)}, u32[]{:S(2)}, u32[]{:S(2)}) collective-permute-start(bf16[32,8,128]{2,1,0:T(8,128)(2,1)S(1)} %add_convert_fusion.1), channel_id=1, source_target_pairs={{0,32},{8,40},{16,48},{24,56},{32,0},{40,8},{48,16},{56,24},{1,33}... | collective-permute-start | bytes 196616 | tf_op jit(solution)/shard_map/ppermute | solution.py:478
  88.1 4.0 %collective-permute-start.16 = (bf16[32,8,128]{2,1,0:T(8,128)(2,1)S(1)}, bf16[32,8,128]{2,1,0:T(8,128)(2,1)S(1)}, u32[]{:S(2)}, u32[]{:S(2)}) collective-permute-start(bf16[32,8,128]{2,1,0:T(8,128)(2,1)S(1)} %add_convert_fusion.1), channel_id=1, source_target_pairs={{0,8},{8,0},{16,24},{24,16},{32,40},{40,32},{48,56},{56,48},{1,9},... | collective-permute-start | bytes 196616 | tf_op jit(solution)/shard_map/ppermute | solution.py:478
  92.1 12.2 %collective-permute-start.21 = (bf16[32,8,128]{2,1,0:T(8,128)(2,1)S(1)}, bf16[32,8,128]{2,1,0:T(8,128)(2,1)S(1)}, u32[]{:S(2)}, u32[]{:S(2)}) collective-permute-start(bf16[32,8,128]{2,1,0:T(8,128)(2,1)S(1)} %add_convert_fusion), channel_id=1, source_target_pairs={{0,6},{1,7},{2,0},{3,1},{4,2},{5,3},{6,4},{7,5},{8,14},{9,15},{10,... | collective-permute-start | bytes 196616 | tf_op jit(solution)/shard_map/ppermute | solution.py:459
  92.2 12.1 %collective-permute-start.20 = (bf16[32,8,128]{2,1,0:T(8,128)(2,1)S(1)}, bf16[32,8,128]{2,1,0:T(8,128)(2,1)S(1)}, u32[]{:S(2)}, u32[]{:S(2)}) collective-permute-start(bf16[32,8,128]{2,1,0:T(8,128)(2,1)S(1)} %add_convert_fusion), channel_id=1, source_target_pairs={{0,2},{1,3},{2,4},{3,5},{4,6},{5,7},{6,0},{7,1},{8,10},{9,11},{10,... | collective-permute-start | bytes 196616 | tf_op jit(solution)/shard_map/ppermute | solution.py:459
  95.8 8.5 %collective-permute-start.19 = (bf16[32,8,128]{2,1,0:T(8,128)(2,1)S(1)}, bf16[32,8,128]{2,1,0:T(8,128)(2,1)S(1)}, u32[]{:S(2)}, u32[]{:S(2)}) collective-permute-start(bf16[32,8,128]{2,1,0:T(8,128)(2,1)S(1)} %add_convert_fusion), channel_id=1, source_target_pairs={{0,4},{1,5},{2,6},{3,7},{4,0},{5,1},{6,2},{7,3},{8,12},{9,13},{10,... | collective-permute-start | bytes 196616 | tf_op jit(solution)/shard_map/ppermute | solution.py:459
  99.1 13.4 %collective-permute-start.7 = (bf16[8,96,256]{2,1,0:T(8,128)(2,1)S(1)}, bf16[8,96,256]{2,1,0:T(8,128)(2,1)S(1)}, u32[]{:S(2)}, u32[]{:S(2)}) collective-permute-start(bf16[8,96,256]{2,1,0:T(8,128)(2,1)S(1)} %copy-done.8), channel_id=1, source_target_pairs={{0,8},{8,0},{16,24},{24,16},{32,40},{40,32},{48,56},{56,48},{1,9},... | collective-permute-start | bytes 1179656 | tf_op jit(solution)/shard_map/ppermute | solution.py:452
  99.9 19.2 %collective-permute-start.8 = (bf16[8,96,256]{2,1,0:T(8,128)(2,1)S(1)}, bf16[8,96,256]{2,1,0:T(8,128)(2,1)S(1)}, u32[]{:S(2)}, u32[]{:S(2)}) collective-permute-start(bf16[8,96,256]{2,1,0:T(8,128)(2,1)S(1)} %copy-done.7), channel_id=1, source_target_pairs={{8,16},{16,8},{24,32},{32,24},{40,48},{48,40},{9,17},{17,9},{25,33... | collective-permute-start | bytes 1179656 | tf_op jit(solution)/shard_map/ppermute | solution.py:451
  104.3 21.8 %collective-permute-start.22 = (f32[32,8,128]{2,1,0:T(8,128)S(1)}, f32[32,8,128]{2,1,0:T(8,128)S(1)}, u32[]{:S(2)}, u32[]{:S(2)}) collective-permute-start(f32[32,8,128]{2,1,0:T(8,128)S(1)} %add_add_fusion), channel_id=1, source_target_pairs={{0,1},{1,0},{2,3},{3,2},{4,5},{5,4},{6,7},{7,6},{8,9},{9,8},{10,11... | collective-permute-start | bytes 393224 | tf_op jit(solution)/shard_map/ppermute | solution.py:483
  112.5 6.6 %copy-start = (bf16[8,96,256]{2,1,0:T(8,128)(2,1)}, bf16[8,96,256]{2,1,0:T(8,128)(2,1)S(1)}, u32[]{:S(2)}) copy-start(bf16[8,96,256]{2,1,0:T(8,128)(2,1)S(1)} %collective-permute-done.7.refs_3_.refs_2_) | copy-start | bytes 1179652
  119.1 0.7 copy-start.1
  122.1 5.2 %collective-permute-start.9 = (bf16[6,96,256]{2,1,0:T(8,128)(2,1)}, bf16[6,96,256]{2,1,0:T(8,128)(2,1)S(1)}, u32[]{:S(2)}, u32[]{:S(2)}) collective-permute-start(bf16[6,96,256]{2,1,0:T(8,128)(2,1)} %get-tuple-element.46), channel_id=1, source_target_pairs={{0,1},{1,0},{2,3},{3,2},{4,5},{5,4},{6,7},{7,6},{8,9},{9,8},{10,11... | collective-permute-start | bytes 884744 | tf_op jit(solution)/shard_map/ppermute | solution.py:452
  125.9 11.6 %collective-permute-start.10 = (bf16[6,96,256]{2,1,0:T(8,128)(2,1)}, bf16[6,96,256]{2,1,0:T(8,128)(2,1)S(1)}, u32[]{:S(2)}, u32[]{:S(2)}) collective-permute-start(bf16[6,96,256]{2,1,0:T(8,128)(2,1)} %get-tuple-element.47), channel_id=1, source_target_pairs={{0,7},{1,2},{2,1},{3,4},{4,3},{5,6},{6,5},{7,0},{8,15},{9,10},{10,... | collective-permute-start | bytes 884744 | tf_op jit(solution)/shard_map/ppermute | solution.py:451
  126.2 24.8 %copy-start.2 = (f32[63,8,128]{2,1,0:T(8,128)}, f32[63,8,128]{2,1,0:T(8,128)S(1)}, u32[]{:S(2)}) copy-start(f32[63,8,128]{2,1,0:T(8,128)S(1)} %pad_maximum_fusion.1) | copy-start | bytes 774148
  127.3 10.2 %copy-start.9 = (bf16[6,96,256]{2,1,0:T(8,128)(2,1)}, bf16[6,96,256]{2,1,0:T(8,128)(2,1)S(1)}, u32[]{:S(2)}) copy-start(bf16[6,96,256]{2,1,0:T(8,128)(2,1)S(1)} %collective-permute-done.9.refs_0_) | copy-start | bytes 884740
  137.5 0.7 copy-start.10

commit v5 on v4

--- a/solution.py
+++ b/solution.py
@@ -21,18 +21,21 @@
     return jax.ShapeDtypeStruct(dims, dtype)
 
 
-def call(body, place, grid, args, in_specs, outs, out_specs, scratch, cost, alias=None):
+def call(body, grid, args, in_specs, outs, out_specs, scratch, cost, alias=None):
+    def placed(*refs):
+        place = (lax.axis_index("azi") & 1, lax.axis_index("rad") & 1, lax.axis_index("dp"))
+        body(place, *refs)
+
     return pl.pallas_call(
-        body,
-        grid_spec=pltpu.PrefetchScalarGridSpec(
-            num_scalar_prefetch=1, grid=(grid,), in_specs=in_specs, out_specs=out_specs,
-            scratch_shapes=scratch),
+        placed,
+        grid_spec=pl.GridSpec(grid=(grid,), in_specs=in_specs, out_specs=out_specs,
+                              scratch_shapes=scratch),
         out_shape=outs,
         input_output_aliases=alias or {},
         compiler_params=pltpu.CompilerParams(
             dimension_semantics=("arbitrary",), vmem_limit_bytes=56 * 1024 * 1024),
         cost_estimate=pl.CostEstimate(flops=cost, transcendentals=0, bytes_accessed=4000000),
-    )(place, *args)
+    )(*args)
 
 
 def put_rows(tmp, cells):
@@ -72,17 +75,17 @@
     far_row[1 : na + 1] = o_ref[(nr - 1) * q]
 
 
-def to_columns(place, field):
+def to_columns(field):
     _, c, nr, na, nz = field.shape
     face, row = shape((nr, c, nz)), shape((na + 2, c, nz))
     part = c // 2
     rest = [face, face, row, row]
     return call(
-        columns_body, place, 2, (field,),
-        [pl.BlockSpec((1, part, nr, na, nz), lambda g, _: (0, g, 0, 0, 0))],
+        columns_body, 2, (field,),
+        [pl.BlockSpec((1, part, nr, na, nz), lambda g: (0, g, 0, 0, 0))],
         [shape((nr, na, c, nz))] + rest,
-        [pl.BlockSpec((nr, na, part, nz), lambda g, _: (0, 0, g, 0))]
-        + [pl.BlockSpec((y.shape[0], part, nz), lambda g, _: (0, g, 0)) for y in rest],
+        [pl.BlockSpec((nr, na, part, nz), lambda g: (0, 0, g, 0))]
+        + [pl.BlockSpec((y.shape[0], part, nz), lambda g: (0, g, 0)) for y in rest],
         [pltpu.VMEM((nz // 128, part * na, 128), f32)], 10000000)
 
 
@@ -110,13 +113,13 @@
         copy.wait()
 
 
-def insert(place, axis, messages, halos):
+def insert(axis, messages, halos):
     near, far = messages
     _, c, z = near.shape
     return call(
-        lambda *refs: insert_body(axis, *refs), place, 1, (near, far, *halos), [ANY] * 4,
+        lambda *refs: insert_body(axis, *refs), 1, (near, far, *halos), [ANY] * 4,
         [shape(near.shape)] * 2, [ANY, ANY],
-        [pltpu.VMEM((4, c, z), bf16), pltpu.SemaphoreType.DMA((2, 4))], 1000000, {1: 0, 2: 1})
+        [pltpu.VMEM((4, c, z), bf16), pltpu.SemaphoreType.DMA((2, 4))], 1000000, {0: 0, 1: 1})
 
 
 class Loader:
@@ -310,23 +313,23 @@
             far_row[...] = delta_ref[0]
 
 
-def forward(place, x, sides, ends, w, b, cot, before=None):
+def forward(x, sides, ends, w, b, cot, before=None):
     _, na, c, z = x.shape
     outer = before is not None
     field = pl.BlockSpec(
-        (1, c, 1, na, z), lambda g, _: (0, 0, 3 * g if outer else 1 + g, 0, 0))
+        (1, c, 1, na, z), lambda g: (0, 0, 3 * g if outer else 1 + g, 0, 0))
     args = [x, *sides, *ends, w, b, cot]
     face, row = shape((6 if outer else 2, c, z)), shape((na, c, z))
     rest = [face, face, shape((c, z), f32)]
     rest += [row, row] if outer else [shape((3 * c, K9), f32)]
     alias = None
     if outer:
-        alias = {1 + len(args): 0}
+        alias = {len(args): 0}
         args += before
     return call(
-        lambda *refs: forward_body(outer, *refs), place, 2,
+        lambda *refs: forward_body(outer, *refs), 2,
         args, [ANY] * len(args), [shape(cot.shape), shape((2, na, c, z))] + rest,
-        [field, pl.BlockSpec((1, na, c, z), lambda g, _: (g, 0, 0, 0))]
+        [field, pl.BlockSpec((1, na, c, z), lambda g: (g, 0, 0, 0))]
         + [full(y) for y in rest],
         ext_scratch(na, c, z) + [pltpu.VMEM((z // 128, c * na, 128), f32)] * 2
         + [pltpu.VMEM((2, c, na, z), bf16), pltpu.VMEM(b.shape, bf16)],
@@ -392,11 +395,11 @@
         pl.when(p == 1)(lambda: tiles(send_ref, keep_ref))
 
 
-def weight_terms(place, x, sides, ends, d_out, bsum, acc):
+def weight_terms(x, sides, ends, d_out, bsum, acc):
     _, na, c, z = x.shape
     half = shape((4, 32, 8, 128))
     return call(
-        weight_body, place, 2, [x, *sides, *ends, d_out, bsum, acc],
+        weight_body, 2, [x, *sides, *ends, d_out, bsum, acc],
         [ANY] * 8,
         [half, half], [full(half), full(half)],
         ext_scratch(na, c, z)[:2] + [pltpu.VMEM((3 * c, K9), f32),
@@ -425,12 +428,12 @@
     out_ref[0, :, 0] = get_rows(res, c, na).astype(bf16)
 
 
-def backward(place, d_in, d_out, sides, ends, w):
+def backward(d_in, d_out, sides, ends, w):
     _, na, c, z = d_in.shape
     args = [d_in, d_out, *sides, *ends, w]
     return call(
-        backward_body, place, 4, args, [ANY] * len(args), shape((1, c, 4, na, z)),
-        pl.BlockSpec((1, c, 1, na, z), lambda r, _: (0, 0, r, 0, 0)),
+        backward_body, 4, args, [ANY] * len(args), shape((1, c, 4, na, z)),
+        pl.BlockSpec((1, c, 1, na, z), lambda r: (0, 0, r, 0, 0)),
         ext_scratch(na, c, z) + [pltpu.VMEM((z // 128, c * na, 128), f32)], 5000000000)
 
 
@@ -500,22 +503,19 @@
 
 
 def on_device(inputs, weight, bias, cotangent):
-    place = jnp.stack(
-        [lax.axis_index("azi") % 2, lax.axis_index("rad") % 2, lax.axis_index("dp")]
-    ).astype(jnp.int32)
-    x, near_face, far_face, near_row, far_row = to_columns(place, inputs)
+    x, near_face, far_face, near_row, far_row = to_columns(inputs)
     sides = swap((near_face, far_face), "azi")
-    ends = swap(insert(place, 0, (near_row, far_row), sides), "rad")
+    ends = swap(insert(0, (near_row, far_row), sides), "rad")
     w_fwd, w_back, b_col = whole_weights(weight, bias)
     out, d_in, near_in, far_in, bsum, acc = forward(
-        place, x, sides, (), w_fwd, b_col, cotangent)
+        x, sides, (), w_fwd, b_col, cotangent)
     output, d_out, near_face, far_face, bsum, d_near, d_far = forward(
-        place, x, sides, ends, w_fwd, b_col, cotangent, [out, near_in, far_in, bsum])
+        x, sides, ends, w_fwd, b_col, cotangent, [out, near_in, far_in, bsum])
     d_ends = swap((d_near, d_far), "rad")
-    keep, send = weight_terms(place, x, sides, ends, d_out, bsum, acc)
-    d_sides = swap(insert(place, 1, (near_face, far_face), d_ends), "azi")
+    keep, send = weight_terms(x, sides, ends, d_out, bsum, acc)
+    d_sides = swap(insert(1, (near_face, far_face), d_ends), "azi")
     tiles = reduce_terms(keep, send)
-    input_grad = backward(place, d_in, d_out, d_sides, d_ends, w_back)
+    input_grad = backward(d_in, d_out, d_sides, d_ends, w_back)
     summed = tiles[:63].reshape(3, 21, 8, 128).transpose(0, 2, 1, 3).reshape(24, 21 * 128)
     return output, input_grad, summed[:, : 27 * C], summed[:, 27 * C]
 

time: 152 us -> 147 us (0.967)
  Pallas kernels: 52.9 us -> 48.2 us
    pallas_call x7, Pallas kernels: 52.9 us -> 48.2 us  [call(): pl.pallas_call(placed, grid_spec=pl.GridSpec(grid=(grid,), in_specs=in_sp...]
  transfers between devices with their start and end apart: 23 -> 23, of which waited for: 12 -> 12; matrix products, arithmetic and copies ran while one was open for 5% -> 4% of each run, Pallas kernels for 14% -> 13%
where the time goes in v5:
time: 147 us
  Pallas kernels  48.2 us (33%)
  starting transfers between devices  45.9 us (31%)
  waiting for transfers between devices  38.6 us (26%)
  local copies, waits for them, and re-layouts  9.72 us (7%)
  other arithmetic  3.06 us (2%)
    pallas_call x7, Pallas kernels, call(): pl.pallas_call(placed, grid_spec=pl.GridSpec(grid=(grid,), in_specs=in_sp...  48.2 us
    ppermute x4, waiting for transfers between devices, swap(): got_far = lax.ppermute(far, axis, far_pairs(axis))  24.8 us
    ppermute x4, starting transfers between devices, swap(): got_far = lax.ppermute(far, axis, far_pairs(axis))  12 us
    ppermute x3, starting transfers between devices, sum_over(): lax.ppermute(x, axis, [(i, (i + step * s) % n) for i in range(n)])  6.99 us
    ppermute x1, starting transfers between devices, reduce_terms(): y = lax.ppermute(total, 'azi', core)  6.33 us
    ppermute x4, starting transfers between devices, swap(): got_near = lax.ppermute(near, axis, near_pairs(axis))  6.21 us
    ppermute x3, starting transfers between devices, reduce_terms(): lax.ppermute(total, 'rad', [(i, i ^ step) for i in range(n)])  5.84 us
    ppermute x3, starting transfers between devices, whole_weights(): lax.ppermute(packed, 'dp', [(i, (i + s) % 4) for i in range(4)])  5.45 us
  transfers between devices with their start and end apart: 23, of which 12 were waited for; matrix products, arithmetic and copies ran while one was open for 4% of the time, Pallas kernels for 13%

profile of v5, /device:TPU:73, one launch (start us, length us, event | category | flops | bytes accessed | tf_op | source)
XLA Modules:
  0.0 146.5 jit_solution(12469325325205783467)
XLA Ops:
  0.6 0.7 broadcast_in_dim.2
  1.4 1.0 fusion.8
  2.3 2.8 %collective-permute-start.5 = (bf16[24,2720]{1,0:T(8,128)(2,1)S(1)}, bf16[24,2720]{1,0:T(8,128)(2,1)S(1)}, u32[]{:S(2)}, u32[]{:S(2)}) collective-permute-start(bf16[24,2720]{1,0:T(8,128)(2,1)S(1)} %get-tuple-element.58), channel_id=1, source_target_pairs={{0,128},{64,192},{128,0},{192,64},{1,129},{65,193},{129,1},{193,65... | collective-permute-start | bytes 391688 | tf_op jit(solution)/shard_map/ppermute | solution.py:495
  5.1 0.3 collective-permute-start.4
  5.4 2.4 %collective-permute-start.6 = (bf16[24,2720]{1,0:T(8,128)(2,1)S(1)}, bf16[24,2720]{1,0:T(8,128)(2,1)S(1)}, u32[]{:S(2)}, u32[]{:S(2)}) collective-permute-start(bf16[24,2720]{1,0:T(8,128)(2,1)S(1)} %get-tuple-element.58), channel_id=1, source_target_pairs={{0,192},{64,0},{128,64},{192,128},{1,193},{65,1},{129,65},{193,129... | collective-permute-start | bytes 391688 | tf_op jit(solution)/shard_map/ppermute | solution.py:495
  7.8 3.2 %shard_map.75 = (bf16[4,8,96,256]{3,2,1,0:T(8,128)(2,1)}, bf16[4,96,256]{2,1,0:T(8,128)(2,1)}, bf16[4,96,256]{2,1,0:T(8,128)(2,1)}, bf16[10,96,256]{2,1,0:T(8,128)(2,1)}, bf16[10,96,256]{2,1,0:T(8,128)(2,1)}) custom-call(bf16[1,96,4,8,256]{4,3,2,1,0:T(8,128)(2,1)} %refs_0_.1), custom_call_target="tpu_custom_call" | custom-call | flops 10000000 | bytes 4000000 | tf_op jit(solution)/shard_map/pallas_call | solution.py:29
  11.0 1.5 %collective-permute-start = (bf16[4,96,256]{2,1,0:T(8,128)(2,1)}, bf16[4,96,256]{2,1,0:T(8,128)(2,1)S(1)}, u32[]{:S(2)}, u32[]{:S(2)}) collective-permute-start(bf16[4,96,256]{2,1,0:T(8,128)(2,1)} %get-tuple-element.29), channel_id=1, source_target_pairs={{0,1},{1,0},{2,3},{3,2},{4,5},{5,4},{6,7},{7,6},{8,9},{9,8},{10,11... | collective-permute-start | bytes 589832 | tf_op jit(solution)/shard_map/ppermute | solution.py:455
  12.5 4.1 %collective-permute-start.1 = (bf16[4,96,256]{2,1,0:T(8,128)(2,1)}, bf16[4,96,256]{2,1,0:T(8,128)(2,1)S(1)}, u32[]{:S(2)}, u32[]{:S(2)}) collective-permute-start(bf16[4,96,256]{2,1,0:T(8,128)(2,1)} %get-tuple-element.30), channel_id=1, source_target_pairs={{0,7},{1,2},{2,1},{3,4},{4,3},{5,6},{6,5},{7,0},{8,15},{9,10},{10,... | collective-permute-start | bytes 589832 | tf_op jit(solution)/shard_map/ppermute | solution.py:454
  16.6 0.0 copy-start.3
  16.7 5.6 %collective-permute-done.1.refs_3_.refs_2_ = bf16[4,96,256]{2,1,0:T(8,128)(2,1)S(1)} collective-permute-done((bf16[4,96,256]{2,1,0:T(8,128)(2,1)}, bf16[4,96,256]{2,1,0:T(8,128)(2,1)S(1)}, u32[]{:S(2)}, u32[]{:S(2)}) %collective-permute-start.1) | collective-permute-done | bytes 196640 | tf_op jit(solution)/shard_map/ppermute | solution.py:454
  22.3 0.7 copy-done.4
  23.0 1.6 %shard_map.76 = (bf16[10,96,256]{2,1,0:T(8,128)(2,1)}, bf16[10,96,256]{2,1,0:T(8,128)(2,1)}) custom-call(bf16[10,96,256]{2,1,0:T(8,128)(2,1)} %get-tuple-element.31.refs_0_, bf16[10,96,256]{2,1,0:T(8,128)(2,1)} %get-tuple-element.32.refs_1_, bf16[4,96,256]{2,1,0:T(8,128)(2,1)} %copy-done.3, ...), custom_call_target="tpu_custom_call", output_to_operand_aliasing={{0}: (0, {}), {1}: (1, {})} | custom-call | flops 1000000 | bytes 4000000 | tf_op jit(solution)/shard_map/pallas_call | solution.py:29
  24.5 0.1 collective-permute-start.2
  24.6 3.2 %collective-permute-start.3 = (bf16[10,96,256]{2,1,0:T(8,128)(2,1)}, bf16[10,96,256]{2,1,0:T(8,128)(2,1)S(1)}, u32[]{:S(2)}, u32[]{:S(2)}) collective-permute-start(bf16[10,96,256]{2,1,0:T(8,128)(2,1)} %get-tuple-element.34), channel_id=1, source_target_pairs={{8,16},{16,8},{24,32},{32,24},{40,48},{48,40},{9,17},{17,9},{25,33... | collective-permute-start | bytes 1474568 | tf_op jit(solution)/shard_map/ppermute | solution.py:454
  27.9 0.0 collective-permute-done.5
  27.9 0.0 collective-permute-done.4
  27.9 0.1 pad_maximum_fusion
  28.0 0.6 gather_fusion
  28.6 0.7 slice.55.refs_4_.refs_6_
  29.3 0.3 copy.15
  29.6 0.7 copy.16
  30.3 1.3 reshape.93.refs_3_.refs_5_
  31.6 12.8 %shard_map.77 = (bf16[1,96,4,8,256]{4,3,2,1,0:T(8,128)(2,1)}, bf16[2,8,96,256]{3,2,1,0:T(8,128)(2,1)}, bf16[2,96,256]{2,1,0:T(8,128)(2,1)}, bf16[2,96,256]{2,1,0...) custom-call(bf16[4,8,96,256]{3,2,1,0:T(8,128)(2,1)} %get-tuple-element.28.refs_0_, bf16[4,96,256]{2,1,0:T(8,128)(2,1)} %copy-done.3, ...), custom_call_target="tpu_custom_call" | custom-call | flops 5000000000 | bytes 4000000 | tf_op jit(solution)/shard_map/pallas_call | solution.py:29
  44.3 2.4 %collective-permute-done.3.refs_4_ = bf16[10,96,256]{2,1,0:T(8,128)(2,1)S(1)} collective-permute-done((bf16[10,96,256]{2,1,0:T(8,128)(2,1)}, bf16[10,96,256]{2,1,0:T(8,128)(2,1)S(1)}, u32[]{:S(2)}, u32[]{:S(2)}) %collective-permute-start.3) | collective-permute-done | bytes 491552 | tf_op jit(solution)/shard_map/ppermute | solution.py:454
  46.7 0.8 copy-done.6
  47.5 9.1 %shard_map.78 = (bf16[1,96,4,8,256]{4,3,2,1,0:T(8,128)(2,1)}, bf16[2,8,96,256]{3,2,1,0:T(8,128)(2,1)}, bf16[6,96,256]{2,1,0:T(8,128)(2,1)}, bf16[6,96,256]{2,1,0...) custom-call(bf16[4,8,96,256]{3,2,1,0:T(8,128)(2,1)} %get-tuple-eleme, ...), custom_call_target="tpu_custom_call", output_to_operand_aliasing={{0}: (8, {})} | custom-call | flops 5000000000 | bytes 4000000 | tf_op jit(solution)/shard_map/pallas_call | solution.py:29
  56.7 7.9 %shard_map.81 = (bf16[4,32,8,128]{3,2,1,0:T(8,128)(2,1)}, bf16[4,32,8,128]{3,2,1,0:T(8,128)(2,1)}) custom-call(bf16[4,8,96,256]{3,2,1,0:T(8,128)(2,1)} %get-tuple-element.28.refs_0_, bf16[4,96,256]{2,1,0:T(8,128)(2,1)} %copy-done.3, bf16[4,96,256]{2,1,0:T(8,128)(2,1)} %copy-done.4, bf16[10,96,256]{2,1,0:T(8,128)(2,1)} %copy-done.5, ...), custom_call_target="tpu_custom_call" | custom-call | flops 2500000000 | bytes 4000000 | tf_op jit(solution)/shard_map/pallas_call | solution.py:29
  64.6 0.2 collective-permute-start.11
  64.8 1.6 %collective-permute-done.11 = bf16[4,32,8,128]{3,2,1,0:T(8,128)(2,1)S(1)} collective-permute-done((bf16[4,32,8,128]{3,2,1,0:T(8,128)(2,1)}, bf16[4,32,8,128]{3,2,1,0:T(8,128)(2,1)S(1)}, u32[]{:S(2)}, u32[]{:S(2)}) %collective-permute-start.11) | collective-permute-done | bytes 262176 | tf_op jit(solution)/shard_map/ppermute | solution.py:470
  66.4 1.0 fusion.3
  67.4 0.1 collective-permute-start.12
  67.4 2.7 %collective-permute-start.14 = (bf16[32,8,128]{2,1,0:T(8,128)(2,1)S(1)}, bf16[32,8,128]{2,1,0:T(8,128)(2,1)S(1)}, u32[]{:S(2)}, u32[]{:S(2)}) collective-permute-start(bf16[32,8,128]{2,1,0:T(8,128)(2,1)S(1)} %get-tuple-element.53), channel_id=1, source_target_pairs={{0,192},{64,0},{128,64},{192,128},{1,193},{65,1},{129,65},{193,129... | collective-permute-start | bytes 196616 | tf_op jit(solution)/shard_map/ppermute | solution.py:474
  70.1 0.0 collective-permute-start.13
  70.1 2.0 %collective-permute-done.12 = bf16[32,8,128]{2,1,0:T(8,128)(2,1)S(1)} collective-permute-done((bf16[32,8,128]{2,1,0:T(8,128)(2,1)S(1)}, bf16[32,8,128]{2,1,0:T(8,128)(2,1)S(1)}, u32[]{:S(2)}, u32[]{:S(2)}) %collective-permute-start.12) | collective-permute-done | bytes 65568 | tf_op jit(solution)/shard_map/ppermute | solution.py:474
  72.1 0.7 collective-permute-done.14
  72.9 1.8 %collective-permute-done.13 = bf16[32,8,128]{2,1,0:T(8,128)(2,1)S(1)} collective-permute-done((bf16[32,8,128]{2,1,0:T(8,128)(2,1)S(1)}, bf16[32,8,128]{2,1,0:T(8,128)(2,1)S(1)}, u32[]{:S(2)}, u32[]{:S(2)}) %collective-permute-start.13) | collective-permute-done | bytes 65568 | tf_op jit(solution)/shard_map/ppermute | solution.py:474
  74.7 0.9 fusion.2
  75.6 0.1 collective-permute-start.15
  75.7 3.1 %collective-permute-done.15 = bf16[32,8,128]{2,1,0:T(8,128)(2,1)S(1)} collective-permute-done((bf16[32,8,128]{2,1,0:T(8,128)(2,1)S(1)}, bf16[32,8,128]{2,1,0:T(8,128)(2,1)S(1)}, u32[]{:S(2)}, u32[]{:S(2)}) %collective-permute-start.15) | collective-permute-done | bytes 65568 | tf_op jit(solution)/shard_map/ppermute | solution.py:478
  78.9 3.6 %collective-permute-start.18 = (bf16[32,8,128]{2,1,0:T(8,128)(2,1)S(1)}, bf16[32,8,128]{2,1,0:T(8,128)(2,1)S(1)}, u32[]{:S(2)}, u32[]{:S(2)}) collective-permute-start(bf16[32,8,128]{2,1,0:T(8,128)(2,1)S(1)} %add_convert_fusion.1), channel_id=1, source_target_pairs={{0,40},{8,32},{16,56},{24,48},{32,8},{40,0},{48,24},{56,16},{1,41}... | collective-permute-start | bytes 196616 | tf_op jit(solution)/shard_map/ppermute | solution.py:481
  82.4 2.2 %collective-permute-start.17 = (bf16[32,8,128]{2,1,0:T(8,128)(2,1)S(1)}, bf16[32,8,128]{2,1,0:T(8,128)(2,1)S(1)}, u32[]{:S(2)}, u32[]{:S(2)}) collective-permute-start(bf16[32,8,128]{2,1,0:T(8,128)(2,1)S(1)} %add_convert_fusion.1), channel_id=1, source_target_pairs={{0,32},{8,40},{16,48},{24,56},{32,0},{40,8},{48,16},{56,24},{1,33}... | collective-permute-start | bytes 196616 | tf_op jit(solution)/shard_map/ppermute | solution.py:481
  84.7 2.4 %collective-permute-done.17 = bf16[32,8,128]{2,1,0:T(8,128)(2,1)S(1)} collective-permute-done((bf16[32,8,128]{2,1,0:T(8,128)(2,1)S(1)}, bf16[32,8,128]{2,1,0:T(8,128)(2,1)S(1)}, u32[]{:S(2)}, u32[]{:S(2)}) %collective-permute-start.17) | collective-permute-done | bytes 65568 | tf_op jit(solution)/shard_map/ppermute | solution.py:481
  87.1 1.6 %collective-permute-done.16 = bf16[32,8,128]{2,1,0:T(8,128)(2,1)S(1)} collective-permute-done((bf16[32,8,128]{2,1,0:T(8,128)(2,1)S(1)}, bf16[32,8,128]{2,1,0:T(8,128)(2,1)S(1)}, u32[]{:S(2)}, u32[]{:S(2)}) %collective-permute-start.16) | collective-permute-done | bytes 65568 | tf_op jit(solution)/shard_map/ppermute | solution.py:481
  88.8 0.1 collective-permute-start.21
  88.8 3.6 %collective-permute-start.20 = (bf16[32,8,128]{2,1,0:T(8,128)(2,1)S(1)}, bf16[32,8,128]{2,1,0:T(8,128)(2,1)S(1)}, u32[]{:S(2)}, u32[]{:S(2)}) collective-permute-start(bf16[32,8,128]{2,1,0:T(8,128)(2,1)S(1)} %add_convert_fusion), channel_id=1, source_target_pairs={{0,2},{1,3},{2,4},{3,5},{4,6},{5,7},{6,0},{7,1},{8,10},{9,11},{10,... | collective-permute-start | bytes 196616 | tf_op jit(solution)/shard_map/ppermute | solution.py:462
  92.4 3.3 %collective-permute-start.19 = (bf16[32,8,128]{2,1,0:T(8,128)(2,1)S(1)}, bf16[32,8,128]{2,1,0:T(8,128)(2,1)S(1)}, u32[]{:S(2)}, u32[]{:S(2)}) collective-permute-start(bf16[32,8,128]{2,1,0:T(8,128)(2,1)S(1)} %add_convert_fusion), channel_id=1, source_target_pairs={{0,4},{1,5},{2,6},{3,7},{4,0},{5,1},{6,2},{7,3},{8,12},{9,13},{10,... | collective-permute-start | bytes 196616 | tf_op jit(solution)/shard_map/ppermute | solution.py:462
  95.8 0.8 collective-permute-start.7
  96.5 4.4 %collective-permute-start.8 = (bf16[8,96,256]{2,1,0:T(8,128)(2,1)S(1)}, bf16[8,96,256]{2,1,0:T(8,128)(2,1)S(1)}, u32[]{:S(2)}, u32[]{:S(2)}) collective-permute-start(bf16[8,96,256]{2,1,0:T(8,128)(2,1)S(1)} %copy-done.7), channel_id=1, source_target_pairs={{8,16},{16,8},{24,32},{32,24},{40,48},{48,40},{9,17},{17,9},{25,33... | collective-permute-start | bytes 1179656 | tf_op jit(solution)/shard_map/ppermute | solution.py:454
  100.9 0.0 collective-permute-done.21
  100.9 0.0 collective-permute-done.19
  101.0 6.3 %collective-permute-start.22 = (f32[32,8,128]{2,1,0:T(8,128)S(1)}, f32[32,8,128]{2,1,0:T(8,128)S(1)}, u32[]{:S(2)}, u32[]{:S(2)}) collective-permute-start(f32[32,8,128]{2,1,0:T(8,128)S(1)} %add_add_fusion), channel_id=1, source_target_pairs={{0,1},{1,0},{2,3},{3,2},{4,5},{5,4},{6,7},{7,6},{8,9},{9,8},{10,11... | collective-permute-start | bytes 393224 | tf_op jit(solution)/shard_map/ppermute | solution.py:486
  107.4 0.5 copy.17
  107.8 1.3 reshape.94.refs_6_
  109.1 6.6 %collective-permute-done.8.refs_3_.refs_5_ = bf16[8,96,256]{2,1,0:T(8,128)(2,1)S(1)} collective-permute-done((bf16[8,96,256]{2,1,0:T(8,128)(2,1)S(1)}, bf16[8,96,256]{2,1,0:T(8,128)(2,1)S(1)}, u32[]{:S(2)}, u32[]{:S(2)}) %collective-permute-start.8) | collective-permute-done | bytes 393248 | tf_op jit(solution)/shard_map/ppermute | solution.py:454
  115.7 0.7 copy-done.1
  116.5 1.6 %shard_map.79 = (bf16[6,96,256]{2,1,0:T(8,128)(2,1)}, bf16[6,96,256]{2,1,0:T(8,128)(2,1)}) custom-call(bf16[6,96,256]{2,1,0:T(8,128)(2,1)} %get-tuple-element.42.refs_0_, bf16[6,96,256]{2,1,0:T(8,128)(2,1)} %get-tuple-element.43.refs_1_, bf16[8,96,256]{2,1,0:T(8,128)(2,1)} %copy-done, ...), custom_call_target="tpu_custom_call", output_to_operand_aliasing={{0}: (0, {}), {1}: (1, {})} | custom-call | flops 1000000 | bytes 4000000 | tf_op jit(solution)/shard_map/pallas_call | solution.py:29
  118.1 3.8 %collective-permute-start.9 = (bf16[6,96,256]{2,1,0:T(8,128)(2,1)}, bf16[6,96,256]{2,1,0:T(8,128)(2,1)S(1)}, u32[]{:S(2)}, u32[]{:S(2)}) collective-permute-start(bf16[6,96,256]{2,1,0:T(8,128)(2,1)} %get-tuple-element.46), channel_id=1, source_target_pairs={{0,1},{1,0},{2,3},{3,2},{4,5},{5,4},{6,7},{7,6},{8,9},{9,8},{10,11... | collective-permute-start | bytes 884744 | tf_op jit(solution)/shard_map/ppermute | solution.py:455
  121.9 0.3 collective-permute-start.10
  122.2 0.0 copy-start.2
  122.2 0.7 slice_reduce_fusion
  122.9 0.4 collective-permute-done.9.refs_2_
  123.3 10.2 %collective-permute-done.10.refs_3_ = bf16[6,96,256]{2,1,0:T(8,128)(2,1)S(1)} collective-permute-done((bf16[6,96,256]{2,1,0:T(8,128)(2,1)}, bf16[6,96,256]{2,1,0:T(8,128)(2,1)S(1)}, u32[]{:S(2)}, u32[]{:S(2)}) %collective-permute-start.10) | collective-permute-done | bytes 294944 | tf_op jit(solution)/shard_map/ppermute | solution.py:454
  133.5 0.7 copy-done.10
  134.2 12.1 %shard_map.80 = bf16[1,96,4,8,256]{4,3,2,1,0:T(8,128)(2,1)} custom-call(bf16[2,8,96,256]{3,2,1,0:T(8,128)(2,1)} %get-tuple-element.40.refs_0_, bf16[2,8,96,256]{3,2,1,0:T(8,128)(2,1)} %get-tuple-element.41.refs_1_.refs_5_, bf16[6,96,256]{2,1,0:T(8,128)(2,1)} %copy-done.9, bf16[6,96,256]{2,1,0:T(8,128)(2,1)} %copy-done.10, bf16[8,96,256]{2,1,0:T(8,128)(2,1)} %copy-done, ...), custom_call_target="tpu_custom_call" | custom-call | flops 5000000000 | bytes 4000000 | tf_op jit(solution)/shard_map/pallas_call | solution.py:29
  (33 shorter events, 0.3 us)
Async XLA Ops:
  2.3 25.5 %collective-permute-start.5 = (bf16[24,2720]{1,0:T(8,128)(2,1)S(1)}, bf16[24,2720]{1,0:T(8,128)(2,1)S(1)}, u32[]{:S(2)}, u32[]{:S(2)}) collective-permute-start(bf16[24,2720]{1,0:T(8,128)(2,1)S(1)} %get-tuple-element.58), channel_id=1, source_target_pairs={{0,128},{64,192},{128,0},{192,64},{1,129},{65,193},{129,1},{193,65... | collective-permute-start | bytes 391688 | tf_op jit(solution)/shard_map/ppermute | solution.py:495
  5.1 22.8 %collective-permute-start.4 = (bf16[24,2720]{1,0:T(8,128)(2,1)S(1)}, bf16[24,2720]{1,0:T(8,128)(2,1)S(1)}, u32[]{:S(2)}, u32[]{:S(2)}) collective-permute-start(bf16[24,2720]{1,0:T(8,128)(2,1)S(1)} %get-tuple-element.58), channel_id=1, source_target_pairs={{0,64},{64,128},{128,192},{192,0},{1,65},{65,129},{129,193},{193,1... | collective-permute-start | bytes 391688 | tf_op jit(solution)/shard_map/ppermute | solution.py:495
  5.4 22.5 %collective-permute-start.6 = (bf16[24,2720]{1,0:T(8,128)(2,1)S(1)}, bf16[24,2720]{1,0:T(8,128)(2,1)S(1)}, u32[]{:S(2)}, u32[]{:S(2)}) collective-permute-start(bf16[24,2720]{1,0:T(8,128)(2,1)S(1)} %get-tuple-element.58), channel_id=1, source_target_pairs={{0,192},{64,0},{128,64},{192,128},{1,193},{65,1},{129,65},{193,129... | collective-permute-start | bytes 391688 | tf_op jit(solution)/shard_map/ppermute | solution.py:495
  11.0 5.7 %collective-permute-start = (bf16[4,96,256]{2,1,0:T(8,128)(2,1)}, bf16[4,96,256]{2,1,0:T(8,128)(2,1)S(1)}, u32[]{:S(2)}, u32[]{:S(2)}) collective-permute-start(bf16[4,96,256]{2,1,0:T(8,128)(2,1)} %get-tuple-element.29), channel_id=1, source_target_pairs={{0,1},{1,0},{2,3},{3,2},{4,5},{5,4},{6,7},{7,6},{8,9},{9,8},{10,11... | collective-permute-start | bytes 589832 | tf_op jit(solution)/shard_map/ppermute | solution.py:455
  12.5 9.8 %collective-permute-start.1 = (bf16[4,96,256]{2,1,0:T(8,128)(2,1)}, bf16[4,96,256]{2,1,0:T(8,128)(2,1)S(1)}, u32[]{:S(2)}, u32[]{:S(2)}) collective-permute-start(bf16[4,96,256]{2,1,0:T(8,128)(2,1)} %get-tuple-element.30), channel_id=1, source_target_pairs={{0,7},{1,2},{2,1},{3,4},{4,3},{5,6},{6,5},{7,0},{8,15},{9,10},{10,... | collective-permute-start | bytes 589832 | tf_op jit(solution)/shard_map/ppermute | solution.py:454
  16.6 5.6 %copy-start.3 = (bf16[4,96,256]{2,1,0:T(8,128)(2,1)}, bf16[4,96,256]{2,1,0:T(8,128)(2,1)S(1)}, u32[]{:S(2)}) copy-start(bf16[4,96,256]{2,1,0:T(8,128)(2,1)S(1)} %collective-permute-done.refs_2_.refs_1_) | copy-start | bytes 589828
  22.3 0.7 copy-start.4
  24.5 19.8 %collective-permute-start.2 = (bf16[10,96,256]{2,1,0:T(8,128)(2,1)}, bf16[10,96,256]{2,1,0:T(8,128)(2,1)S(1)}, u32[]{:S(2)}, u32[]{:S(2)}) collective-permute-start(bf16[10,96,256]{2,1,0:T(8,128)(2,1)} %get-tuple-element.33), channel_id=1, source_target_pairs={{0,8},{8,0},{16,24},{24,16},{32,40},{40,32},{48,56},{56,48},{1,9},... | collective-permute-start | bytes 1474568 | tf_op jit(solution)/shard_map/ppermute | solution.py:455
  24.6 22.1 %collective-permute-start.3 = (bf16[10,96,256]{2,1,0:T(8,128)(2,1)}, bf16[10,96,256]{2,1,0:T(8,128)(2,1)S(1)}, u32[]{:S(2)}, u32[]{:S(2)}) collective-permute-start(bf16[10,96,256]{2,1,0:T(8,128)(2,1)} %get-tuple-element.34), channel_id=1, source_target_pairs={{8,16},{16,8},{24,32},{32,24},{40,48},{48,40},{9,17},{17,9},{25,33... | collective-permute-start | bytes 1474568 | tf_op jit(solution)/shard_map/ppermute | solution.py:454
  44.3 2.4 %copy-start.5 = (bf16[10,96,256]{2,1,0:T(8,128)(2,1)}, bf16[10,96,256]{2,1,0:T(8,128)(2,1)S(1)}, u32[]{:S(2)}) copy-start(bf16[10,96,256]{2,1,0:T(8,128)(2,1)S(1)} %collective-permute-done.2.refs_3_) | copy-start | bytes 1474564
  46.7 0.8 copy-start.6
  56.7 39.1 %copy-start.8 = (bf16[8,96,256]{2,1,0:T(8,128)(2,1)S(1)}, bf16[8,96,256]{2,1,0:T(8,128)(2,1)}, u32[]{:S(2)}) copy-start(bf16[8,96,256]{2,1,0:T(8,128)(2,1)} %get-tuple-element.44) | copy-start | bytes 1179652
  56.7 39.9 %copy-start.7 = (bf16[8,96,256]{2,1,0:T(8,128)(2,1)S(1)}, bf16[8,96,256]{2,1,0:T(8,128)(2,1)}, u32[]{:S(2)}) copy-start(bf16[8,96,256]{2,1,0:T(8,128)(2,1)} %get-tuple-element.45) | copy-start | bytes 1179652
  64.6 1.8 %collective-permute-start.11 = (bf16[4,32,8,128]{3,2,1,0:T(8,128)(2,1)}, bf16[4,32,8,128]{3,2,1,0:T(8,128)(2,1)S(1)}, u32[]{:S(2)}, u32[]{:S(2)}) collective-permute-start(bf16[4,32,8,128]{3,2,1,0:T(8,128)(2,1)} %get-tuple-element.51), channel_id=1, source_target_pairs={{0,1},{1,0},{2,3},{3,2},{4,5},{5,4},{6,7},{7,6},{8,9},{9,8},{10,11... | collective-permute-start | bytes 786440 | tf_op jit(solution)/shard_map/ppermute | solution.py:470
  67.4 4.8 %collective-permute-start.12 = (bf16[32,8,128]{2,1,0:T(8,128)(2,1)S(1)}, bf16[32,8,128]{2,1,0:T(8,128)(2,1)S(1)}, u32[]{:S(2)}, u32[]{:S(2)}) collective-permute-start(bf16[32,8,128]{2,1,0:T(8,128)(2,1)S(1)} %get-tuple-element.52), channel_id=1, source_target_pairs={{0,64},{64,128},{128,192},{192,0},{1,65},{65,129},{129,193},{193,1... | collective-permute-start | bytes 196616 | tf_op jit(solution)/shard_map/ppermute | solution.py:474
  67.4 5.4 %collective-permute-start.14 = (bf16[32,8,128]{2,1,0:T(8,128)(2,1)S(1)}, bf16[32,8,128]{2,1,0:T(8,128)(2,1)S(1)}, u32[]{:S(2)}, u32[]{:S(2)}) collective-permute-start(bf16[32,8,128]{2,1,0:T(8,128)(2,1)S(1)} %get-tuple-element.53), channel_id=1, source_target_pairs={{0,192},{64,0},{128,64},{192,128},{1,193},{65,1},{129,65},{193,129... | collective-permute-start | bytes 196616 | tf_op jit(solution)/shard_map/ppermute | solution.py:474
  70.1 4.6 %collective-permute-start.13 = (bf16[32,8,128]{2,1,0:T(8,128)(2,1)S(1)}, bf16[32,8,128]{2,1,0:T(8,128)(2,1)S(1)}, u32[]{:S(2)}, u32[]{:S(2)}) collective-permute-start(bf16[32,8,128]{2,1,0:T(8,128)(2,1)S(1)} %get-tuple-element.54), channel_id=1, source_target_pairs={{0,128},{64,192},{128,0},{192,64},{1,129},{65,193},{129,1},{193,65... | collective-permute-start | bytes 196616 | tf_op jit(solution)/shard_map/ppermute | solution.py:474
  75.6 3.2 %collective-permute-start.15 = (bf16[32,8,128]{2,1,0:T(8,128)(2,1)S(1)}, bf16[32,8,128]{2,1,0:T(8,128)(2,1)S(1)}, u32[]{:S(2)}, u32[]{:S(2)}) collective-permute-start(bf16[32,8,128]{2,1,0:T(8,128)(2,1)S(1)} %fusion.2), channel_id=1, source_target_pairs={{0,16},{8,24},{16,0},{24,8},{32,48},{40,56},{48,32},{56,40},{1,17}... | collective-permute-start | bytes 196616 | tf_op jit(solution)/shard_map/ppermute | solution.py:478
  78.9 5.8 %collective-permute-start.18 = (bf16[32,8,128]{2,1,0:T(8,128)(2,1)S(1)}, bf16[32,8,128]{2,1,0:T(8,128)(2,1)S(1)}, u32[]{:S(2)}, u32[]{:S(2)}) collective-permute-start(bf16[32,8,128]{2,1,0:T(8,128)(2,1)S(1)} %add_convert_fusion.1), channel_id=1, source_target_pairs={{0,40},{8,32},{16,56},{24,48},{32,8},{40,0},{48,24},{56,16},{1,41}... | collective-permute-start | bytes 196616 | tf_op jit(solution)/shard_map/ppermute | solution.py:481
  82.4 4.6 %collective-permute-start.17 = (bf16[32,8,128]{2,1,0:T(8,128)(2,1)S(1)}, bf16[32,8,128]{2,1,0:T(8,128)(2,1)S(1)}, u32[]{:S(2)}, u32[]{:S(2)}) collective-permute-start(bf16[32,8,128]{2,1,0:T(8,128)(2,1)S(1)} %add_convert_fusion.1), channel_id=1, source_target_pairs={{0,32},{8,40},{16,48},{24,56},{32,0},{40,8},{48,16},{56,24},{1,33}... | collective-permute-start | bytes 196616 | tf_op jit(solution)/shard_map/ppermute | solution.py:481
  84.7 4.0 %collective-permute-start.16 = (bf16[32,8,128]{2,1,0:T(8,128)(2,1)S(1)}, bf16[32,8,128]{2,1,0:T(8,128)(2,1)S(1)}, u32[]{:S(2)}, u32[]{:S(2)}) collective-permute-start(bf16[32,8,128]{2,1,0:T(8,128)(2,1)S(1)} %add_convert_fusion.1), channel_id=1, source_target_pairs={{0,8},{8,0},{16,24},{24,16},{32,40},{40,32},{48,56},{56,48},{1,9},... | collective-permute-start | bytes 196616 | tf_op jit(solution)/shard_map/ppermute | solution.py:481
  88.8 12.2 %collective-permute-start.21 = (bf16[32,8,128]{2,1,0:T(8,128)(2,1)S(1)}, bf16[32,8,128]{2,1,0:T(8,128)(2,1)S(1)}, u32[]{:S(2)}, u32[]{:S(2)}) collective-permute-start(bf16[32,8,128]{2,1,0:T(8,128)(2,1)S(1)} %add_convert_fusion), channel_id=1, source_target_pairs={{0,6},{1,7},{2,0},{3,1},{4,2},{5,3},{6,4},{7,5},{8,14},{9,15},{10,... | collective-permute-start | bytes 196616 | tf_op jit(solution)/shard_map/ppermute | solution.py:462
  88.8 12.1 %collective-permute-start.20 = (bf16[32,8,128]{2,1,0:T(8,128)(2,1)S(1)}, bf16[32,8,128]{2,1,0:T(8,128)(2,1)S(1)}, u32[]{:S(2)}, u32[]{:S(2)}) collective-permute-start(bf16[32,8,128]{2,1,0:T(8,128)(2,1)S(1)} %add_convert_fusion), channel_id=1, source_target_pairs={{0,2},{1,3},{2,4},{3,5},{4,6},{5,7},{6,0},{7,1},{8,10},{9,11},{10,... | collective-permute-start | bytes 196616 | tf_op jit(solution)/shard_map/ppermute | solution.py:462
  92.4 8.5 %collective-permute-start.19 = (bf16[32,8,128]{2,1,0:T(8,128)(2,1)S(1)}, bf16[32,8,128]{2,1,0:T(8,128)(2,1)S(1)}, u32[]{:S(2)}, u32[]{:S(2)}) collective-permute-start(bf16[32,8,128]{2,1,0:T(8,128)(2,1)S(1)} %add_convert_fusion), channel_id=1, source_target_pairs={{0,4},{1,5},{2,6},{3,7},{4,0},{5,1},{6,2},{7,3},{8,12},{9,13},{10,... | collective-permute-start | bytes 196616 | tf_op jit(solution)/shard_map/ppermute | solution.py:462
  95.8 13.4 %collective-permute-start.7 = (bf16[8,96,256]{2,1,0:T(8,128)(2,1)S(1)}, bf16[8,96,256]{2,1,0:T(8,128)(2,1)S(1)}, u32[]{:S(2)}, u32[]{:S(2)}) collective-permute-start(bf16[8,96,256]{2,1,0:T(8,128)(2,1)S(1)} %copy-done.8), channel_id=1, source_target_pairs={{0,8},{8,0},{16,24},{24,16},{32,40},{40,32},{48,56},{56,48},{1,9},... | collective-permute-start | bytes 1179656 | tf_op jit(solution)/shard_map/ppermute | solution.py:455
  96.5 19.2 %collective-permute-start.8 = (bf16[8,96,256]{2,1,0:T(8,128)(2,1)S(1)}, bf16[8,96,256]{2,1,0:T(8,128)(2,1)S(1)}, u32[]{:S(2)}, u32[]{:S(2)}) collective-permute-start(bf16[8,96,256]{2,1,0:T(8,128)(2,1)S(1)} %copy-done.7), channel_id=1, source_target_pairs={{8,16},{16,8},{24,32},{32,24},{40,48},{48,40},{9,17},{17,9},{25,33... | collective-permute-start | bytes 1179656 | tf_op jit(solution)/shard_map/ppermute | solution.py:454
  101.0 21.2 %collective-permute-start.22 = (f32[32,8,128]{2,1,0:T(8,128)S(1)}, f32[32,8,128]{2,1,0:T(8,128)S(1)}, u32[]{:S(2)}, u32[]{:S(2)}) collective-permute-start(f32[32,8,128]{2,1,0:T(8,128)S(1)} %add_add_fusion), channel_id=1, source_target_pairs={{0,1},{1,0},{2,3},{3,2},{4,5},{5,4},{6,7},{7,6},{8,9},{9,8},{10,11... | collective-permute-start | bytes 393224 | tf_op jit(solution)/shard_map/ppermute | solution.py:486
  109.1 6.6 %copy-start = (bf16[8,96,256]{2,1,0:T(8,128)(2,1)}, bf16[8,96,256]{2,1,0:T(8,128)(2,1)S(1)}, u32[]{:S(2)}) copy-start(bf16[8,96,256]{2,1,0:T(8,128)(2,1)S(1)} %collective-permute-done.7.refs_2_.refs_4_) | copy-start | bytes 1179652
  115.7 0.7 copy-start.1
  118.1 5.2 %collective-permute-start.9 = (bf16[6,96,256]{2,1,0:T(8,128)(2,1)}, bf16[6,96,256]{2,1,0:T(8,128)(2,1)S(1)}, u32[]{:S(2)}, u32[]{:S(2)}) collective-permute-start(bf16[6,96,256]{2,1,0:T(8,128)(2,1)} %get-tuple-element.46), channel_id=1, source_target_pairs={{0,1},{1,0},{2,3},{3,2},{4,5},{5,4},{6,7},{7,6},{8,9},{9,8},{10,11... | collective-permute-start | bytes 884744 | tf_op jit(solution)/shard_map/ppermute | solution.py:455
  121.9 11.6 %collective-permute-start.10 = (bf16[6,96,256]{2,1,0:T(8,128)(2,1)}, bf16[6,96,256]{2,1,0:T(8,128)(2,1)S(1)}, u32[]{:S(2)}, u32[]{:S(2)}) collective-permute-start(bf16[6,96,256]{2,1,0:T(8,128)(2,1)} %get-tuple-element.47), channel_id=1, source_target_pairs={{0,7},{1,2},{2,1},{3,4},{4,3},{5,6},{6,5},{7,0},{8,15},{9,10},{10,... | collective-permute-start | bytes 884744 | tf_op jit(solution)/shard_map/ppermute | solution.py:454
  122.2 24.1 %copy-start.2 = (f32[63,8,128]{2,1,0:T(8,128)}, f32[63,8,128]{2,1,0:T(8,128)S(1)}, u32[]{:S(2)}) copy-start(f32[63,8,128]{2,1,0:T(8,128)S(1)} %pad_maximum_fusion.1) | copy-start | bytes 774148
  123.3 10.2 %copy-start.9 = (bf16[6,96,256]{2,1,0:T(8,128)(2,1)}, bf16[6,96,256]{2,1,0:T(8,128)(2,1)S(1)}, u32[]{:S(2)}) copy-start(bf16[6,96,256]{2,1,0:T(8,128)(2,1)S(1)} %collective-permute-done.9.refs_2_) | copy-start | bytes 884740
  133.5 0.7 copy-start.10
